TPU v7x, 256 devices: a whole 4x4x8 slice. The times are simulated.
256 devices in a mesh: shard: 16 (over y, z_hi, core), rep: 16 (over x, z_lo).
Axes of the slice: x: 4, y: 4, z: 8 (z_hi: 2, z_lo: 4; z = z_hi * 4 + z_lo), core: 2. Of those that a mesh axis runs over, the one named last changes fastest.
Arguments:
- inputs: bfloat16 [50432, 768], P(('shard', 'rep')), may hold values from -6 to 6
- norm1_gain: float32 [768], replicated, may hold values from 0.25 to 1.75
- w_qkv: bfloat16 [768, 2304], P('shard'), may hold values from -0.21875 to 0.21875
- w_proj: bfloat16 [768, 768], P('shard'), may hold values from -0.875 to 0.875
- norm2_gain: float32 [768], replicated, may hold values from 0.25 to 1.75
- w_router: bfloat16 [768, 32], P('shard'), may hold values from -0.21875 to 0.21875
- w_expert_in: bfloat16 [2, 768, 3072], P(None, 'shard'), may hold values from -0.21875 to 0.21875
- w_expert_out: bfloat16 [2, 3072, 768], P(None, 'shard'), may hold values from -0.875 to 0.875
- expert_ids: int32 [50432, 2], P(('shard', 'rep')), may hold values from 0 to 1, all different within a row
- capacity: int32 [2], replicated, may hold values from 64 to 128, as said below
- cotangent: bfloat16 [50432, 768], P(('shard', 'rep')), may hold values from -6 to 6
Outputs:
- outputs: bfloat16 [50432, 768], P(('shard', 'rep'))
- grad_inputs: float32 [50432, 768], P(('shard', 'rep'))
- grad_norm1_gain: float32 [768], replicated
- grad_qkv: float32 [768, 2304], P('shard')
- grad_proj: float32 [768, 768], P('shard')
- grad_norm2_gain: float32 [768], replicated
- grad_router: float32 [768, 32], P('shard')
- grad_expert_in: float32 [2, 768, 3072], P(None, 'shard')
- grad_expert_out: float32 [2, 3072, 768], P(None, 'shard')
Inputs may be any that keep to these rules, and one draw needn't show every extreme that they name: Every expert's capacity is 64 to 128; some expert has exactly 128. `expert_ids`: the two experts of a token differ.
All inputs are finite; a program needn't handle non-finite values.
Results may differ from a plain program's by a relative error of at most 0.025.
Values may be sent and summed in bfloat16 or wider, within the bound.
No kernel may reach another device: no remote copies, remote signals or barrier semaphores. Data moves between devices by JAX's collectives and lax.ppermute only.
A program may use at most 128 MiB of HBM per device.

v0:
```python
import jax
import jax.numpy as jnp
from jax import lax
from jax.sharding import PartitionSpec as P

HEADS = 12
HD = 64
EXPERTS = 32
E_WIN = 2
SEQ = 197
CAP = 128


EPS = 1e-06


def layer_norm(values, gain):
    centred = values - jnp.mean(values, axis=-1, keepdims=True)
    inverse = lax.rsqrt(jnp.mean(centred * centred, axis=-1, keepdims=True) + EPS)
    normed = centred * inverse
    return (normed, inverse, (normed * gain).astype(jnp.bfloat16))


def layer_norm_back(grad_out, normed, inverse, gain):
    scaled = grad_out * gain
    grad_in = inverse * (
        scaled
        - jnp.mean(scaled, axis=-1, keepdims=True)
        - normed * jnp.mean(scaled * normed, axis=-1, keepdims=True)
    )
    return (grad_in, jnp.sum(grad_out * normed, axis=0))


def heads_view(block, images):
    return block.reshape(images, SEQ, HEADS, HD)


def attention_scores(qkv, images):
    width = HEADS * HD
    query = heads_view(qkv[:, :width], images)
    keys = heads_view(qkv[:, width : 2 * width], images)
    values = heads_view(qkv[:, 2 * width :], images)
    scores = jnp.einsum(
        "bqhd,bkhd->bhqk", query, keys, preferred_element_type=jnp.float32
    ) * HD ** (-0.5)
    return (query, keys, values, scores)


def attention_forward(qkv, images):
    query, keys, values, scores = attention_scores(qkv, images)
    logsum = jax.nn.logsumexp(scores, axis=-1, keepdims=True)
    probs = jnp.exp(scores - logsum).astype(jnp.bfloat16)
    mixed = jnp.einsum("bhqk,bkhd->bqhd", probs, values, preferred_element_type=jnp.float32).astype(
        jnp.bfloat16
    )
    return (mixed.reshape(images * SEQ, HEADS * HD), logsum)


def attention_backward(qkv, mixed, logsum, grad_mixed, images):
    query, keys, values, scores = attention_scores(qkv, images)
    probs_full = jnp.exp(scores - logsum)
    probs = probs_full.astype(jnp.bfloat16)
    grad_out = heads_view(grad_mixed, images)
    out_rows = heads_view(mixed, images)
    grad_values = jnp.einsum("bhqk,bqhd->bkhd", probs, grad_out, preferred_element_type=jnp.float32)
    grad_probs = jnp.einsum("bqhd,bkhd->bhqk", grad_out, values, preferred_element_type=jnp.float32)
    delta = jnp.sum(grad_out.astype(jnp.float32) * out_rows.astype(jnp.float32), axis=-1)
    delta = jnp.transpose(delta, (0, 2, 1))[..., None]
    grad_scores = (probs_full * (grad_probs - delta)).astype(jnp.bfloat16)
    scale = HD ** (-0.5)
    grad_query = (
        jnp.einsum("bhqk,bkhd->bqhd", grad_scores, keys, preferred_element_type=jnp.float32) * scale
    )
    grad_keys = (
        jnp.einsum("bhqk,bqhd->bkhd", grad_scores, query, preferred_element_type=jnp.float32)
        * scale
    )
    width = HEADS * HD
    rows = images * SEQ
    return jnp.concatenate(
        [
            grad_query.reshape(rows, width),
            grad_keys.reshape(rows, width),
            grad_values.reshape(rows, width),
        ],
        axis=1,
    ).astype(jnp.bfloat16)


def route_masks(expert_ids, capacity):
    count = expert_ids.shape[0]
    picked_hot = (expert_ids[:, :, None] == jnp.arange(E_WIN)[None, None, :]).astype(jnp.int32)
    ordered = jnp.transpose(picked_hot, (1, 0, 2)).reshape(2 * count, E_WIN)
    before = jnp.cumsum(ordered, axis=0) - ordered
    position = jnp.sum(before * ordered, axis=1).reshape(2, count).T
    limit = jnp.sum(picked_hot * capacity[None, None, :], axis=2)
    kept_mask = (position < limit).astype(jnp.float32)
    slot_hot = (position[:, :, None] == jnp.arange(CAP)[None, None, :]).astype(jnp.float32)
    return (
        kept_mask[:, :, None, None]
        * picked_hot.astype(jnp.float32)[:, :, :, None]
        * slot_hot[:, :, None, :]
    )


def body(
    inputs,
    norm1_gain,
    w_qkv,
    w_proj,
    norm2_gain,
    w_router,
    w_expert_in,
    w_expert_out,
    expert_ids,
    capacity,
    cotangent,
):
    high = lax.Precision.HIGHEST
    images = inputs.shape[0] // SEQ
    shard_rows = w_qkv.shape[0]
    hid_rows = w_expert_out.shape[1]
    full_qkv, full_proj, full_router = (
        lax.all_gather(w_qkv, "shard", axis=0, tiled=True),
        lax.all_gather(w_proj, "shard", axis=0, tiled=True),
        lax.all_gather(w_router, "shard", axis=0, tiled=True),
    )
    x_float = inputs.astype(jnp.float32)
    normed1, inverse1, hidden1 = layer_norm(x_float, norm1_gain)
    qkv = jnp.dot(hidden1, full_qkv, preferred_element_type=jnp.float32).astype(jnp.bfloat16)
    mixed, logsum = attention_forward(qkv, images)
    attended = x_float + jnp.dot(mixed, full_proj, preferred_element_type=jnp.float32)
    normed2, inverse2, hidden2 = layer_norm(attended, norm2_gain)
    logits = jnp.dot(hidden2, full_router, preferred_element_type=jnp.float32)
    router = jax.nn.softmax(logits, axis=-1)
    expert_hot = (expert_ids[:, :, None] == jnp.arange(EXPERTS)[None, None, :]).astype(jnp.float32)
    gate = jnp.sum(router[:, None, :] * expert_hot, axis=2)
    masks = route_masks(expert_ids, capacity)
    dispatch_float = jnp.sum(masks, axis=1)
    dispatch = dispatch_float.astype(jnp.bfloat16)
    combine = jnp.sum(masks * gate[:, :, None, None], axis=1)
    expert_rows = jnp.einsum(
        "rec,rd->ecd", dispatch, hidden2, preferred_element_type=jnp.float32
    ).astype(jnp.bfloat16)
    kept_weights = []
    pre_list = []
    activated_list = []
    eout_list = []
    for expert in range(E_WIN):
        first, second = (
            lax.all_gather(w_expert_in[expert], "shard", axis=0, tiled=True),
            lax.all_gather(w_expert_out[expert], "shard", axis=0, tiled=True),
        )
        kept_weights.append((first, second))
        pre = jnp.dot(expert_rows[expert], first, preferred_element_type=jnp.float32)
        activated = jax.nn.gelu(pre, approximate=False).astype(jnp.bfloat16)
        pre_list.append(pre)
        activated_list.append(activated)
        eout_list.append(
            jnp.dot(activated, second, preferred_element_type=jnp.float32).astype(jnp.bfloat16)
        )
    expert_out = jnp.stack(eout_list)
    eout_float = expert_out.astype(jnp.float32)
    moe = jnp.einsum("rec,ecd->rd", combine, eout_float, precision=high)
    outputs = (attended + moe).astype(jnp.bfloat16)
    grad = cotangent.astype(jnp.float32)
    matched = jnp.einsum("rd,ecd->rec", grad, eout_float, precision=high)
    grad_gate = jnp.sum(masks * matched[:, None, :, :], axis=(2, 3))
    grad_eout = jnp.einsum("rec,rd->ecd", combine, grad, precision=high).astype(jnp.bfloat16)
    back_qkv, back_proj, back_router = (full_qkv, full_proj, full_router)
    in_list = []
    out_list = []
    grad_rows_list = []
    for expert in range(E_WIN):
        first, second = kept_weights[expert]
        pre = pre_list[expert]
        grad_act = jnp.einsum(
            "cd,hd->ch", grad_eout[expert], second, preferred_element_type=jnp.float32
        )
        slope = (
            0.5 * (1.0 + jax.scipy.special.erf(pre * 0.7071067811865476))
            + pre * jnp.exp(-0.5 * pre * pre) * 0.3989422804014327
        )
        grad_pre = (grad_act * slope).astype(jnp.bfloat16)
        grad_rows_list.append(
            jnp.einsum("ch,dh->cd", grad_pre, first, preferred_element_type=jnp.float32).astype(
                jnp.bfloat16
            )
        )
        rows_here = expert_rows[expert]
        act_here = activated_list[expert]
        eout_here = grad_eout[expert]

        def in_term(start, count, rows_here=rows_here, grad_pre=grad_pre):
            return jnp.einsum("cd,ch->dh", rows_here, grad_pre, preferred_element_type=jnp.float32)

        def out_term(start, count, act_here=act_here, eout_here=eout_here):
            return jnp.einsum("ch,cd->hd", act_here, eout_here, preferred_element_type=jnp.float32)

        in_list.append(
            lax.psum_scatter(
                in_term(jnp.int32(0), shard_rows * lax.axis_size("shard")).astype(jnp.bfloat16),
                "shard",
                scatter_dimension=0,
                tiled=True,
            ).astype(jnp.float32)
        )
        out_list.append(
            lax.psum_scatter(
                out_term(jnp.int32(0), hid_rows * lax.axis_size("shard")).astype(jnp.bfloat16),
                "shard",
                scatter_dimension=0,
                tiled=True,
            ).astype(jnp.float32)
        )
    grad_rows = jnp.stack(grad_rows_list)
    grad_probs = jnp.sum(grad_gate[:, :, None] * expert_hot, axis=1)
    grad_logits = (
        router * (grad_probs - jnp.sum(router * grad_probs, axis=-1, keepdims=True))
    ).astype(jnp.bfloat16)
    grad_hidden2 = jnp.einsum(
        "rec,ecd->rd", dispatch, grad_rows, preferred_element_type=jnp.float32
    ) + jnp.einsum("re,de->rd", grad_logits, back_router, preferred_element_type=jnp.float32)
    grad_norm2, gain2 = layer_norm_back(grad_hidden2, normed2, inverse2, norm2_gain)
    grad_attended = grad + grad_norm2
    grad_branch = grad_attended.astype(jnp.bfloat16)
    grad_mixed = jnp.einsum(
        "rk,dk->rd", grad_branch, back_proj, preferred_element_type=jnp.float32
    ).astype(jnp.bfloat16)
    grad_qkv_rows = attention_backward(qkv, mixed, logsum, grad_mixed, images)
    grad_hidden1 = jnp.einsum(
        "rk,dk->rd", grad_qkv_rows, back_qkv, preferred_element_type=jnp.float32
    )
    grad_norm1, gain1 = layer_norm_back(grad_hidden1, normed1, inverse1, norm1_gain)
    grad_inputs = grad_attended + grad_norm1
    gain1_total, gain2_total = lax.psum((gain1, gain2), ("shard", "rep"))
    dense_local = lax.psum_scatter(
        jnp.concatenate(
            [
                jnp.einsum("rc,rk->ck", hidden1, grad_qkv_rows, preferred_element_type=jnp.float32),
                jnp.einsum("rc,rk->ck", mixed, grad_branch, preferred_element_type=jnp.float32),
                jnp.einsum("rc,rk->ck", hidden2, grad_logits, preferred_element_type=jnp.float32),
            ],
            axis=1,
        ).astype(jnp.bfloat16),
        "shard",
        scatter_dimension=0,
        tiled=True,
    )
    dense_total, in_total, out_total = (
        lax.psum(dense_local, "rep").astype(jnp.float32),
        lax.psum(jnp.stack(in_list).astype(jnp.bfloat16), "rep").astype(jnp.float32),
        lax.psum(jnp.stack(out_list).astype(jnp.bfloat16), "rep").astype(jnp.float32),
    )
    width = HEADS * HD
    return (
        outputs,
        grad_inputs,
        gain1_total,
        dense_total[:, : 3 * width],
        dense_total[:, 3 * width : 4 * width],
        gain2_total,
        dense_total[:, 4 * width :],
        in_total,
        out_total,
    )


def solution(mesh):
    in_specs = (
        P(("shard", "rep"), None),
        P(),
        P("shard", None),
        P("shard", None),
        P(),
        P("shard", None),
        P(None, "shard", None),
        P(None, "shard", None),
        P(("shard", "rep"), None),
        P(),
        P(("shard", "rep"), None),
    )
    out_specs = (
        P(("shard", "rep"), None),
        P(("shard", "rep"), None),
        P(),
        P("shard", None),
        P("shard", None),
        P(),
        P("shard", None),
        P(None, "shard", None),
        P(None, "shard", None),
    )
    return jax.shard_map(body, mesh=mesh, in_specs=in_specs, out_specs=out_specs, check_vma=False)
```

profile of v0, /device:TPU:8, one launch (start us, length us, event | category | flops | bytes accessed | tf_op | source)
XLA Modules:
  0.0 1203.3 jit_solution(413905897846838815)
XLA Ops:
  8.7 1.9 fusion.130
  14.3 31.6 %all-gather.4 = bf16[16,48,32]{1,2,0:T(8,128)(2,1)S(1)} all-gather(bf16[1,48,32]{1,2,0:T(8,128)(2,1)S(1)} %bitcast.199), channel_id=1, replica_groups=mesh['shard'=16,'rep'=16] {'shard'}, dimensions={0}, use_global_device_ids=true | all-gather | bytes 52224 | tf_op jit(solution)/shard_map/all_gather | solution.py:126
  48.4 38.7 %all-gather.12.cloned.1.call-done = bf16[768,2304]{1,0:T(8,128)(2,1)} async-done(((bf16[48,2304]{1,0:T(8,128)(2,1)}), bf16[768,2304]{1,0:T(8,128)(2,1)}) %all-gather.12.cloned.1.call-update) | async-done | bytes 3538960 | tf_op jit(solution)/shard_map/all_gather | solution.py:124
  87.0 3.0 convolution_convert_fusion.5
  92.1 1.8 multiply_reduce_fusion
  94.5 1.4 convolution_convert_fusion.10
  95.8 46.1 %all-gather.14.cloned.1.call-done = bf16[768,768]{1,0:T(8,128)(2,1)} async-done(((bf16[48,768]{1,0:T(8,128)(2,1)}), bf16[768,768]{1,0:T(8,128)(2,1)}) %all-gather.14.cloned.1.call-update) | async-done | bytes 1179664 | tf_op jit(solution)/shard_map/all_gather | solution.py:125
  141.9 1.9 fusion.131
  146.4 1.4 copy.113
  147.9 2.0 convolution_convert_fusion.9
  149.9 72.3 %all-gather.20.cloned.1.call-done = bf16[1,768,3072]{2,1,0:T(8,128)(2,1)} async-done(((bf16[1,48,3072]{2,1,0:T(8,128)(2,1)}), bf16[1,768,3072]{2,1,0:T(8,128)(2,1)}) %all-gather.20.cloned.1.call-update) | async-done | bytes 4718608 | tf_op jit(solution)/shard_map/all_gather | solution.py:151
  222.2 7.7 fusion.34
  229.9 71.5 %all-gather.22.cloned.1.call-done = bf16[1,3072,768]{2,1,0:T(8,128)(2,1)} async-done(((bf16[1,192,768]{2,1,0:T(8,128)(2,1)}), bf16[1,3072,768]{2,1,0:T(8,128)(2,1)}) %all-gather.22.cloned.1.call-update) | async-done | bytes 4718608 | tf_op jit(solution)/shard_map/all_gather | solution.py:152
  301.4 4.0 fusion.73
  305.4 75.7 %all-gather.16.cloned.1.call-done = bf16[1,768,3072]{2,1,0:T(8,128)(2,1)} async-done(((bf16[1,48,3072]{2,1,0:T(8,128)(2,1)}), bf16[1,768,3072]{2,1,0:T(8,128)(2,1)}) %all-gather.16.cloned.1.call-update) | async-done | bytes 4718608 | tf_op jit(solution)/shard_map/all_gather | solution.py:151
  381.1 7.9 fusion.31
  389.1 71.2 %all-gather.18.cloned.1.call-done = bf16[1,3072,768]{2,1,0:T(8,128)(2,1)} async-done(((bf16[1,192,768]{2,1,0:T(8,128)(2,1)}), bf16[1,3072,768]{2,1,0:T(8,128)(2,1)}) %all-gather.18.cloned.1.call-update) | async-done | bytes 4718608 | tf_op jit(solution)/shard_map/all_gather | solution.py:152
  460.3 3.4 fusion.79
  464.9 7.0 fusion.100
  473.9 3.7 convolution_convert_fusion
  477.6 4.7 convolution_convert_fusion.1
  482.5 4.8 fusion.22
  488.2 3.7 convolution_convert_fusion.2
  491.8 9.8 reduce-scatter.8.cloned.1.call-start
  501.6 4.6 fusion.25
  507.1 3.5 convolution_convert_fusion.3
  510.7 1.6 copy.119
  513.0 4.7 fusion.82
  517.7 4.1 fusion.76
  523.9 1.3 convolution_convert_fusion.11
  525.2 1.9 copy.120
  527.1 2.0 copy.121
  531.0 1.4 multiply_reduce_fusion.1
  532.4 1.9 multiply_convert_fusion
  537.6 1.3 convolution_convert_fusion.4
  538.9 2.4 pad_maximum_fusion
  541.3 40.2 %reduce-scatter.14.cloned.1.call-done = bf16[192,768]{1,0:T(8,128)(2,1)} async-done(((bf16[3072,768]{1,0:T(8,128)(2,1)}), bf16[192,768]{1,0:T(8,128)(2,1)}) %reduce-scatter.14.cloned.1.call-update) | async-done | bytes 294928 | tf_op jit(solution)/shard_map/reduce_scatter | solution.py:209
  581.6 109.0 %reduce-scatter.12.cloned.1.call-done = bf16[192,768]{1,0:T(8,128)(2,1)} async-done(((bf16[3072,768]{1,0:T(8,128)(2,1)}), bf16[192,768]{1,0:T(8,128)(2,1)}) %reduce-scatter.12.cloned.1.call-update) | async-done | bytes 294928 | tf_op jit(solution)/shard_map/reduce_scatter | solution.py:209
  690.6 1.9 pad_maximum_fusion.3
  692.6 106.5 %reduce-scatter.10.cloned.1.call-done = bf16[48,3072]{1,0:T(8,128)(2,1)} async-done(((bf16[768,3072]{1,0:T(8,128)(2,1)}), bf16[48,3072]{1,0:T(8,128)(2,1)}) %reduce-scatter.10.cloned.1.call-update) | async-done | bytes 294928 | tf_op jit(solution)/shard_map/reduce_scatter | solution.py:201
  799.0 108.9 %reduce-scatter.8.cloned.1.call-done = bf16[48,3072]{1,0:T(8,128)(2,1)} async-done(((bf16[768,3072]{1,0:T(8,128)(2,1)}), bf16[48,3072]{1,0:T(8,128)(2,1)}) %reduce-scatter.8.cloned.1.call-update) | async-done | bytes 294928 | tf_op jit(solution)/shard_map/reduce_scatter | solution.py:201
  907.9 1.9 pad_maximum_fusion.2
  909.9 108.4 %reduce-scatter.6.cloned.1.call-done = bf16[48,3104]{1,0:T(8,128)(2,1)} async-done(((bf16[768,3104]{1,0:T(8,128)(2,1)}), bf16[48,3104]{1,0:T(8,128)(2,1)}) %reduce-scatter.6.cloned.1.call-update) | async-done | bytes 298000 | tf_op jit(solution)/shard_map/reduce_scatter | solution.py:237
  1018.4 4.2 fusion.96
  1022.5 74.5 %all-reduce.1 = (f32[768]{0:T(1024)}, f32[768]{0:T(1024)}) all-reduce(f32[768]{0:T(1024)S(1)} %get-tuple-element.56, f32[768]{0:T(1024)S(1)} %get-tuple-element.54), channel_id=1, replica_groups=mesh['shard'=16,'rep'=16] {'shard','rep'}, use_global_device_ids=true, to_apply=%region_24.25 | all-reduce | flops 1536 | bytes 12288 | tf_op jit(solution)/shard_map/psum | solution.py:236
  1100.7 88.6 %all-reduce.5.cloned.1.call-done = (bf16[48,3104]{1,0:T(8,128)(2,1)}, bf16[2,48,3072]{2,1,0:T(8,128)(2,1)}, bf16[2,192,768]{2,1,0:T(8,128)(2,1)}) async-done(((bf16[48,3104]{1,0:T(8,128)(2,1)}, bf16[2,48,3072]{2,1,0:T(8,128)(2,1)}, bf16[2,192,768]{2,1,0:T(8,128)(2,1)}), (bf16[48,3104]{1,0:T(8,128)(2,1)}, bf16[2,48,3072]{2,1,0:T(8,128)(2,1)}, bf16[2,192,768]{2,1,0:T(8,128)(2,1)})) %all-reduce.5.cloned.1.call-update) | async-done | bytes 1477648 | tf_op jit(solution)/shard_map/psum | solution.py:251
  1190.1 1.6 slice.85
  1191.6 1.7 slice.84
  (195 shorter events, 32.8 us)
Async XLA Ops:
  7.2 3.5 copy-start.33
  7.2 79.8 %all-gather.12.cloned.1.call-start = ((), (), s32[]{:S(2)}) async-start(), calls=%async_computation.5 | async-start | bytes 3760128 | tf_op jit(solution)/shard_map/all_gather | solution.py:124
  7.9 134.0 %all-gather.14.cloned.1.call-start = ((), (), s32[]{:S(2)}) async-start(), calls=%async_computation.6 | async-start | bytes 1253376 | tf_op jit(solution)/shard_map/all_gather | solution.py:125
  8.7 4.2 copy-start.43
  8.7 213.5 %all-gather.20.cloned.1.call-start = ((), (), s32[]{:S(2)}) async-start(), calls=%async_computation.14 | async-start | bytes 5013504 | tf_op jit(solution)/shard_map/all_gather | solution.py:151
  10.6 3.7 copy-start.52
  10.6 36.2 %copy-start.53 = (s32[2]{0:T(128)S(1)}, s32[2]{0:T(128)}, u32[]{:S(2)}) copy-start(s32[2]{0:T(128)} %param.20) | copy-start | bytes 28
  10.7 36.4 %copy-start.3 = (bf16[197,768]{1,0:T(8,128)(2,1)S(1)}, bf16[197,768]{1,0:T(8,128)(2,1)}, u32[]{:S(2)}) copy-start(bf16[197,768]{1,0:T(8,128)(2,1)} %param.11) | copy-start | bytes 907780
  10.7 290.7 %all-gather.22.cloned.1.call-start = ((), (), s32[]{:S(2)}) async-start(), calls=%async_computation.15 | async-start | bytes 5013504 | tf_op jit(solution)/shard_map/all_gather | solution.py:152
  11.6 75.4 %copy-start.45 = (f32[768]{0:T(1024)S(1)}, f32[768]{0:T(1024)}, u32[]{:S(2)}) copy-start(f32[768]{0:T(1024)} %param.12) | copy-start | bytes 9220
  11.6 369.5 %all-gather.16.cloned.1.call-start = ((), (), s32[]{:S(2)}) async-start(), calls=%async_computation.12 | async-start | bytes 5013504 | tf_op jit(solution)/shard_map/all_gather | solution.py:151
  12.2 448.1 %all-gather.18.cloned.1.call-start = ((), (), s32[]{:S(2)}) async-start(), calls=%async_computation.13 | async-start | bytes 5013504 | tf_op jit(solution)/shard_map/all_gather | solution.py:152
  12.8 568.8 %reduce-scatter.14.cloned.1.call-start = ((), (), s32[]{:S(2)}) async-start(), calls=%async_computation.11 | async-start | bytes 5013504 | tf_op jit(solution)/shard_map/reduce_scatter | solution.py:209
  47.1 42.9 %copy-start.19 = (f32[197,2,2]{2,1,0:T(2,128)}, f32[197,2,2]{2,1,0:T(2,128)S(1)}, u32[]{:S(2)}) copy-start(f32[197,2,2]{2,1,0:T(2,128)S(1)} %copy.110) | copy-start | bytes 9460
  47.2 42.8 %copy-start.46 = (f32[197]{0:T(256)}, f32[197]{0:T(256)S(1)}, u32[]{:S(2)}) copy-start(f32[197]{0:T(256)S(1)} %broadcast_multiply_fusion.5) | copy-start | bytes 2368
  47.5 42.5 %copy-start.50 = (f32[197]{0:T(256)}, f32[197]{0:T(256)S(1)}, u32[]{:S(2)}) copy-start(f32[197]{0:T(256)S(1)} %add_rsqrt_fusion.1) | copy-start | bytes 2368
  47.8 42.2 %copy-start.21 = (f32[197,2,128]{2,1,0:T(2,128)}, f32[197,2,128]{2,1,0:T(2,128)S(1)}, u32[]{:S(2)}) copy-start(f32[197,2,128]{2,1,0:T(2,128)S(1)} %compare_convert_fusion) | copy-start | bytes 605188
  92.1 2.3 copy-start.8
  95.8 48.8 %copy-start.44 = (f32[768]{0:T(1024)S(1)}, f32[768]{0:T(1024)}, u32[]{:S(2)}) copy-start(f32[768]{0:T(1024)} %param.15) | copy-start | bytes 9220
  141.9 3.6 copy-start.34
  460.3 3.4 copy-start.24
  460.3 3.4 copy-start.26
  460.3 3.9 copy-start.36
  463.8 8.1 copy-start.28
  463.8 10.1 copy-start.5
  477.6 213.1 %reduce-scatter.12.cloned.1.call-start = ((), (), s32[]{:S(2)}) async-start(), calls=%async_computation.10 | async-start | bytes 5013504 | tf_op jit(solution)/shard_map/reduce_scatter | solution.py:209
  482.4 316.6 %reduce-scatter.10.cloned.1.call-start = ((), (), s32[]{:S(2)}) async-start(), calls=%async_computation.9 | async-start | bytes 5013504 | tf_op jit(solution)/shard_map/reduce_scatter | solution.py:201
  482.4 5.7 copy-start.15
  491.8 416.1 %reduce-scatter.8.cloned.1.call-start = ((), (), s32[]{:S(2)}) async-start(), calls=%async_computation.8 | async-start | bytes 5013504 | tf_op jit(solution)/shard_map/reduce_scatter | solution.py:201
  501.6 5.5 copy-start.16
  510.7 507.6 %reduce-scatter.6.cloned.1.call-start = ((), (), s32[]{:S(2)}) async-start(), calls=%async_computation.7 | async-start | bytes 5222400 | tf_op jit(solution)/shard_map/reduce_scatter | solution.py:237
  513.0 4.7 copy-start.13
  517.7 4.4 copy-start.35
  517.7 4.4 copy-start.49
  522.1 1.8 copy-start.7
  532.4 1.9 copy-start.11
  535.4 2.1 copy-start.39
  535.7 1.8 copy-start.41
  541.3 648.0 %all-reduce.5.cloned.1.call-start = ((), (), s32[]{:S(2)}) async-start(), calls=%async_computation.16 | async-start | bytes 2973696 | tf_op jit(solution)/shard_map/psum | solution.py:251
  692.6 325.8 %copy-start.38 = (bf16[12,64,197]{2,1,0:T(8,128)(2,1)S(1)}, bf16[12,64,197]{2,1,0:T(8,128)(2,1)}, u32[]{:S(2)}) copy-start(bf16[12,64,197]{2,1,0:T(8,128)(2,1)} %copy-done.37) | copy-start | bytes 907780
  692.6 325.8 %copy-start.40 = (bf16[12,64,197]{2,1,0:T(8,128)(2,1)S(1)}, bf16[12,64,197]{2,1,0:T(8,128)(2,1)}, u32[]{:S(2)}) copy-start(bf16[12,64,197]{2,1,0:T(8,128)(2,1)} %copy-done.39) | copy-start | bytes 907780
  692.6 325.8 %copy-start.42 = (bf16[12,64,197]{2,1,0:T(8,128)(2,1)S(1)}, bf16[12,64,197]{2,1,0:T(8,128)(2,1)}, u32[]{:S(2)}) copy-start(bf16[12,64,197]{2,1,0:T(8,128)(2,1)} %copy-done.41) | copy-start | bytes 907780
  1018.3 80.1 %copy-start.18 = (f32[197,2,128]{2,1,0:T(2,128)S(1)}, f32[197,2,128]{2,1,0:T(2,128)}, u32[]{:S(2)}) copy-start(f32[197,2,128]{2,1,0:T(2,128)} %copy-done.17) | copy-start | bytes 605188
  1018.4 80.1 %copy-start.27 = (bf16[1,128,768]{2,1,0:T(8,128)(2,1)S(1)}, bf16[1,128,768]{2,1,0:T(8,128)(2,1)}, u32[]{:S(2)}) copy-start(bf16[1,128,768]{2,1,0:T(8,128)(2,1)} %fusion.73) | copy-start | bytes 589828
  1018.4 80.1 %copy-start.29 = (bf16[1,128,768]{2,1,0:T(8,128)(2,1)S(1)}, bf16[1,128,768]{2,1,0:T(8,128)(2,1)}, u32[]{:S(2)}) copy-start(bf16[1,128,768]{2,1,0:T(8,128)(2,1)} %copy-done.28) | copy-start | bytes 589828
  1022.5 77.1 %copy-start.2 = (f32[197,768]{1,0:T(8,128)S(1)}, f32[197,768]{1,0:T(8,128)}, u32[]{:S(2)}) copy-start(f32[197,768]{1,0:T(8,128)} %copy-done) | copy-start | bytes 1815556
  1189.3 4.8 copy-start.32
  1189.3 5.9 copy-start.31
  (18 other events, 17.3 us)
Sparse Core Ops, SparseCore 0:
  10.7 76.2 all-gather.11
  89.7 52.1 all-gather.13
  145.2 76.9 all-gather.19
  224.8 76.5 all-gather.21
  304.5 76.5 all-gather.15
  383.7 76.5 all-gather.17
  477.7 103.8 reduce-scatter.13
  586.6 104.0 reduce-scatter.11
  695.0 103.9 reduce-scatter.9
  803.9 104.0 reduce-scatter.7
  912.4 105.8 reduce-scatter.5
  1022.2 167.0 all-reduce.4
where the time goes:
time: 1210 us; the launch traced here: 1200 us
  waiting for transfers between devices  940 us (78%)
  blocking collectives  106 us (9%)
  matrix products  81.6 us (7%)
  local copies, waits for them, and re-layouts  26.4 us (2%)
  other arithmetic  24 us (2%)
  between operations  15.2 us (1%)
    reduce_scatter x2, waiting for transfers between devices, body(): lax.psum_scatter(in_term(jnp.int32(0), shard_rows * lax.axis_size('shard'...  215 us
    reduce_scatter x2, waiting for transfers between devices, body(): lax.psum_scatter(out_term(jnp.int32(0), hid_rows * lax.axis_size('shard')...  149 us
    all_gather x2, waiting for transfers between devices, body(): lax.all_gather(w_expert_in[expert], 'shard', axis=0, tiled=True)  148 us
    all_gather x2, waiting for transfers between devices, body(): lax.all_gather(w_expert_out[expert], 'shard', axis=0, tiled=True)  143 us
    reduce_scatter x1, waiting for transfers between devices, body(): lax.psum_scatter(jnp.concatenate([jnp.einsum('rc,rk->ck', hidden1, grad_q...  108 us
    psum x1, waiting for transfers between devices, body(): lax.psum(dense_local, 'rep').astype(jnp.float32)  88.6 us
    psum x1, blocking collectives, body(): gain1_total, gain2_total = lax.psum((gain1, gain2), ('shard', 'rep'))  74.5 us
    all_gather x1, waiting for transfers between devices, body(): lax.all_gather(w_proj, 'shard', axis=0, tiled=True)  46.1 us
  transfers between devices with their start and end apart: 12, of which 12 were waited for; matrix products, arithmetic and copies ran while one was open for 9% of the time, Pallas kernels for 0%

commit v1 on v0

--- a/solution.py
+++ b/solution.py
@@ -29,6 +29,17 @@
         - normed * jnp.mean(scaled * normed, axis=-1, keepdims=True)
     )
     return (grad_in, jnp.sum(grad_out * normed, axis=0))
+
+
+def butterfly_sum(value, axis, size, wire=None):
+    step = 1
+    while step < size:
+        pairs = [(i, i ^ step) for i in range(size)]
+        sent = value if wire is None else value.astype(wire)
+        other = lax.ppermute(sent, axis, pairs)
+        value = sent.astype(jnp.float32) + other.astype(jnp.float32)
+        step *= 2
+    return value
 
 
 def heads_view(block, images):
@@ -120,10 +131,14 @@
     images = inputs.shape[0] // SEQ
     shard_rows = w_qkv.shape[0]
     hid_rows = w_expert_out.shape[1]
+    width = HEADS * HD
+    dense_all = lax.all_gather(
+        jnp.concatenate([w_qkv, w_proj, w_router], axis=1), "shard", axis=0, tiled=True
+    )
     full_qkv, full_proj, full_router = (
-        lax.all_gather(w_qkv, "shard", axis=0, tiled=True),
-        lax.all_gather(w_proj, "shard", axis=0, tiled=True),
-        lax.all_gather(w_router, "shard", axis=0, tiled=True),
+        dense_all[:, : 3 * width],
+        dense_all[:, 3 * width : 4 * width],
+        dense_all[:, 4 * width :],
     )
     x_float = inputs.astype(jnp.float32)
     normed1, inverse1, hidden1 = layer_norm(x_float, norm1_gain)
@@ -203,7 +218,7 @@
                 "shard",
                 scatter_dimension=0,
                 tiled=True,
-            ).astype(jnp.float32)
+            )
         )
         out_list.append(
             lax.psum_scatter(
@@ -211,7 +226,7 @@
                 "shard",
                 scatter_dimension=0,
                 tiled=True,
-            ).astype(jnp.float32)
+            )
         )
     grad_rows = jnp.stack(grad_rows_list)
     grad_probs = jnp.sum(grad_gate[:, :, None] * expert_hot, axis=1)
@@ -233,7 +248,11 @@
     )
     grad_norm1, gain1 = layer_norm_back(grad_hidden1, normed1, inverse1, norm1_gain)
     grad_inputs = grad_attended + grad_norm1
-    gain1_total, gain2_total = lax.psum((gain1, gain2), ("shard", "rep"))
+    n_shard = lax.axis_size("shard")
+    n_rep = lax.axis_size("rep")
+    gains = butterfly_sum(jnp.stack([gain1, gain2]), "shard", n_shard)
+    gains = butterfly_sum(gains, "rep", n_rep)
+    gain1_total, gain2_total = gains[0], gains[1]
     dense_local = lax.psum_scatter(
         jnp.concatenate(
             [
@@ -248,11 +267,10 @@
         tiled=True,
     )
     dense_total, in_total, out_total = (
-        lax.psum(dense_local, "rep").astype(jnp.float32),
-        lax.psum(jnp.stack(in_list).astype(jnp.bfloat16), "rep").astype(jnp.float32),
-        lax.psum(jnp.stack(out_list).astype(jnp.bfloat16), "rep").astype(jnp.float32),
-    )
-    width = HEADS * HD
+        butterfly_sum(dense_local, "rep", n_rep, jnp.bfloat16),
+        butterfly_sum(jnp.stack(in_list), "rep", n_rep, jnp.bfloat16),
+        butterfly_sum(jnp.stack(out_list), "rep", n_rep, jnp.bfloat16),
+    )
     return (
         outputs,
         grad_inputs,

time: 1210 us -> 1130 us (0.934)
  blocking collectives: 106 us -> 0 us
  waiting for transfers between devices: 940 us -> 960 us
  starting transfers between devices: 10.2 us -> 28 us
    ppermute x0 -> x20, waiting for transfers between devices: none -> 129 us  [butterfly_sum(): other = lax.ppermute(sent, axis, pairs)]
    psum x1 -> x0, waiting for transfers between devices: 88.6 us -> none  [body(): lax.psum(dense_local, 'rep').astype(jnp.float32)]
    reduce_scatter x1, waiting for transfers between devices: 108 us -> 32.3 us  [body(): lax.psum_scatter(jnp.concatenate([jnp.einsum('rc,rk->ck', hidden1, grad_q...]
    psum x1 -> x0, blocking collectives: 74.5 us -> none  [body(): gain1_total, gain2_total = lax.psum((gain1, gain2), ('shard', 'rep'))]
    reduce_scatter x2, waiting for transfers between devices: 149 us -> 216 us  [body(): lax.psum_scatter(out_term(jnp.int32(0), hid_rows * lax.axis_size('shard')...]
    all_gather x1 -> x0, blocking collectives: 31.6 us -> none  [body(): lax.all_gather(w_router, 'shard', axis=0, tiled=True)]
    ppermute x0 -> x20, starting transfers between devices: none -> 27.4 us  [butterfly_sum(): other = lax.ppermute(sent, axis, pairs)]
    all_gather x2 -> x1, waiting for transfers between devices: 84.7 us -> 78.7 us  [body(): lax.all_gather(jnp.concatenate([w_qkv, w_proj, w_router], axis=1), 'shard...]
  transfers between devices with their start and end apart: 12 -> 30, of which waited for: 12 -> 26; matrix products, arithmetic and copies ran while one was open for 9% -> 6% of each run, Pallas kernels for 0% -> 0%
where the time goes in v1:
time: 1130 us; the launch traced here: 1120 us
  waiting for transfers between devices  960 us (85%)
  matrix products  75.7 us (7%)
  starting transfers between devices  28 us (2%)
  other arithmetic  22.5 us (2%)
  local copies, waits for them, and re-layouts  21.3 us (2%)
  between operations  15.3 us (1%)
    reduce_scatter x2, waiting for transfers between devices, body(): lax.psum_scatter(in_term(jnp.int32(0), shard_rows * lax.axis_size('shard'...  217 us
    reduce_scatter x2, waiting for transfers between devices, body(): lax.psum_scatter(out_term(jnp.int32(0), hid_rows * lax.axis_size('shard')...  216 us
    all_gather x2, waiting for transfers between devices, body(): lax.all_gather(w_expert_out[expert], 'shard', axis=0, tiled=True)  143 us
    all_gather x2, waiting for transfers between devices, body(): lax.all_gather(w_expert_in[expert], 'shard', axis=0, tiled=True)  143 us
    ppermute x20, waiting for transfers between devices, butterfly_sum(): other = lax.ppermute(sent, axis, pairs)  129 us
    all_gather x1, waiting for transfers between devices, body(): lax.all_gather(jnp.concatenate([w_qkv, w_proj, w_router], axis=1), 'shard...  78.7 us
    reduce_scatter x1, waiting for transfers between devices, body(): lax.psum_scatter(jnp.concatenate([jnp.einsum('rc,rk->ck', hidden1, grad_q...  32.3 us
    ppermute x20, starting transfers between devices, butterfly_sum(): other = lax.ppermute(sent, axis, pairs)  27.4 us
  transfers between devices with their start and end apart: 30, of which 26 were waited for; matrix products, arithmetic and copies ran while one was open for 6% of the time, Pallas kernels for 0%

profile of v1, /device:TPU:8, one launch (start us, length us, event | category | flops | bytes accessed | tf_op | source)
XLA Modules:
  0.0 1123.3 jit_solution(11112674143956462636)
XLA Ops:
  9.9 1.9 fusion.138
  17.6 78.7 %all-gather.10.cloned.1.call-done = bf16[768,3104]{1,0:T(8,128)(2,1)} async-done(((bf16[48,3104]{1,0:T(8,128)(2,1)}), bf16[768,3104]{1,0:T(8,128)(2,1)}) %all-gather.10.cloned.1.call-update) | async-done | bytes 4767760 | tf_op jit(solution)/shard_map/all_gather | solution.py:135
  96.3 3.0 convolution_convert_fusion.5
  103.5 1.9 fusion.139
  109.0 67.2 %all-gather.16.cloned.1.call-done = bf16[1,768,3072]{2,1,0:T(8,128)(2,1)} async-done(((bf16[1,48,3072]{2,1,0:T(8,128)(2,1)}), bf16[1,768,3072]{2,1,0:T(8,128)(2,1)}) %all-gather.16.cloned.1.call-update) | async-done | bytes 4718608 | tf_op jit(solution)/shard_map/all_gather | solution.py:166
  176.2 7.7 fusion.37
  183.9 72.2 %all-gather.18.cloned.1.call-done = bf16[1,3072,768]{2,1,0:T(8,128)(2,1)} async-done(((bf16[1,192,768]{2,1,0:T(8,128)(2,1)}), bf16[1,3072,768]{2,1,0:T(8,128)(2,1)}) %all-gather.18.cloned.1.call-update) | async-done | bytes 4718608 | tf_op jit(solution)/shard_map/all_gather | solution.py:167
  256.1 4.1 fusion.76
  260.2 75.7 %all-gather.12.cloned.1.call-done = bf16[1,768,3072]{2,1,0:T(8,128)(2,1)} async-done(((bf16[1,48,3072]{2,1,0:T(8,128)(2,1)}), bf16[1,768,3072]{2,1,0:T(8,128)(2,1)}) %all-gather.12.cloned.1.call-update) | async-done | bytes 4718608 | tf_op jit(solution)/shard_map/all_gather | solution.py:166
  335.9 8.0 fusion.34
  343.9 71.2 %all-gather.14.cloned.1.call-done = bf16[1,3072,768]{2,1,0:T(8,128)(2,1)} async-done(((bf16[1,192,768]{2,1,0:T(8,128)(2,1)}), bf16[1,3072,768]{2,1,0:T(8,128)(2,1)}) %all-gather.14.cloned.1.call-update) | async-done | bytes 4718608 | tf_op jit(solution)/shard_map/all_gather | solution.py:167
  415.0 3.4 fusion.82
  419.6 7.1 fusion.104
  427.9 1.8 convolution_convert_fusion.8
  429.7 4.9 fusion.22
  442.7 2.6 convolution_convert_fusion.11
  446.4 2.0 copy.102
  454.4 2.4 convolution_convert_fusion.4
  456.8 2.4 pad_maximum_fusion
  460.5 3.7 convolution_convert_fusion.2
  465.3 3.5 convolution_convert_fusion.3
  470.2 3.6 convolution_convert_fusion
  474.9 3.6 convolution_convert_fusion.1
  479.5 3.8 fusion.101
  484.7 7.5 collective-permute-done.1
  493.2 2.8 collective-permute-done.2
  496.0 2.1 collective-permute-start.3
  498.1 3.1 collective-permute-done.3
  501.8 4.2 collective-permute-done.4
  506.1 18.0 %collective-permute-done.5 = f32[2,768]{1,0:T(2,128)S(1)} collective-permute-done((f32[2,768]{1,0:T(2,128)S(1)}, f32[2,768]{1,0:T(2,128)S(1)}, u32[]{:S(2)}, u32[]{:S(2)}) %collective-permute-start.5) | collective-permute-done | bytes 6176 | tf_op jit(solution)/shard_map/ppermute | solution.py:39
  527.7 3.0 collective-permute-start.7
  533.4 32.3 %reduce-scatter.6.cloned.1.call-done = bf16[48,3104]{1,0:T(8,128)(2,1)} async-done(((bf16[768,3104]{1,0:T(8,128)(2,1)}), bf16[48,3104]{1,0:T(8,128)(2,1)}) %reduce-scatter.6.cloned.1.call-update) | async-done | bytes 298000 | tf_op jit(solution)/shard_map/reduce_scatter | solution.py:256
  566.1 107.9 %reduce-scatter.10.cloned.1.call-done = bf16[48,3072]{1,0:T(8,128)(2,1)} async-done(((bf16[768,3072]{1,0:T(8,128)(2,1)}), bf16[48,3072]{1,0:T(8,128)(2,1)}) %reduce-scatter.10.cloned.1.call-update) | async-done | bytes 294928 | tf_op jit(solution)/shard_map/reduce_scatter | solution.py:216
  674.0 109.1 %reduce-scatter.8.cloned.1.call-done = bf16[48,3072]{1,0:T(8,128)(2,1)} async-done(((bf16[768,3072]{1,0:T(8,128)(2,1)}), bf16[48,3072]{1,0:T(8,128)(2,1)}) %reduce-scatter.8.cloned.1.call-update) | async-done | bytes 294928 | tf_op jit(solution)/shard_map/reduce_scatter | solution.py:216
  784.8 106.8 %reduce-scatter.14.cloned.1.call-done = bf16[192,768]{1,0:T(8,128)(2,1)} async-done(((bf16[3072,768]{1,0:T(8,128)(2,1)}), bf16[192,768]{1,0:T(8,128)(2,1)}) %reduce-scatter.14.cloned.1.call-update) | async-done | bytes 294928 | tf_op jit(solution)/shard_map/reduce_scatter | solution.py:224
  891.6 108.9 %reduce-scatter.12.cloned.1.call-done = bf16[192,768]{1,0:T(8,128)(2,1)} async-done(((bf16[3072,768]{1,0:T(8,128)(2,1)}), bf16[192,768]{1,0:T(8,128)(2,1)}) %reduce-scatter.12.cloned.1.call-update) | async-done | bytes 294928 | tf_op jit(solution)/shard_map/reduce_scatter | solution.py:224
  1003.5 2.2 collective-permute-start.13
  1005.7 20.2 %collective-permute-done.16 = bf16[2,192,768]{2,1,0:T(8,128)(2,1)S(1)} collective-permute-done((bf16[2,192,768]{2,1,0:T(8,128)(2,1)S(1)}, bf16[2,192,768]{2,1,0:T(8,128)(2,1)S(1)}, u32[]{:S(2)}, u32[]{:S(2)}) %collective-permute-start.16) | collective-permute-done | bytes 589856 | tf_op jit(solution)/shard_map/ppermute | solution.py:39
  1028.3 29.8 %collective-permute-done.13 = bf16[2,48,3072]{2,1,0:T(8,128)(2,1)S(1)} collective-permute-done((bf16[2,48,3072]{2,1,0:T(8,128)(2,1)S(1)}, bf16[2,48,3072]{2,1,0:T(8,128)(2,1)S(1)}, u32[]{:S(2)}, u32[]{:S(2)}) %collective-permute-start.13) | collective-permute-done | bytes 589856 | tf_op jit(solution)/shard_map/ppermute | solution.py:39
  1060.0 2.8 collective-permute-start.11
  1062.8 5.3 collective-permute-done.17
  1069.9 4.8 collective-permute-done.14
  1074.8 3.1 collective-permute-start.15
  1077.9 5.5 collective-permute-done.11
  1085.6 8.3 collective-permute-done.18
  1094.1 3.1 collective-permute-start.19
  1097.1 11.6 %collective-permute-done.15 = bf16[2,48,3072]{2,1,0:T(8,128)(2,1)S(1)} collective-permute-done((bf16[2,48,3072]{2,1,0:T(8,128)(2,1)S(1)}, bf16[2,48,3072]{2,1,0:T(8,128)(2,1)S(1)}, u32[]{:S(2)}, u32[]{:S(2)}) %collective-permute-start.15) | collective-permute-done | bytes 589856 | tf_op jit(solution)/shard_map/ppermute | solution.py:39
  1109.8 5.2 collective-permute-done.19
  (263 shorter events, 64.3 us)
Async XLA Ops:
  7.2 89.1 %all-gather.10.cloned.1.call-start = ((), (), s32[]{:S(2)}) async-start(), calls=%async_computation.5 | async-start | bytes 5222400 | tf_op jit(solution)/shard_map/all_gather | solution.py:135
  9.8 166.4 %all-gather.16.cloned.1.call-start = ((), (), s32[]{:S(2)}) async-start(), calls=%async_computation.13 | async-start | bytes 5013504 | tf_op jit(solution)/shard_map/all_gather | solution.py:166
  11.8 244.3 %all-gather.18.cloned.1.call-start = ((), (), s32[]{:S(2)}) async-start(), calls=%async_computation.14 | async-start | bytes 5013504 | tf_op jit(solution)/shard_map/all_gather | solution.py:167
  12.7 83.6 %copy-start.50 = (f32[768]{0:T(1024)S(1)}, f32[768]{0:T(1024)}, u32[]{:S(2)}) copy-start(f32[768]{0:T(1024)} %param.12) | copy-start | bytes 9220
  12.7 323.1 %all-gather.12.cloned.1.call-start = ((), (), s32[]{:S(2)}) async-start(), calls=%async_computation.11 | async-start | bytes 5013504 | tf_op jit(solution)/shard_map/all_gather | solution.py:166
  13.3 401.7 %all-gather.14.cloned.1.call-start = ((), (), s32[]{:S(2)}) async-start(), calls=%async_computation.12 | async-start | bytes 5013504 | tf_op jit(solution)/shard_map/all_gather | solution.py:167
  13.9 551.8 %reduce-scatter.6.cloned.1.call-start = ((), (), s32[]{:S(2)}) async-start(), calls=%async_computation.6 | async-start | bytes 5222400 | tf_op jit(solution)/shard_map/reduce_scatter | solution.py:256
  15.7 83.5 %copy-start.25 = (f32[197,2,2]{2,1,0:T(2,128)}, f32[197,2,2]{2,1,0:T(2,128)S(1)}, u32[]{:S(2)}) copy-start(f32[197,2,2]{2,1,0:T(2,128)S(1)} %copy.92) | copy-start | bytes 9460
  15.9 80.4 %copy-start.48 = (f32[197]{0:T(256)}, f32[197]{0:T(256)S(1)}, u32[]{:S(2)}) copy-start(f32[197]{0:T(256)S(1)} %broadcast_multiply_fusion.5) | copy-start | bytes 2368
  16.1 80.2 %copy-start.52 = (f32[197]{0:T(256)}, f32[197]{0:T(256)S(1)}, u32[]{:S(2)}) copy-start(f32[197]{0:T(256)S(1)} %add_rsqrt_fusion.1) | copy-start | bytes 2368
  16.4 82.9 %copy-start.27 = (f32[197,2,128]{2,1,0:T(2,128)}, f32[197,2,128]{2,1,0:T(2,128)S(1)}, u32[]{:S(2)}) copy-start(f32[197,2,128]{2,1,0:T(2,128)S(1)} %compare_convert_fusion) | copy-start | bytes 605188
  418.5 8.2 copy-start.36
  427.9 6.8 copy-start.4
  427.9 6.8 copy-start.55
  429.7 6.7 slice-start.2
  429.7 8.4 slice-start
  459.3 214.7 %reduce-scatter.10.cloned.1.call-start = ((), (), s32[]{:S(2)}) async-start(), calls=%async_computation.8 | async-start | bytes 5013504 | tf_op jit(solution)/shard_map/reduce_scatter | solution.py:216
  464.2 318.9 %reduce-scatter.8.cloned.1.call-start = ((), (), s32[]{:S(2)}) async-start(), calls=%async_computation.7 | async-start | bytes 5013504 | tf_op jit(solution)/shard_map/reduce_scatter | solution.py:216
  468.9 422.7 %reduce-scatter.14.cloned.1.call-start = ((), (), s32[]{:S(2)}) async-start(), calls=%async_computation.10 | async-start | bytes 5013504 | tf_op jit(solution)/shard_map/reduce_scatter | solution.py:224
  473.8 526.7 %reduce-scatter.12.cloned.1.call-start = ((), (), s32[]{:S(2)}) async-start(), calls=%async_computation.9 | async-start | bytes 5013504 | tf_op jit(solution)/shard_map/reduce_scatter | solution.py:224
  483.3 47.4 %copy-start.24 = (f32[197,2,128]{2,1,0:T(2,128)S(1)}, f32[197,2,128]{2,1,0:T(2,128)}, u32[]{:S(2)}) copy-start(f32[197,2,128]{2,1,0:T(2,128)} %get-tuple-element.52) | copy-start | bytes 605188
  483.3 47.4 %copy-start.35 = (bf16[1,128,768]{2,1,0:T(8,128)(2,1)S(1)}, bf16[1,128,768]{2,1,0:T(8,128)(2,1)}, u32[]{:S(2)}) copy-start(bf16[1,128,768]{2,1,0:T(8,128)(2,1)} %fusion.76) | copy-start | bytes 589828
  483.3 47.4 %copy-start.37 = (bf16[1,128,768]{2,1,0:T(8,128)(2,1)S(1)}, bf16[1,128,768]{2,1,0:T(8,128)(2,1)}, u32[]{:S(2)}) copy-start(bf16[1,128,768]{2,1,0:T(8,128)(2,1)} %copy-done.36) | copy-start | bytes 589828
  483.4 1.3 collective-permute-start
  484.6 7.6 collective-permute-start.1
  492.3 3.7 collective-permute-start.2
  496.0 5.1 collective-permute-start.3
  501.1 4.9 collective-permute-start.4
  506.1 18.0 %collective-permute-start.5 = (f32[2,768]{1,0:T(2,128)S(1)}, f32[2,768]{1,0:T(2,128)S(1)}, u32[]{:S(2)}, u32[]{:S(2)}) collective-permute-start(f32[2,768]{1,0:T(2,128)S(1)} %add.137), channel_id=1, source_target_pairs={{0,2},{1,3},{2,0},{3,1},{4,6},{5,7},{6,4},{7,5},{8,10},{9,11},{10,... | collective-permute-start | bytes 18440 | tf_op jit(solution)/shard_map/ppermute | solution.py:39
  524.1 3.6 collective-permute-start.6
  527.7 5.1 collective-permute-start.7
  565.7 436.6 %copy-start.42 = (bf16[48,3104]{1,0:T(8,128)(2,1)S(1)}, bf16[48,3104]{1,0:T(8,128)(2,1)}, u32[]{:S(2)}) copy-start(bf16[48,3104]{1,0:T(8,128)(2,1)} %reduce-scatter.6.cloned.1.call-done) | copy-start | bytes 893956
  565.7 436.6 %collective-permute-start.8 = (bf16[48,3104]{1,0:T(8,128)(2,1)}, bf16[48,3104]{1,0:T(8,128)(2,1)S(1)}, u32[]{:S(2)}, u32[]{:S(2)}) collective-permute-start(bf16[48,3104]{1,0:T(8,128)(2,1)} %reduce-scatter.6.cloned.1.call-done), channel_id=1, source_target_pairs={{0,1},{1,0},{2,3},{3,2},{4,5},{5,4},{6,7},{7,6},{8,9},{9,8},{10,11... | collective-permute-start | bytes 893960 | tf_op jit(solution)/shard_map/ppermute | solution.py:39
  783.1 220.3 %copy-start.20 = (bf16[48,3072]{1,0:T(8,128)(2,1)S(1)}, bf16[48,3072]{1,0:T(8,128)(2,1)}, u32[]{:S(2)}) copy-start(bf16[48,3072]{1,0:T(8,128)(2,1)} %reduce-scatter.10.cloned.1.call-done) | copy-start | bytes 884740
  783.1 220.3 %copy-start.22 = (bf16[48,3072]{1,0:T(8,128)(2,1)S(1)}, bf16[48,3072]{1,0:T(8,128)(2,1)}, u32[]{:S(2)}) copy-start(bf16[48,3072]{1,0:T(8,128)(2,1)} %reduce-scatter.8.cloned.1.call-done) | copy-start | bytes 884740
  784.2 219.1 %collective-permute-start.12 = (bf16[2,48,3072]{2,1,0:T(8,128)(2,1)S(1)}, bf16[2,48,3072]{2,1,0:T(8,128)(2,1)S(1)}, u32[]{:S(2)}, u32[]{:S(2)}) collective-permute-start(bf16[2,48,3072]{2,1,0:T(8,128)(2,1)S(1)} %pad_maximum_fusion.2), channel_id=1, source_target_pairs={{0,1},{1,0},{2,3},{3,2},{4,5},{5,4},{6,7},{7,6},{8,9},{9,8},{10,11... | collective-permute-start | bytes 1769480 | tf_op jit(solution)/shard_map/ppermute | solution.py:39
  1001.6 24.3 %copy-start.21 = (bf16[192,768]{1,0:T(8,128)(2,1)S(1)}, bf16[192,768]{1,0:T(8,128)(2,1)}, u32[]{:S(2)}) copy-start(bf16[192,768]{1,0:T(8,128)(2,1)} %reduce-scatter.14.cloned.1.call-done) | copy-start | bytes 884740
  1001.6 24.3 %copy-start.23 = (bf16[192,768]{1,0:T(8,128)(2,1)S(1)}, bf16[192,768]{1,0:T(8,128)(2,1)}, u32[]{:S(2)}) copy-start(bf16[192,768]{1,0:T(8,128)(2,1)} %reduce-scatter.12.cloned.1.call-done) | copy-start | bytes 884740
  1001.6 24.3 %collective-permute-start.16 = (bf16[2,192,768]{2,1,0:T(8,128)(2,1)S(1)}, bf16[2,192,768]{2,1,0:T(8,128)(2,1)S(1)}, u32[]{:S(2)}, u32[]{:S(2)}) collective-permute-start(bf16[2,192,768]{2,1,0:T(8,128)(2,1)S(1)} %pad_maximum_fusion.3), channel_id=1, source_target_pairs={{0,1},{1,0},{2,3},{3,2},{4,5},{5,4},{6,7},{7,6},{8,9},{9,8},{10,11... | collective-permute-start | bytes 1769480 | tf_op jit(solution)/shard_map/ppermute | solution.py:39
  1002.4 24.5 %collective-permute-start.9 = (bf16[48,3104]{1,0:T(8,128)(2,1)S(1)}, bf16[48,3104]{1,0:T(8,128)(2,1)S(1)}, u32[]{:S(2)}, u32[]{:S(2)}) collective-permute-start(bf16[48,3104]{1,0:T(8,128)(2,1)S(1)} %add_convert_fusion.8), channel_id=1, source_target_pairs={{0,2},{1,3},{2,0},{3,1},{4,6},{5,7},{6,4},{7,5},{8,10},{9,11},{10,... | collective-permute-start | bytes 893960 | tf_op jit(solution)/shard_map/ppermute | solution.py:39
  1003.5 54.6 %collective-permute-start.13 = (bf16[2,48,3072]{2,1,0:T(8,128)(2,1)S(1)}, bf16[2,48,3072]{2,1,0:T(8,128)(2,1)S(1)}, u32[]{:S(2)}, u32[]{:S(2)}) collective-permute-start(bf16[2,48,3072]{2,1,0:T(8,128)(2,1)S(1)} %add_convert_fusion.5), channel_id=1, source_target_pairs={{0,2},{1,3},{2,0},{3,1},{4,6},{5,7},{6,4},{7,5},{8,10},{9,11},{10,... | collective-permute-start | bytes 1769480 | tf_op jit(solution)/shard_map/ppermute | solution.py:39
  1026.1 42.0 %collective-permute-start.17 = (bf16[2,192,768]{2,1,0:T(8,128)(2,1)S(1)}, bf16[2,192,768]{2,1,0:T(8,128)(2,1)S(1)}, u32[]{:S(2)}, u32[]{:S(2)}) collective-permute-start(bf16[2,192,768]{2,1,0:T(8,128)(2,1)S(1)} %add_convert_fusion.2), channel_id=1, source_target_pairs={{0,2},{1,3},{2,0},{3,1},{4,6},{5,7},{6,4},{7,5},{8,10},{9,11},{10,... | collective-permute-start | bytes 1769480 | tf_op jit(solution)/shard_map/ppermute | solution.py:39
  1027.0 32.9 %collective-permute-start.10 = (bf16[48,3104]{1,0:T(8,128)(2,1)S(1)}, bf16[48,3104]{1,0:T(8,128)(2,1)S(1)}, u32[]{:S(2)}, u32[]{:S(2)}) collective-permute-start(bf16[48,3104]{1,0:T(8,128)(2,1)S(1)} %add_convert_fusion.7), channel_id=1, source_target_pairs={{0,4},{1,5},{2,6},{3,7},{4,0},{5,1},{6,2},{7,3},{8,12},{9,13},{10,... | collective-permute-start | bytes 893960 | tf_op jit(solution)/shard_map/ppermute | solution.py:39
  1058.3 16.4 %collective-permute-start.14 = (bf16[2,48,3072]{2,1,0:T(8,128)(2,1)S(1)}, bf16[2,48,3072]{2,1,0:T(8,128)(2,1)S(1)}, u32[]{:S(2)}, u32[]{:S(2)}) collective-permute-start(bf16[2,48,3072]{2,1,0:T(8,128)(2,1)S(1)} %add_convert_fusion.4), channel_id=1, source_target_pairs={{0,4},{1,5},{2,6},{3,7},{4,0},{5,1},{6,2},{7,3},{8,12},{9,13},{10,... | collective-permute-start | bytes 1769480 | tf_op jit(solution)/shard_map/ppermute | solution.py:39
  1060.0 23.4 %collective-permute-start.11 = (bf16[48,3104]{1,0:T(8,128)(2,1)S(1)}, bf16[48,3104]{1,0:T(8,128)(2,1)S(1)}, u32[]{:S(2)}, u32[]{:S(2)}) collective-permute-start(bf16[48,3104]{1,0:T(8,128)(2,1)S(1)} %add_convert_fusion.6), channel_id=1, source_target_pairs={{0,8},{1,9},{2,10},{3,11},{4,12},{5,13},{6,14},{7,15},{8,0},{9,1},... | collective-permute-start | bytes 893960 | tf_op jit(solution)/shard_map/ppermute | solution.py:39
  1068.3 25.6 %collective-permute-start.18 = (bf16[2,192,768]{2,1,0:T(8,128)(2,1)S(1)}, bf16[2,192,768]{2,1,0:T(8,128)(2,1)S(1)}, u32[]{:S(2)}, u32[]{:S(2)}) collective-permute-start(bf16[2,192,768]{2,1,0:T(8,128)(2,1)S(1)} %add_convert_fusion.1), channel_id=1, source_target_pairs={{0,4},{1,5},{2,6},{3,7},{4,0},{5,1},{6,2},{7,3},{8,12},{9,13},{10,... | collective-permute-start | bytes 1769480 | tf_op jit(solution)/shard_map/ppermute | solution.py:39
  1074.8 33.8 %collective-permute-start.15 = (bf16[2,48,3072]{2,1,0:T(8,128)(2,1)S(1)}, bf16[2,48,3072]{2,1,0:T(8,128)(2,1)S(1)}, u32[]{:S(2)}, u32[]{:S(2)}) collective-permute-start(bf16[2,48,3072]{2,1,0:T(8,128)(2,1)S(1)} %add_convert_fusion.3), channel_id=1, source_target_pairs={{0,8},{1,9},{2,10},{3,11},{4,12},{5,13},{6,14},{7,15},{8,0},{9,1},... | collective-permute-start | bytes 1769480 | tf_op jit(solution)/shard_map/ppermute | solution.py:39
  1094.1 21.0 %collective-permute-start.19 = (bf16[2,192,768]{2,1,0:T(8,128)(2,1)S(1)}, bf16[2,192,768]{2,1,0:T(8,128)(2,1)S(1)}, u32[]{:S(2)}, u32[]{:S(2)}) collective-permute-start(bf16[2,192,768]{2,1,0:T(8,128)(2,1)S(1)} %add_convert_fusion), channel_id=1, source_target_pairs={{0,8},{1,9},{2,10},{3,11},{4,12},{5,13},{6,14},{7,15},{8,0},{9,1},... | collective-permute-start | bytes 1769480 | tf_op jit(solution)/shard_map/ppermute | solution.py:39
  (42 other events, 89.9 us)
Sparse Core Ops, SparseCore 0:
  11.2 85.0 all-gather.9
  99.6 76.5 all-gather.15
  179.5 76.5 all-gather.17
  259.2 76.5 all-gather.11
  338.4 76.5 all-gather.13
  459.4 106.2 reduce-scatter.5
  570.1 103.8 reduce-scatter.9
  678.9 104.0 reduce-scatter.7
  787.4 104.0 reduce-scatter.13
  896.4 104.0 reduce-scatter.11

commit v2 on v1

--- a/solution.py
+++ b/solution.py
@@ -157,24 +157,14 @@
     expert_rows = jnp.einsum(
         "rec,rd->ecd", dispatch, hidden2, preferred_element_type=jnp.float32
     ).astype(jnp.bfloat16)
-    kept_weights = []
-    pre_list = []
-    activated_list = []
-    eout_list = []
-    for expert in range(E_WIN):
-        first, second = (
-            lax.all_gather(w_expert_in[expert], "shard", axis=0, tiled=True),
-            lax.all_gather(w_expert_out[expert], "shard", axis=0, tiled=True),
-        )
-        kept_weights.append((first, second))
-        pre = jnp.dot(expert_rows[expert], first, preferred_element_type=jnp.float32)
-        activated = jax.nn.gelu(pre, approximate=False).astype(jnp.bfloat16)
-        pre_list.append(pre)
-        activated_list.append(activated)
-        eout_list.append(
-            jnp.dot(activated, second, preferred_element_type=jnp.float32).astype(jnp.bfloat16)
-        )
-    expert_out = jnp.stack(eout_list)
+    w_in_cols = lax.all_to_all(w_expert_in, "shard", 2, 1, tiled=True)
+    rows_all = lax.all_gather(expert_rows, "shard", axis=1, tiled=True)
+    pre = jnp.einsum("erd,edh->erh", rows_all, w_in_cols, preferred_element_type=jnp.float32)
+    activated = jax.nn.gelu(pre, approximate=False).astype(jnp.bfloat16)
+    out_part = jnp.einsum(
+        "erh,ehd->erd", activated, w_expert_out, preferred_element_type=jnp.float32
+    ).astype(jnp.bfloat16)
+    expert_out = lax.psum_scatter(out_part, "shard", scatter_dimension=1, tiled=True)
     eout_float = expert_out.astype(jnp.float32)
     moe = jnp.einsum("rec,ecd->rd", combine, eout_float, precision=high)
     outputs = (attended + moe).astype(jnp.bfloat16)
@@ -183,52 +173,24 @@
     grad_gate = jnp.sum(masks * matched[:, None, :, :], axis=(2, 3))
     grad_eout = jnp.einsum("rec,rd->ecd", combine, grad, precision=high).astype(jnp.bfloat16)
     back_qkv, back_proj, back_router = (full_qkv, full_proj, full_router)
-    in_list = []
-    out_list = []
-    grad_rows_list = []
-    for expert in range(E_WIN):
-        first, second = kept_weights[expert]
-        pre = pre_list[expert]
-        grad_act = jnp.einsum(
-            "cd,hd->ch", grad_eout[expert], second, preferred_element_type=jnp.float32
-        )
-        slope = (
-            0.5 * (1.0 + jax.scipy.special.erf(pre * 0.7071067811865476))
-            + pre * jnp.exp(-0.5 * pre * pre) * 0.3989422804014327
-        )
-        grad_pre = (grad_act * slope).astype(jnp.bfloat16)
-        grad_rows_list.append(
-            jnp.einsum("ch,dh->cd", grad_pre, first, preferred_element_type=jnp.float32).astype(
-                jnp.bfloat16
-            )
-        )
-        rows_here = expert_rows[expert]
-        act_here = activated_list[expert]
-        eout_here = grad_eout[expert]
-
-        def in_term(start, count, rows_here=rows_here, grad_pre=grad_pre):
-            return jnp.einsum("cd,ch->dh", rows_here, grad_pre, preferred_element_type=jnp.float32)
-
-        def out_term(start, count, act_here=act_here, eout_here=eout_here):
-            return jnp.einsum("ch,cd->hd", act_here, eout_here, preferred_element_type=jnp.float32)
-
-        in_list.append(
-            lax.psum_scatter(
-                in_term(jnp.int32(0), shard_rows * lax.axis_size("shard")).astype(jnp.bfloat16),
-                "shard",
-                scatter_dimension=0,
-                tiled=True,
-            )
-        )
-        out_list.append(
-            lax.psum_scatter(
-                out_term(jnp.int32(0), hid_rows * lax.axis_size("shard")).astype(jnp.bfloat16),
-                "shard",
-                scatter_dimension=0,
-                tiled=True,
-            )
-        )
-    grad_rows = jnp.stack(grad_rows_list)
+    geout_all = lax.all_gather(grad_eout, "shard", axis=1, tiled=True)
+    grad_act = jnp.einsum(
+        "erd,ehd->erh", geout_all, w_expert_out, preferred_element_type=jnp.float32
+    )
+    slope = (
+        0.5 * (1.0 + jax.scipy.special.erf(pre * 0.7071067811865476))
+        + pre * jnp.exp(-0.5 * pre * pre) * 0.3989422804014327
+    )
+    grad_pre = (grad_act * slope).astype(jnp.bfloat16)
+    rows_part = jnp.einsum(
+        "erh,edh->erd", grad_pre, w_in_cols, preferred_element_type=jnp.float32
+    ).astype(jnp.bfloat16)
+    grad_rows = lax.psum_scatter(rows_part, "shard", scatter_dimension=1, tiled=True)
+    gin_cols = jnp.einsum("erd,erh->edh", rows_all, grad_pre, preferred_element_type=jnp.float32)
+    gin_local = lax.all_to_all(gin_cols.astype(jnp.bfloat16), "shard", 1, 2, tiled=True)
+    gout_local = jnp.einsum(
+        "erh,erd->ehd", activated, geout_all, preferred_element_type=jnp.float32
+    ).astype(jnp.bfloat16)
     grad_probs = jnp.sum(grad_gate[:, :, None] * expert_hot, axis=1)
     grad_logits = (
         router * (grad_probs - jnp.sum(router * grad_probs, axis=-1, keepdims=True))
@@ -268,8 +230,8 @@
     )
     dense_total, in_total, out_total = (
         butterfly_sum(dense_local, "rep", n_rep, jnp.bfloat16),
-        butterfly_sum(jnp.stack(in_list), "rep", n_rep, jnp.bfloat16),
-        butterfly_sum(jnp.stack(out_list), "rep", n_rep, jnp.bfloat16),
+        butterfly_sum(gin_local, "rep", n_rep, jnp.bfloat16),
+        butterfly_sum(gout_local, "rep", n_rep, jnp.bfloat16),
     )
     return (
         outputs,

time: 1130 us -> 788 us (0.70)
  waiting for transfers between devices: 960 us -> 570 us
  blocking collectives: 0 us -> 29.7 us
  local copies, waits for them, and re-layouts: 21.3 us -> 40.6 us
  matrix products: 75.7 us -> 59.2 us
  other arithmetic: 22.5 us -> 33.9 us
    reduce_scatter x4 -> x2, waiting for transfers between devices: 433 us -> 229 us  [the longest x1 115 us: body(): lax.psum_scatter(rows_part, 'shard', scatter_dimension=1, tiled=True)]
    all_gather x4 -> x2, waiting for transfers between devices: 286 us -> 139 us  [the longest x1 88.4 us: body(): geout_all = lax.all_gather(grad_eout, 'shard', axis=1, tiled=True)]
    reduce_scatter x1, waiting for transfers between devices: 32.3 us -> 0.01 us  [body(): lax.psum_scatter(jnp.concatenate([jnp.einsum('rc,rk->ck', hidden1, grad_q...]
    all_to_all x0 -> x1, blocking collectives: none -> 29.7 us  [body(): w_in_cols = lax.all_to_all(w_expert_in, 'shard', 2, 1, tiled=True)]
    ppermute x20, waiting for transfers between devices: 129 us -> 103 us  [butterfly_sum(): other = lax.ppermute(sent, axis, pairs)]
    all_to_all x0 -> x1, waiting for transfers between devices: none -> 19.8 us  [body(): lax.all_to_all(gin_cols.astype(jnp.bfloat16), 'shard', 1, 2, tiled=True)]
    dot_general x12 -> x6, matrix products: 47.5 us -> 31.6 us  [the longest x1 7.47 us: body(): jnp.einsum('erd,ehd->erh', geout_all, w_expert_out, preferred_element_typ...]
    unnamed x123 -> x96, local copies, waits for them, and re-layouts: 9.22 us -> 23.1 us
  transfers between devices with their start and end apart: 30 -> 27, of which waited for: 26 -> 20; matrix products, arithmetic and copies ran while one was open for 6% -> 6% of each run, Pallas kernels for 0% -> 0%
where the time goes in v2:
time: 788 us; the launch traced here: 781 us
  waiting for transfers between devices  570 us (72%)
  matrix products  59.2 us (8%)
  local copies, waits for them, and re-layouts  40.6 us (5%)
  other arithmetic  33.9 us (4%)
  starting transfers between devices  32.5 us (4%)
  blocking collectives  29.7 us (4%)
  between operations  15.2 us (2%)
    reduce_scatter x1, waiting for transfers between devices, body(): lax.psum_scatter(rows_part, 'shard', scatter_dimension=1, tiled=True)  115 us
    reduce_scatter x1, waiting for transfers between devices, body(): lax.psum_scatter(out_part, 'shard', scatter_dimension=1, tiled=True)  114 us
    ppermute x20, waiting for transfers between devices, butterfly_sum(): other = lax.ppermute(sent, axis, pairs)  103 us
    all_gather x1, waiting for transfers between devices, body(): geout_all = lax.all_gather(grad_eout, 'shard', axis=1, tiled=True)  88.4 us
    all_gather x1, waiting for transfers between devices, body(): lax.all_gather(jnp.concatenate([w_qkv, w_proj, w_router], axis=1), 'shard...  78.7 us
    all_gather x1, waiting for transfers between devices, body(): rows_all = lax.all_gather(expert_rows, 'shard', axis=1, tiled=True)  50.4 us
    all_to_all x1, blocking collectives, body(): w_in_cols = lax.all_to_all(w_expert_in, 'shard', 2, 1, tiled=True)  29.7 us
    ppermute x20, starting transfers between devices, butterfly_sum(): other = lax.ppermute(sent, axis, pairs)  27.5 us
  transfers between devices with their start and end apart: 27, of which 20 were waited for; matrix products, arithmetic and copies ran while one was open for 6% of the time, Pallas kernels for 0%

profile of v2, /device:TPU:8, one launch (start us, length us, event | category | flops | bytes accessed | tf_op | source)
XLA Modules:
  0.0 781.2 jit_solution(11249608258166544119)
XLA Ops:
  8.1 1.7 pad_maximum_fusion.4
  17.6 78.7 %all-gather.4.cloned.1.call-done = bf16[768,3104]{1,0:T(8,128)(2,1)} async-done(((bf16[48,3104]{1,0:T(8,128)(2,1)}), bf16[768,3104]{1,0:T(8,128)(2,1)}) %all-gather.4.cloned.1.call-update) | async-done | bytes 4767760 | tf_op jit(solution)/shard_map/all_gather | solution.py:135
  96.3 3.1 convolution_convert_fusion.3
  101.5 1.8 multiply_reduce_fusion
  104.5 1.9 fusion.68
  108.6 4.3 copy.160
  112.9 4.1 reshape.249
  117.0 29.7 %all_to_all.36 = bf16[16,2,9216]{2,1,0:T(2,128)(2,1)} all-to-all(bf16[16,2,9216]{2,1,0:T(2,128)(2,1)} %reshape.249), channel_id=1, replica_groups=mesh['shard'=16,'rep'=16] {'shard'}, dimensions={0} | all-to-all | bytes 1179648 | tf_op jit(solution)/shard_map/all_to_all | solution.py:160
  146.7 3.3 reshape.250
  150.1 4.7 copy.161
  154.8 50.4 %all-gather.6.cloned.1.call-done = bf16[2,2048,768]{2,1,0:T(8,128)(2,1)} async-done(((bf16[2,128,768]{2,1,0:T(8,128)(2,1)}), bf16[2,2048,768]{2,1,0:T(8,128)(2,1)}) %all-gather.6.cloned.1.call-update) | async-done | bytes 6291472 | tf_op jit(solution)/shard_map/all_gather | solution.py:161
  205.2 5.8 fusion.26
  211.0 1.7 copy-done.17
  212.7 7.2 fusion.2
  221.0 4.6 convolution_convert_fusion.2
  227.7 114.2 %reduce-scatter.4.cloned.1.call-done = bf16[2,128,768]{2,1,0:T(8,128)(2,1)} async-done(((bf16[2,2048,768]{2,1,0:T(8,128)(2,1)}), bf16[2,128,768]{2,1,0:T(8,128)(2,1)}) %reduce-scatter.4.cloned.1.call-update) | async-done | bytes 393232 | tf_op jit(solution)/shard_map/reduce_scatter | solution.py:167
  343.5 8.0 %fusion.41 = (f32[197,2]{1,0:T(8,128)}, f32[197,2,128]{2,1,0:T(2,128)S(1)}) fusion(f32[197,2,128]{2,1,0:T(2,128)S(1)} %copy.167, f32[197,2,128]{2,1,0:T(2,128)} %copy-done.24, f32[197,2,2]{2,1,0:T(2,128)} %copy-done.23, f32[197,2]{1,0:T(8,128)} %copy.158), kind=kLoop, calls=%fused_computation.107 | loop fusion | flops 453494 | bytes 611488 | tf_op jit(solution)/shard_map/reduce_sum | solution.py:173
  352.1 2.3 convolution_convert_fusion.8
  354.7 88.4 %all-gather.8.cloned.1.call-done = bf16[2,2048,768]{2,1,0:T(8,128)(2,1)} async-done(((bf16[2,128,768]{2,1,0:T(8,128)(2,1)}), bf16[2,2048,768]{2,1,0:T(8,128)(2,1)}) %all-gather.8.cloned.1.call-update) | async-done | bytes 6291472 | tf_op jit(solution)/shard_map/all_gather | solution.py:176
  443.1 7.5 fusion.8
  451.8 4.9 convolution_convert_fusion.1
  458.1 115.0 %reduce-scatter.6.cloned.1.call-done = bf16[2,128,768]{2,1,0:T(8,128)(2,1)} async-done(((bf16[2,2048,768]{2,1,0:T(8,128)(2,1)}), bf16[2,128,768]{2,1,0:T(8,128)(2,1)}) %reduce-scatter.6.cloned.1.call-update) | async-done | bytes 393232 | tf_op jit(solution)/shard_map/reduce_scatter | solution.py:188
  574.3 1.6 multiply_reduce_fusion.3
  578.1 2.5 convolution_convert_fusion.11
  581.8 2.0 copy.170
  588.9 2.3 pad_maximum_fusion
  592.6 4.3 convolution_convert_fusion.6
  597.4 4.5 convolution_convert_fusion.5
  602.0 1.8 copy.177
  603.8 4.5 all-to-all-start.1
  608.3 2.2 collective-permute-done.16
  611.6 19.8 %all-to-all-done.1 = bf16[2,768,192]{2,0,1:T(2,128)(2,1)S(1)} async-done(((bf16[2,768,192]{2,0,1:T(2,128)(2,1)}), bf16[2,768,192]{2,0,1:T(2,128)(2,1)S(1)}, u32[]{:S(2)}, u32[]{:S(2)}) %all-to-all-start.1) | async-done | bytes 589856 | tf_op jit(solution)/shard_map/all_to_all | solution.py:190
  632.6 2.5 collective-permute-start.12
  635.0 45.7 %collective-permute-done.17 = bf16[2,192,768]{2,1,0:T(8,128)(2,1)S(1)} collective-permute-done((bf16[2,192,768]{2,1,0:T(8,128)(2,1)S(1)}, bf16[2,192,768]{2,1,0:T(8,128)(2,1)S(1)}, u32[]{:S(2)}, u32[]{:S(2)}) %collective-permute-start.17) | collective-permute-done | bytes 589856 | tf_op jit(solution)/shard_map/ppermute | solution.py:39
  682.7 13.0 %collective-permute-done.18 = bf16[2,192,768]{2,1,0:T(8,128)(2,1)S(1)} collective-permute-done((bf16[2,192,768]{2,1,0:T(8,128)(2,1)S(1)}, bf16[2,192,768]{2,1,0:T(8,128)(2,1)S(1)}, u32[]{:S(2)}, u32[]{:S(2)}) %collective-permute-start.18) | collective-permute-done | bytes 589856 | tf_op jit(solution)/shard_map/ppermute | solution.py:39
  695.8 3.0 collective-permute-start.19
  698.9 3.6 fusion.38
  702.6 13.6 %collective-permute-done.13 = bf16[2,48,3072]{2,1,0:T(8,128)(2,1)S(1)} collective-permute-done((bf16[2,48,3072]{2,1,0:T(8,128)(2,1)S(1)}, bf16[2,48,3072]{2,1,0:T(8,128)(2,1)S(1)}, u32[]{:S(2)}, u32[]{:S(2)}) %collective-permute-start.13) | collective-permute-done | bytes 589856 | tf_op jit(solution)/shard_map/ppermute | solution.py:39
  717.1 4.8 collective-permute-start.1
  723.1 1.7 collective-permute-done.1
  726.7 1.7 collective-permute-done.2
  728.5 2.2 collective-permute-start.3
  733.1 2.8 collective-permute-start.15
  740.2 8.9 %collective-permute-done.15 = bf16[2,48,3072]{2,1,0:T(8,128)(2,1)S(1)} collective-permute-done((bf16[2,48,3072]{2,1,0:T(8,128)(2,1)S(1)}, bf16[2,48,3072]{2,1,0:T(8,128)(2,1)S(1)}, u32[]{:S(2)}, u32[]{:S(2)}) %collective-permute-start.15) | collective-permute-done | bytes 589856 | tf_op jit(solution)/shard_map/ppermute | solution.py:39
  750.4 2.6 collective-permute-done.9
  755.5 5.6 collective-permute-done.6
  761.1 2.2 collective-permute-start.7
  766.9 5.0 collective-permute-done.11
  (221 shorter events, 58.2 us)
Async XLA Ops:
  7.2 213.9 %copy-start = (bf16[2,192,768]{2,1,0:T(8,128)(2,1)S(1)}, bf16[2,192,768]{2,1,0:T(8,128)(2,1)}, u32[]{:S(2)}) copy-start(bf16[2,192,768]{2,1,0:T(8,128)(2,1)} %param.18) | copy-start | bytes 1769476
  7.2 89.1 %all-gather.4.cloned.1.call-start = ((), (), s32[]{:S(2)}) async-start(), calls=%async_computation.5 | async-start | bytes 5222400 | tf_op jit(solution)/shard_map/all_gather | solution.py:135
  9.8 195.3 %all-gather.6.cloned.1.call-start = ((), (), s32[]{:S(2)}) async-start(), calls=%async_computation.6 | async-start | bytes 6684672 | tf_op jit(solution)/shard_map/all_gather | solution.py:161
  13.7 85.7 %copy-start.23 = (f32[197,2,2]{2,1,0:T(2,128)}, f32[197,2,2]{2,1,0:T(2,128)S(1)}, u32[]{:S(2)}) copy-start(f32[197,2,2]{2,1,0:T(2,128)S(1)} %copy.156) | copy-start | bytes 9460
  14.9 84.5 %copy-start.40 = (f32[197]{0:T(256)}, f32[197]{0:T(256)S(1)}, u32[]{:S(2)}) copy-start(f32[197]{0:T(256)S(1)} %broadcast_multiply_fusion.5) | copy-start | bytes 2368
  16.1 83.3 %copy-start.43 = (f32[197]{0:T(256)}, f32[197]{0:T(256)S(1)}, u32[]{:S(2)}) copy-start(f32[197]{0:T(256)S(1)} %add_rsqrt_fusion.1) | copy-start | bytes 2368
  101.5 3.0 copy-start.9
  103.9 3.4 copy-start.38
  107.3 9.7 %copy-start.39 = (f32[197]{0:T(256)}, f32[197]{0:T(256)S(1)}, u32[]{:S(2)}) copy-start(f32[197]{0:T(256)S(1)} %add_rsqrt_fusion) | copy-start | bytes 2368
  108.5 233.5 %reduce-scatter.4.cloned.1.call-start = ((), (), s32[]{:S(2)}) async-start(), calls=%async_computation.7 | async-start | bytes 6684672 | tf_op jit(solution)/shard_map/reduce_scatter | solution.py:167
  225.6 217.5 %all-gather.8.cloned.1.call-start = ((), (), s32[]{:S(2)}) async-start(), calls=%async_computation.8 | async-start | bytes 6684672 | tf_op jit(solution)/shard_map/all_gather | solution.py:176
  354.4 218.6 %reduce-scatter.6.cloned.1.call-start = ((), (), s32[]{:S(2)}) async-start(), calls=%async_computation.9 | async-start | bytes 6684672 | tf_op jit(solution)/shard_map/reduce_scatter | solution.py:188
  443.1 8.7 %copy-start.15 = (bf16[2,48,16,192]{3,1,2,0:T(8,128)(2,1)S(1)}, bf16[2,48,16,192]{3,1,2,0:T(8,128)(2,1)}, u32[]{:S(2)}) copy-start(bf16[2,48,16,192]{3,1,2,0:T(8,128)(2,1)} %copy.161) | copy-start | bytes 1769476
  456.7 119.3 %copy-start.18 = (bf16[197,768]{1,0:T(8,128)(2,1)S(1)}, bf16[197,768]{1,0:T(8,128)(2,1)}, u32[]{:S(2)}) copy-start(bf16[197,768]{1,0:T(8,128)(2,1)} %param.21) | copy-start | bytes 907780
  456.7 274.0 %reduce-scatter.8.cloned.1.call-start = ((), (), s32[]{:S(2)}) async-start(), calls=%async_computation.10 | async-start | bytes 5222400 | tf_op jit(solution)/shard_map/reduce_scatter | solution.py:218
  575.9 8.0 %copy-start.36 = (f32[12,197]{1,0:T(8,128)S(1)}, f32[12,197]{1,0:T(8,128)}, u32[]{:S(2)}) copy-start(f32[12,197]{1,0:T(8,128)} %copy-done.35) | copy-start | bytes 28372
  580.6 4.6 copy-start.10
  584.4 3.1 copy-start.29
  592.6 4.8 copy-start.27
  596.9 13.6 %collective-permute-start.16 = (bf16[2,192,768]{2,1,0:T(8,128)(2,1)S(1)}, bf16[2,192,768]{2,1,0:T(8,128)(2,1)S(1)}, u32[]{:S(2)}, u32[]{:S(2)}) collective-permute-start(bf16[2,192,768]{2,1,0:T(8,128)(2,1)S(1)} %convolution_convert_fusion.6), channel_id=1, source_target_pairs={{0,1},{1,0},{2,3},{3,2},{4,5},{5,4},{6,7},{7,6},{8,9},{9,8},{10,11... | collective-permute-start | bytes 1769480 | tf_op jit(solution)/shard_map/ppermute | solution.py:39
  603.8 27.6 %all-to-all-start.1 = ((bf16[2,768,192]{2,0,1:T(2,128)(2,1)}), bf16[2,768,192]{2,0,1:T(2,128)(2,1)S(1)}, u32[]{:S(2)}, u32[]{:S(2)}) async-start(bf16[2,768,192]{2,0,1:T(2,128)(2,1)} %copy.177), calls=%async_computation.4 | async-start | bytes 1572864 | tf_op jit(solution)/shard_map/all_to_all | solution.py:190
  610.7 70.1 %collective-permute-start.17 = (bf16[2,192,768]{2,1,0:T(8,128)(2,1)S(1)}, bf16[2,192,768]{2,1,0:T(8,128)(2,1)S(1)}, u32[]{:S(2)}, u32[]{:S(2)}) collective-permute-start(bf16[2,192,768]{2,1,0:T(8,128)(2,1)S(1)} %add_convert_fusion.2), channel_id=1, source_target_pairs={{0,2},{1,3},{2,0},{3,1},{4,6},{5,7},{6,4},{7,5},{8,10},{9,11},{10,... | collective-permute-start | bytes 1769480 | tf_op jit(solution)/shard_map/ppermute | solution.py:39
  631.7 67.1 %copy-start.30 = (bf16[12,64,197]{2,1,0:T(8,128)(2,1)S(1)}, bf16[12,64,197]{2,1,0:T(8,128)(2,1)}, u32[]{:S(2)}) copy-start(bf16[12,64,197]{2,1,0:T(8,128)(2,1)} %copy-done.29) | copy-start | bytes 907780
  632.6 66.3 %copy-start.32 = (bf16[12,64,197]{2,1,0:T(8,128)(2,1)S(1)}, bf16[12,64,197]{2,1,0:T(8,128)(2,1)}, u32[]{:S(2)}) copy-start(bf16[12,64,197]{2,1,0:T(8,128)(2,1)} %copy-done.31) | copy-start | bytes 907780
  632.6 66.3 %copy-start.34 = (bf16[12,64,197]{2,1,0:T(8,128)(2,1)S(1)}, bf16[12,64,197]{2,1,0:T(8,128)(2,1)}, u32[]{:S(2)}) copy-start(bf16[12,64,197]{2,1,0:T(8,128)(2,1)} %copy-done.33) | copy-start | bytes 907780
  632.6 49.9 %collective-permute-start.12 = (bf16[2,48,3072]{2,1,0:T(8,128)(2,1)S(1)}, bf16[2,48,3072]{2,1,0:T(8,128)(2,1)S(1)}, u32[]{:S(2)}, u32[]{:S(2)}) collective-permute-start(bf16[2,48,3072]{2,1,0:T(8,128)(2,1)S(1)} %all_to_all.33), channel_id=1, source_target_pairs={{0,1},{1,0},{2,3},{3,2},{4,5},{5,4},{6,7},{7,6},{8,9},{9,8},{10,11... | collective-permute-start | bytes 1769480 | tf_op jit(solution)/shard_map/ppermute | solution.py:39
  680.9 14.8 %collective-permute-start.18 = (bf16[2,192,768]{2,1,0:T(8,128)(2,1)S(1)}, bf16[2,192,768]{2,1,0:T(8,128)(2,1)S(1)}, u32[]{:S(2)}, u32[]{:S(2)}) collective-permute-start(bf16[2,192,768]{2,1,0:T(8,128)(2,1)S(1)} %add_convert_fusion.1), channel_id=1, source_target_pairs={{0,4},{1,5},{2,6},{3,7},{4,0},{5,1},{6,2},{7,3},{8,12},{9,13},{10,... | collective-permute-start | bytes 1769480 | tf_op jit(solution)/shard_map/ppermute | solution.py:39
  682.6 33.7 %collective-permute-start.13 = (bf16[2,48,3072]{2,1,0:T(8,128)(2,1)S(1)}, bf16[2,48,3072]{2,1,0:T(8,128)(2,1)S(1)}, u32[]{:S(2)}, u32[]{:S(2)}) collective-permute-start(bf16[2,48,3072]{2,1,0:T(8,128)(2,1)S(1)} %add_convert_fusion.5), channel_id=1, source_target_pairs={{0,2},{1,3},{2,0},{3,1},{4,6},{5,7},{6,4},{7,5},{8,10},{9,11},{10,... | collective-permute-start | bytes 1769480 | tf_op jit(solution)/shard_map/ppermute | solution.py:39
  695.8 29.8 %collective-permute-start.19 = (bf16[2,192,768]{2,1,0:T(8,128)(2,1)S(1)}, bf16[2,192,768]{2,1,0:T(8,128)(2,1)S(1)}, u32[]{:S(2)}, u32[]{:S(2)}) collective-permute-start(bf16[2,192,768]{2,1,0:T(8,128)(2,1)S(1)} %add_convert_fusion), channel_id=1, source_target_pairs={{0,8},{1,9},{2,10},{3,11},{4,12},{5,13},{6,14},{7,15},{8,0},{9,1},... | collective-permute-start | bytes 1769480 | tf_op jit(solution)/shard_map/ppermute | solution.py:39
  698.9 23.0 %copy-start.3 = (f32[197,768]{1,0:T(8,128)S(1)}, f32[197,768]{1,0:T(8,128)}, u32[]{:S(2)}) copy-start(f32[197,768]{1,0:T(8,128)} %copy-done.2) | copy-start | bytes 1815556
  698.9 23.0 %copy-start.22 = (f32[197,2,128]{2,1,0:T(2,128)S(1)}, f32[197,2,128]{2,1,0:T(2,128)}, u32[]{:S(2)}) copy-start(f32[197,2,128]{2,1,0:T(2,128)} %copy-done.21) | copy-start | bytes 605188
  698.9 23.0 %copy-start.25 = (bf16[2,128,768]{2,1,0:T(8,128)(2,1)S(1)}, bf16[2,128,768]{2,1,0:T(8,128)(2,1)}, u32[]{:S(2)}) copy-start(bf16[2,128,768]{2,1,0:T(8,128)(2,1)} %reduce-scatter.4.cloned.1.call-done) | copy-start | bytes 1179652
  702.5 14.6 %collective-permute-start = (f32[2,768]{1,0:T(2,128)S(1)}, f32[2,768]{1,0:T(2,128)S(1)}, u32[]{:S(2)}, u32[]{:S(2)}) collective-permute-start(f32[2,768]{1,0:T(2,128)S(1)} %pad_maximum_fusion.5), channel_id=1, source_target_pairs={{0,16},{16,0},{32,48},{48,32},{64,80},{80,64},{96,112},{112,96},{1... | collective-permute-start | bytes 18440 | tf_op jit(solution)/shard_map/ppermute | solution.py:39
  716.4 15.4 %collective-permute-start.14 = (bf16[2,48,3072]{2,1,0:T(8,128)(2,1)S(1)}, bf16[2,48,3072]{2,1,0:T(8,128)(2,1)}, u32[]{:S(2)}, u32[]{:S(2)}) collective-permute-start(bf16[2,48,3072]{2,1,0:T(8,128)(2,1)S(1)} %add_convert_fusion.4), channel_id=1, source_target_pairs={{0,4},{1,5},{2,6},{3,7},{4,0},{5,1},{6,2},{7,3},{8,12},{9,13},{10,... | collective-permute-start | bytes 1769480 | tf_op jit(solution)/shard_map/ppermute | solution.py:39
  717.1 7.6 collective-permute-start.1
  724.8 3.7 collective-permute-start.2
  728.5 36.3 %copy-start.6 = (f32[197,768]{1,0:T(8,128)S(1)}, f32[197,768]{1,0:T(8,128)}, u32[]{:S(2)}) copy-start(f32[197,768]{1,0:T(8,128)} %copy-done.4) | copy-start | bytes 1815556
  728.5 7.4 collective-permute-start.3
  730.6 7.1 collective-permute-start.8
  733.1 16.0 %collective-permute-start.15 = (bf16[2,48,3072]{2,1,0:T(8,128)(2,1)S(1)}, bf16[2,48,3072]{2,1,0:T(8,128)(2,1)S(1)}, u32[]{:S(2)}, u32[]{:S(2)}) collective-permute-start(bf16[2,48,3072]{2,1,0:T(8,128)(2,1)S(1)} %add_convert_fusion.3), channel_id=1, source_target_pairs={{0,8},{1,9},{2,10},{3,11},{4,12},{5,13},{6,14},{7,15},{8,0},{9,1},... | collective-permute-start | bytes 1769480 | tf_op jit(solution)/shard_map/ppermute | solution.py:39
  735.9 14.4 %collective-permute-start.4 = (f32[2,768]{1,0:T(2,128)S(1)}, f32[2,768]{1,0:T(2,128)S(1)}, u32[]{:S(2)}, u32[]{:S(2)}) collective-permute-start(f32[2,768]{1,0:T(2,128)S(1)} %add.124), channel_id=1, source_target_pairs={{0,1},{1,0},{2,3},{3,2},{4,5},{5,4},{6,7},{7,6},{8,9},{9,8},{10,11... | collective-permute-start | bytes 18440 | tf_op jit(solution)/shard_map/ppermute | solution.py:39
  738.8 14.2 %collective-permute-start.9 = (bf16[48,3104]{1,0:T(8,128)(2,1)S(1)}, bf16[48,3104]{1,0:T(8,128)(2,1)S(1)}, u32[]{:S(2)}, u32[]{:S(2)}) collective-permute-start(bf16[48,3104]{1,0:T(8,128)(2,1)S(1)} %add_convert_fusion.8), channel_id=1, source_target_pairs={{0,2},{1,3},{2,0},{3,1},{4,6},{5,7},{6,4},{7,5},{8,10},{9,11},{10,... | collective-permute-start | bytes 893960 | tf_op jit(solution)/shard_map/ppermute | solution.py:39
  750.2 23.9 %copy-start.1 = (bf16[2,192,768]{2,1,0:T(8,128)(2,1)S(1)}, bf16[2,192,768]{2,1,0:T(8,128)(2,1)}, u32[]{:S(2)}) copy-start(bf16[2,192,768]{2,1,0:T(8,128)(2,1)} %param.18) | copy-start | bytes 1769476
  750.2 4.6 collective-permute-start.5
  753.0 10.3 %collective-permute-start.10 = (bf16[48,3104]{1,0:T(8,128)(2,1)S(1)}, bf16[48,3104]{1,0:T(8,128)(2,1)S(1)}, u32[]{:S(2)}, u32[]{:S(2)}) collective-permute-start(bf16[48,3104]{1,0:T(8,128)(2,1)S(1)} %add_convert_fusion.7), channel_id=1, source_target_pairs={{0,4},{1,5},{2,6},{3,7},{4,0},{5,1},{6,2},{7,3},{8,12},{9,13},{10,... | collective-permute-start | bytes 893960 | tf_op jit(solution)/shard_map/ppermute | solution.py:39
  754.9 6.2 collective-permute-start.6
  761.1 5.2 collective-permute-start.7
  763.4 8.5 %collective-permute-start.11 = (bf16[48,3104]{1,0:T(8,128)(2,1)S(1)}, bf16[48,3104]{1,0:T(8,128)(2,1)S(1)}, u32[]{:S(2)}, u32[]{:S(2)}) collective-permute-start(bf16[48,3104]{1,0:T(8,128)(2,1)S(1)} %add_convert_fusion.6), channel_id=1, source_target_pairs={{0,8},{1,9},{2,10},{3,11},{4,12},{5,13},{6,14},{7,15},{8,0},{9,1},... | collective-permute-start | bytes 893960 | tf_op jit(solution)/shard_map/ppermute | solution.py:39
  (24 other events, 34.4 us)
Sparse Core Ops, SparseCore 0:
  11.2 85.0 all-gather.3
  108.6 96.4 all-gather.5
  225.8 116.1 reduce-scatter.3
  354.5 88.5 all-gather.7
  456.8 116.1 reduce-scatter.5
  591.3 124.3 reduce-scatter.7

commit v3 on v2

--- a/solution.py
+++ b/solution.py
@@ -1,7 +1,7 @@
 import jax
 import jax.numpy as jnp
 from jax import lax
-from jax.sharding import PartitionSpec as P
+from jax.sharding import Mesh, PartitionSpec as P
 
 HEADS = 12
 HD = 64
@@ -9,6 +9,7 @@
 E_WIN = 2
 SEQ = 197
 CAP = 128
+SHARD = ("chip", "core")
 
 
 EPS = 1e-06
@@ -130,10 +131,11 @@
     high = lax.Precision.HIGHEST
     images = inputs.shape[0] // SEQ
     shard_rows = w_qkv.shape[0]
-    hid_rows = w_expert_out.shape[1]
+    n_chip = lax.axis_size("chip")
+    n_core = lax.axis_size("core")
     width = HEADS * HD
     dense_all = lax.all_gather(
-        jnp.concatenate([w_qkv, w_proj, w_router], axis=1), "shard", axis=0, tiled=True
+        jnp.concatenate([w_qkv, w_proj, w_router], axis=1), SHARD, axis=0, tiled=True
     )
     full_qkv, full_proj, full_router = (
         dense_all[:, : 3 * width],
@@ -157,14 +159,19 @@
     expert_rows = jnp.einsum(
         "rec,rd->ecd", dispatch, hidden2, preferred_element_type=jnp.float32
     ).astype(jnp.bfloat16)
-    w_in_cols = lax.all_to_all(w_expert_in, "shard", 2, 1, tiled=True)
-    rows_all = lax.all_gather(expert_rows, "shard", axis=1, tiled=True)
-    pre = jnp.einsum("erd,edh->erh", rows_all, w_in_cols, preferred_element_type=jnp.float32)
+    w_out_chip = lax.all_gather(w_expert_out, "core", axis=1, tiled=True)
+    w_in_part = lax.all_to_all(w_expert_in, "chip", 2, 1, tiled=True)
+    w_in_part = w_in_part.reshape(E_WIN, n_chip, shard_rows, -1)
+    w_in_chip = lax.all_gather(w_in_part, "core", axis=2, tiled=False).reshape(
+        E_WIN, n_chip * n_core * shard_rows, -1
+    )
+    rows_all = lax.all_gather(expert_rows, "chip", axis=1, tiled=True)
+    pre = jnp.einsum("erd,edh->erh", rows_all, w_in_chip, preferred_element_type=jnp.float32)
     activated = jax.nn.gelu(pre, approximate=False).astype(jnp.bfloat16)
     out_part = jnp.einsum(
-        "erh,ehd->erd", activated, w_expert_out, preferred_element_type=jnp.float32
-    ).astype(jnp.bfloat16)
-    expert_out = lax.psum_scatter(out_part, "shard", scatter_dimension=1, tiled=True)
+        "erh,ehd->erd", activated, w_out_chip, preferred_element_type=jnp.float32
+    ).astype(jnp.bfloat16)
+    expert_out = lax.psum_scatter(out_part, "chip", scatter_dimension=1, tiled=True)
     eout_float = expert_out.astype(jnp.float32)
     moe = jnp.einsum("rec,ecd->rd", combine, eout_float, precision=high)
     outputs = (attended + moe).astype(jnp.bfloat16)
@@ -173,9 +180,9 @@
     grad_gate = jnp.sum(masks * matched[:, None, :, :], axis=(2, 3))
     grad_eout = jnp.einsum("rec,rd->ecd", combine, grad, precision=high).astype(jnp.bfloat16)
     back_qkv, back_proj, back_router = (full_qkv, full_proj, full_router)
-    geout_all = lax.all_gather(grad_eout, "shard", axis=1, tiled=True)
+    geout_all = lax.all_gather(grad_eout, "chip", axis=1, tiled=True)
     grad_act = jnp.einsum(
-        "erd,ehd->erh", geout_all, w_expert_out, preferred_element_type=jnp.float32
+        "erd,ehd->erh", geout_all, w_out_chip, preferred_element_type=jnp.float32
     )
     slope = (
         0.5 * (1.0 + jax.scipy.special.erf(pre * 0.7071067811865476))
@@ -183,14 +190,17 @@
     )
     grad_pre = (grad_act * slope).astype(jnp.bfloat16)
     rows_part = jnp.einsum(
-        "erh,edh->erd", grad_pre, w_in_cols, preferred_element_type=jnp.float32
-    ).astype(jnp.bfloat16)
-    grad_rows = lax.psum_scatter(rows_part, "shard", scatter_dimension=1, tiled=True)
-    gin_cols = jnp.einsum("erd,erh->edh", rows_all, grad_pre, preferred_element_type=jnp.float32)
-    gin_local = lax.all_to_all(gin_cols.astype(jnp.bfloat16), "shard", 1, 2, tiled=True)
-    gout_local = jnp.einsum(
+        "erh,edh->erd", grad_pre, w_in_chip, preferred_element_type=jnp.float32
+    ).astype(jnp.bfloat16)
+    grad_rows = lax.psum_scatter(rows_part, "chip", scatter_dimension=1, tiled=True)
+    gin_chip = jnp.einsum("erd,erh->edh", rows_all, grad_pre, preferred_element_type=jnp.float32)
+    gin_chip = gin_chip.astype(jnp.bfloat16).reshape(E_WIN, n_chip, n_core, shard_rows, -1)
+    gin_core = lax.psum_scatter(gin_chip, "core", scatter_dimension=2, tiled=True)
+    gin_local = lax.all_to_all(gin_core, "chip", 1, 4, tiled=True).reshape(E_WIN, shard_rows, -1)
+    gout_chip = jnp.einsum(
         "erh,erd->ehd", activated, geout_all, preferred_element_type=jnp.float32
     ).astype(jnp.bfloat16)
+    gout_local = lax.psum_scatter(gout_chip, "core", scatter_dimension=1, tiled=True)
     grad_probs = jnp.sum(grad_gate[:, :, None] * expert_hot, axis=1)
     grad_logits = (
         router * (grad_probs - jnp.sum(router * grad_probs, axis=-1, keepdims=True))
@@ -210,9 +220,9 @@
     )
     grad_norm1, gain1 = layer_norm_back(grad_hidden1, normed1, inverse1, norm1_gain)
     grad_inputs = grad_attended + grad_norm1
-    n_shard = lax.axis_size("shard")
+    n_shard = n_chip * n_core
     n_rep = lax.axis_size("rep")
-    gains = butterfly_sum(jnp.stack([gain1, gain2]), "shard", n_shard)
+    gains = butterfly_sum(jnp.stack([gain1, gain2]), SHARD, n_shard)
     gains = butterfly_sum(gains, "rep", n_rep)
     gain1_total, gain2_total = gains[0], gains[1]
     dense_local = lax.psum_scatter(
@@ -224,7 +234,7 @@
             ],
             axis=1,
         ).astype(jnp.bfloat16),
-        "shard",
+        SHARD,
         scatter_dimension=0,
         tiled=True,
     )
@@ -248,27 +258,29 @@
 
 def solution(mesh):
     in_specs = (
-        P(("shard", "rep"), None),
-        P(),
-        P("shard", None),
-        P("shard", None),
-        P(),
-        P("shard", None),
-        P(None, "shard", None),
-        P(None, "shard", None),
-        P(("shard", "rep"), None),
-        P(),
-        P(("shard", "rep"), None),
+        P(("chip", "core", "rep"), None),
+        P(),
+        P(SHARD, None),
+        P(SHARD, None),
+        P(),
+        P(SHARD, None),
+        P(None, SHARD, None),
+        P(None, SHARD, None),
+        P(("chip", "core", "rep"), None),
+        P(),
+        P(("chip", "core", "rep"), None),
     )
     out_specs = (
-        P(("shard", "rep"), None),
-        P(("shard", "rep"), None),
-        P(),
-        P("shard", None),
-        P("shard", None),
-        P(),
-        P("shard", None),
-        P(None, "shard", None),
-        P(None, "shard", None),
-    )
-    return jax.shard_map(body, mesh=mesh, in_specs=in_specs, out_specs=out_specs, check_vma=False)
+        P(("chip", "core", "rep"), None),
+        P(("chip", "core", "rep"), None),
+        P(),
+        P(SHARD, None),
+        P(SHARD, None),
+        P(),
+        P(SHARD, None),
+        P(None, SHARD, None),
+        P(None, SHARD, None),
+    )
+    n_shard, n_rep = mesh.devices.shape
+    split = Mesh(mesh.devices.reshape(n_shard // 2, 2, n_rep), ("chip", "core", "rep"))
+    return jax.shard_map(body, mesh=split, in_specs=in_specs, out_specs=out_specs, check_vma=False)

time: 788 us -> 796 us (1.010)
  waiting for transfers between devices: 570 us -> 583 us
  local copies, waits for them, and re-layouts: 40.6 us -> 31.1 us
  starting transfers between devices: 32.5 us -> 41.3 us
    reduce_scatter x2 -> x3, waiting for transfers between devices: 229 us -> 201 us  [the longest x1 107 us: body(): lax.psum_scatter(out_part, 'chip', scatter_dimension=1, tiled=True)]
    reduce_scatter x1, waiting for transfers between devices: 0.01 us -> 16.5 us  [body(): lax.psum_scatter(jnp.concatenate([jnp.einsum('rc,rk->ck', hidden1, grad_q...]
    all_gather x3 -> x5, waiting for transfers between devices: 217 us -> 233 us  [the longest x1 95.7 us: body(): rows_all = lax.all_gather(expert_rows, 'chip', axis=1, tiled=True)]
    unnamed x6 -> x11, waiting for transfers between devices: 0.1 us -> 8.84 us
    unnamed x96 -> x84, local copies, waits for them, and re-layouts: 23.1 us -> 17.6 us
  transfers between devices with their start and end apart: 27 -> 31, of which waited for: 20 -> 20; matrix products, arithmetic and copies ran while one was open for 6% -> 11% of each run, Pallas kernels for 0% -> 0%
where the time goes in v3:
time: 796 us; the launch traced here: 790 us
  waiting for transfers between devices  583 us (73%)
  matrix products  59.6 us (7%)
  starting transfers between devices  41.3 us (5%)
  other arithmetic  32.4 us (4%)
  local copies, waits for them, and re-layouts  31.1 us (4%)
  blocking collectives  27 us (3%)
  between operations  15.5 us (2%)
    reduce_scatter x1, waiting for transfers between devices, body(): lax.psum_scatter(out_part, 'chip', scatter_dimension=1, tiled=True)  107 us
    ppermute x20, waiting for transfers between devices, butterfly_sum(): other = lax.ppermute(sent, axis, pairs)  103 us
    all_gather x1, waiting for transfers between devices, body(): rows_all = lax.all_gather(expert_rows, 'chip', axis=1, tiled=True)  95.7 us
    reduce_scatter x1, waiting for transfers between devices, body(): lax.psum_scatter(rows_part, 'chip', scatter_dimension=1, tiled=True)  93.5 us
    all_gather x1, waiting for transfers between devices, body(): geout_all = lax.all_gather(grad_eout, 'chip', axis=1, tiled=True)  87.4 us
    all_gather x1, waiting for transfers between devices, body(): lax.all_gather(jnp.concatenate([w_qkv, w_proj, w_router], axis=1), SHARD,...  48.5 us
    ppermute x20, starting transfers between devices, butterfly_sum(): other = lax.ppermute(sent, axis, pairs)  29 us
    all_to_all x1, blocking collectives, body(): lax.all_to_all(gin_core, 'chip', 1, 4, tiled=True)  27 us
  transfers between devices with their start and end apart: 31, of which 20 were waited for; matrix products, arithmetic and copies ran while one was open for 11% of the time, Pallas kernels for 0%

profile of v3, /device:TPU:8, one launch (start us, length us, event | category | flops | bytes accessed | tf_op | source)
XLA Modules:
  0.0 789.8 jit_solution(2400998380782752619)
XLA Ops:
  8.0 1.8 pad_maximum_fusion.4
  9.8 3.7 copy.161
  13.5 3.4 reshape.268
  16.8 11.5 %all-to-all-start = ((bf16[8,2,18432]{2,1,0:T(2,128)(2,1)}), bf16[8,2,18432]{2,1,0:T(2,128)(2,1)S(1)}, u32[]{:S(2)}, u32[]{:S(2)}) async-start(bf16[8,2,18432]{2,1,0:T(2,128)(2,1)} %reshape.268), calls=%async_computation | async-start | bytes 1179648 | tf_op jit(solution)/shard_map/all_to_all | solution.py:163
  32.1 20.7 %all-to-all-done = bf16[8,2,18432]{2,1,0:T(2,128)(2,1)S(1)} async-done(((bf16[8,2,18432]{2,1,0:T(2,128)(2,1)}), bf16[8,2,18432]{2,1,0:T(2,128)(2,1)S(1)}, u32[]{:S(2)}, u32[]{:S(2)}) %all-to-all-start) | async-done | bytes 589856 | tf_op jit(solution)/shard_map/all_to_all | solution.py:163
  54.3 2.6 copy.162
  57.0 48.5 %all-gather.7.cloned.1.call-done = bf16[768,3104]{1,0:T(8,128)(2,1)} async-done(((bf16[48,3104]{1,0:T(8,128)(2,1)}), bf16[768,3104]{1,0:T(8,128)(2,1)}) %all-gather.7.cloned.1.call-update) | async-done | bytes 4767760 | tf_op jit(solution)/shard_map/all_gather | solution.py:137
  105.5 3.0 convolution_convert_fusion.1
  112.7 1.9 fusion.68
  118.3 95.7 %all-gather.9.cloned.1.call-done = bf16[2,1024,768]{2,1,0:T(8,128)(2,1)} async-done(((bf16[2,128,768]{2,1,0:T(8,128)(2,1)}), bf16[2,1024,768]{2,1,0:T(8,128)(2,1)}) %all-gather.9.cloned.1.call-update) | async-done | bytes 3145744 | tf_op jit(solution)/shard_map/all_gather | solution.py:168
  214.0 4.6 fusion.26
  218.6 1.7 copy-done.11
  220.4 8.0 %fusion.2 = bf16[2,1024,384]{2,1,0:T(8,128)(2,1)} fusion(f32[2,1024,384]{2,1,0:T(8,128)S(1)} %get-tuple-element.82, u8[1024,384]{1,0:T(8,128)(4,1)S(1)} %get-tuple-element.64, u8[1024,384]{1,0:T(8,128)(4,1)S(1)} %get-tuple-element.63), kind=kLoop, calls=%fused_computation.7 | loop fusion | flops 55050240 | bytes 5505024 | tf_op jit(solution)/shard_map/convert_element_type | solution.py:170
  228.4 5.3 convolution_convert_fusion.3
  235.8 107.5 %reduce-scatter.8.cloned.1.call-done = bf16[2,128,768]{2,1,0:T(8,128)(2,1)} async-done(((bf16[2,1024,768]{2,1,0:T(8,128)(2,1)}), bf16[2,128,768]{2,1,0:T(8,128)(2,1)}) %reduce-scatter.8.cloned.1.call-update) | async-done | bytes 393232 | tf_op jit(solution)/shard_map/reduce_scatter | solution.py:174
  344.7 7.4 fusion.41
  352.8 2.3 convolution_convert_fusion.8
  355.2 87.4 %all-gather.13.cloned.1.call-done = bf16[2,1024,768]{2,1,0:T(8,128)(2,1)} async-done(((bf16[2,128,768]{2,1,0:T(8,128)(2,1)}), bf16[2,1024,768]{2,1,0:T(8,128)(2,1)}) %all-gather.13.cloned.1.call-update) | async-done | bytes 3145744 | tf_op jit(solution)/shard_map/all_gather | solution.py:183
  442.6 5.6 fusion.8
  449.4 3.6 convolution_convert_fusion.2
  453.2 5.2 convolution_convert_fusion.5
  460.9 4.9 convolution_convert_fusion.4
  465.8 93.5 %reduce-scatter.10.cloned.1.call-done = bf16[2,128,768]{2,1,0:T(8,128)(2,1)} async-done(((bf16[2,1024,768]{2,1,0:T(8,128)(2,1)}), bf16[2,128,768]{2,1,0:T(8,128)(2,1)}) %reduce-scatter.10.cloned.1.call-update) | async-done | bytes 393232 | tf_op jit(solution)/shard_map/reduce_scatter | solution.py:195
  564.1 2.5 convolution_convert_fusion.11
  566.6 1.9 copy.168
  568.5 2.0 copy.169
  572.1 1.9 multiply_convert_fusion
  577.4 2.4 pad_maximum_fusion
  581.1 8.2 %all-reduce.4.cloned.1.call-done = bf16[2,8,2,48,384]{4,3,2,1,0:T(8,128)(2,1)} async-done(((bf16[2,8,2,48,384]{4,3,2,1,0:T(8,128)(2,1)}), bf16[2,8,2,48,384]{4,3,2,1,0:T(8,128)(2,1)}) %all-reduce.4.cloned.1.call-update) | async-done | bytes 1179664
  589.3 1.8 constant_dynamic-slice_fusion
  591.1 27.0 %all_to_all.30 = bf16[2,8,1,48,384]{4,3,2,0,1:T(8,128)(2,1)S(1)} all-to-all(bf16[2,8,1,48,384]{4,3,2,0,1:T(8,128)(2,1)S(1)} %copy.177), channel_id=1, replica_groups=mesh['chip'=8,'core'=2,'rep'=16] {'chip'}, dimensions={1} | all-to-all | bytes 1179648 | tf_op jit(solution)/shard_map/all_to_all | solution.py:199
  618.5 3.7 collective-permute-start.12
  622.4 14.1 %collective-permute-done.12 = bf16[2,48,3072]{2,1,0:T(8,128)(2,1)S(1)} collective-permute-done((bf16[2,48,3072]{2,1,0:T(8,128)(2,1)S(1)}, bf16[2,48,3072]{2,1,0:T(8,128)(2,1)S(1)}, u32[]{:S(2)}, u32[]{:S(2)}) %collective-permute-start.12) | collective-permute-done | bytes 589856 | tf_op jit(solution)/shard_map/ppermute | solution.py:40
  636.6 2.2 collective-permute-start.13
  638.8 2.3 fusion.22
  641.1 25.5 %collective-permute-done.16 = bf16[2,192,768]{2,1,0:T(8,128)(2,1)S(1)} collective-permute-done((bf16[2,192,768]{2,1,0:T(8,128)(2,1)}, bf16[2,192,768]{2,1,0:T(8,128)(2,1)S(1)}, u32[]{:S(2)}, u32[]{:S(2)}) %collective-permute-start.16) | collective-permute-done | bytes 589856 | tf_op jit(solution)/shard_map/ppermute | solution.py:40
  666.7 2.9 collective-permute-start.17
  669.6 33.8 %collective-permute-done.13 = bf16[2,48,3072]{2,1,0:T(8,128)(2,1)S(1)} collective-permute-done((bf16[2,48,3072]{2,1,0:T(8,128)(2,1)S(1)}, bf16[2,48,3072]{2,1,0:T(8,128)(2,1)S(1)}, u32[]{:S(2)}, u32[]{:S(2)}) %collective-permute-start.13) | collective-permute-done | bytes 589856 | tf_op jit(solution)/shard_map/ppermute | solution.py:40
  705.1 4.6 fusion.38
  709.9 4.7 collective-permute-done.17
  717.3 2.8 collective-permute-start.15
  720.1 16.5 %reduce-scatter.12.cloned.1.call-done = bf16[48,3104]{1,0:T(8,128)(2,1)} async-done(((bf16[768,3104]{1,0:T(8,128)(2,1)}), bf16[48,3104]{1,0:T(8,128)(2,1)}) %reduce-scatter.12.cloned.1.call-update) | async-done | bytes 298000 | tf_op jit(solution)/shard_map/reduce_scatter | solution.py:228
  738.0 3.0 collective-permute-start.19
  748.0 8.0 %collective-permute-done.19 = bf16[2,192,768]{2,1,0:T(8,128)(2,1)S(1)} collective-permute-done((bf16[2,192,768]{2,1,0:T(8,128)(2,1)S(1)}, bf16[2,192,768]{2,1,0:T(8,128)(2,1)S(1)}, u32[]{:S(2)}, u32[]{:S(2)}) %collective-permute-start.19) | collective-permute-done | bytes 589856 | tf_op jit(solution)/shard_map/ppermute | solution.py:40
  757.3 1.7 collective-permute-done.9
  762.0 6.0 collective-permute-done.6
  768.1 3.1 collective-permute-start.7
  773.8 6.5 collective-permute-done.11
  (220 shorter events, 55.7 us)
Async XLA Ops:
  7.2 98.4 %all-gather.7.cloned.1.call-start = ((), (), s32[]{:S(2)}) async-start(), calls=%async_computation.6 | async-start | bytes 5222400 | tf_op jit(solution)/shard_map/all_gather | solution.py:137
  8.0 20.4 %copy-start.26 = (s32[197,2]{0,1:T(2,128)S(1)}, s32[197,2]{0,1:T(2,128)}, u32[]{:S(2)}) copy-start(s32[197,2]{0,1:T(2,128)} %param.19) | copy-start | bytes 4732
  8.0 21.7 %copy-start.34 = (s32[2]{0:T(128)S(1)}, s32[2]{0:T(128)}, u32[]{:S(2)}) copy-start(s32[2]{0:T(128)} %param.20) | copy-start | bytes 28
  8.0 21.8 %copy-start.12 = (bf16[197,768]{1,0:T(8,128)(2,1)S(1)}, bf16[197,768]{1,0:T(8,128)(2,1)}, u32[]{:S(2)}) copy-start(bf16[197,768]{1,0:T(8,128)(2,1)} %param.11) | copy-start | bytes 907780
  16.8 35.9 %all-to-all-start = ((bf16[8,2,18432]{2,1,0:T(2,128)(2,1)}), bf16[8,2,18432]{2,1,0:T(2,128)(2,1)S(1)}, u32[]{:S(2)}, u32[]{:S(2)}) async-start(bf16[8,2,18432]{2,1,0:T(2,128)(2,1)} %reshape.268), calls=%async_computation | async-start | bytes 1179648 | tf_op jit(solution)/shard_map/all_to_all | solution.py:163
  28.4 89.9 %all-gather.15.cloned.1.call-start = ((), (), s32[]{:S(2)}) async-start(), calls=%async_computation.14 | async-start | bytes 1769472 | tf_op jit(solution)/shard_map/all_gather | solution.py:165
  30.0 75.5 %copy-start.28 = (f32[197]{0:T(256)}, f32[197]{0:T(256)S(1)}, u32[]{:S(2)}) copy-start(f32[197]{0:T(256)S(1)} %broadcast_multiply_fusion.5) | copy-start | bytes 2368
  30.1 75.4 %copy-start.30 = (f32[768]{0:T(1024)S(1)}, f32[768]{0:T(1024)}, u32[]{:S(2)}) copy-start(f32[768]{0:T(1024)} %param.12) | copy-start | bytes 9220
  30.6 77.9 %copy-start.32 = (f32[197]{0:T(256)}, f32[197]{0:T(256)S(1)}, u32[]{:S(2)}) copy-start(f32[197]{0:T(256)S(1)} %add_rsqrt_fusion.1) | copy-start | bytes 2368
  57.0 157.0 %all-gather.9.cloned.1.call-start = ((), (), s32[]{:S(2)}) async-start(), calls=%async_computation.7 | async-start | bytes 3538944 | tf_op jit(solution)/shard_map/all_gather | solution.py:168
  108.8 3.3 copy-start.6
  109.9 2.8 copy-start.3
  112.1 2.8 copy-start.27
  112.1 3.0 copy-start.18
  116.2 112.2 %all-gather.11.cloned.1.call-start = ((), (), s32[]{:S(2)}) async-start(), calls=%async_computation.8 | async-start | bytes 1769472 | tf_op jit(solution)/shard_map/all_gather | solution.py:162
  116.8 226.5 %reduce-scatter.8.cloned.1.call-start = ((), (), s32[]{:S(2)}) async-start(), calls=%async_computation.9 | async-start | bytes 3538944 | tf_op jit(solution)/shard_map/reduce_scatter | solution.py:174
  233.7 208.9 %all-gather.13.cloned.1.call-start = ((), (), s32[]{:S(2)}) async-start(), calls=%async_computation.10 | async-start | bytes 3538944 | tf_op jit(solution)/shard_map/all_gather | solution.py:183
  355.1 204.2 %reduce-scatter.10.cloned.1.call-start = ((), (), s32[]{:S(2)}) async-start(), calls=%async_computation.11 | async-start | bytes 3538944 | tf_op jit(solution)/shard_map/reduce_scatter | solution.py:195
  442.6 6.8 copy-start.35
  452.9 136.3 %all-reduce.4.cloned.1.call-start = ((), (), s32[]{:S(2)}) async-start(), calls=%async_computation.15 | async-start | bytes 2359296
  458.4 163.8 %reduce-scatter.14.cloned.1.call-start = ((), (), s32[]{:S(2)}) async-start(), calls=%async_computation.13 | async-start | bytes 1769472 | tf_op jit(solution)/shard_map/reduce_scatter | solution.py:203
  460.9 98.4 %copy-start.19 = (bf16[197,2,128]{2,1,0:T(2,128)(2,1)S(1)}, bf16[197,2,128]{2,1,0:T(2,128)(2,1)}, u32[]{:S(2)}) copy-start(bf16[197,2,128]{2,1,0:T(2,128)(2,1)} %multiply_reduce_fusion.2) | copy-start | bytes 302596
  465.8 270.8 %reduce-scatter.12.cloned.1.call-start = ((), (), s32[]{:S(2)}) async-start(), calls=%async_computation.12 | async-start | bytes 5222400 | tf_op jit(solution)/shard_map/reduce_scatter | solution.py:228
  562.0 10.0 %copy-start.4 = (bf16[197,768]{0,1:T(8,128)(2,1)S(1)}, bf16[197,768]{0,1:T(8,128)(2,1)}, u32[]{:S(2)}) copy-start(bf16[197,768]{0,1:T(8,128)(2,1)} %copy-done.3) | copy-start | bytes 907780
  570.6 3.4 copy-start.8
  618.5 17.9 %collective-permute-start.12 = (bf16[2,48,3072]{2,1,0:T(8,128)(2,1)S(1)}, bf16[2,48,3072]{2,1,0:T(8,128)(2,1)S(1)}, u32[]{:S(2)}, u32[]{:S(2)}) collective-permute-start(bf16[2,48,3072]{2,1,0:T(8,128)(2,1)S(1)} %reshape.253), channel_id=1, source_target_pairs={{0,1},{1,0},{2,3},{3,2},{4,5},{5,4},{6,7},{7,6},{8,9},{9,8},{10,11... | collective-permute-start | bytes 1769480 | tf_op jit(solution)/shard_map/ppermute | solution.py:40
  622.2 44.3 %copy-start.22 = (bf16[2,192,768]{2,1,0:T(8,128)(2,1)S(1)}, bf16[2,192,768]{2,1,0:T(8,128)(2,1)}, u32[]{:S(2)}) copy-start(bf16[2,192,768]{2,1,0:T(8,128)(2,1)} %reduce-scatter.14.cloned.1.call-done) | copy-start | bytes 1769476
  622.2 44.3 %collective-permute-start.16 = (bf16[2,192,768]{2,1,0:T(8,128)(2,1)}, bf16[2,192,768]{2,1,0:T(8,128)(2,1)S(1)}, u32[]{:S(2)}, u32[]{:S(2)}) collective-permute-start(bf16[2,192,768]{2,1,0:T(8,128)(2,1)} %reduce-scatter.14.cloned.1.call-done), channel_id=1, source_target_pairs={{0,1},{1,0},{2,3},{3,2},{4,5},{5,4},{6,7},{7,6},{8,9},{9,8},{10,11... | collective-permute-start | bytes 1769480 | tf_op jit(solution)/shard_map/ppermute | solution.py:40
  636.6 66.8 %collective-permute-start.13 = (bf16[2,48,3072]{2,1,0:T(8,128)(2,1)S(1)}, bf16[2,48,3072]{2,1,0:T(8,128)(2,1)S(1)}, u32[]{:S(2)}, u32[]{:S(2)}) collective-permute-start(bf16[2,48,3072]{2,1,0:T(8,128)(2,1)S(1)} %add_convert_fusion.5), channel_id=1, source_target_pairs={{0,2},{1,3},{2,0},{3,1},{4,6},{5,7},{6,4},{7,5},{8,10},{9,11},{10,... | collective-permute-start | bytes 1769480 | tf_op jit(solution)/shard_map/ppermute | solution.py:40
  666.7 47.8 %collective-permute-start.17 = (bf16[2,192,768]{2,1,0:T(8,128)(2,1)S(1)}, bf16[2,192,768]{2,1,0:T(8,128)(2,1)S(1)}, u32[]{:S(2)}, u32[]{:S(2)}) collective-permute-start(bf16[2,192,768]{2,1,0:T(8,128)(2,1)S(1)} %add_convert_fusion.2), channel_id=1, source_target_pairs={{0,2},{1,3},{2,0},{3,1},{4,6},{5,7},{6,4},{7,5},{8,10},{9,11},{10,... | collective-permute-start | bytes 1769480 | tf_op jit(solution)/shard_map/ppermute | solution.py:40
  703.5 13.6 %collective-permute-start.14 = (bf16[2,48,3072]{2,1,0:T(8,128)(2,1)S(1)}, bf16[2,48,3072]{2,1,0:T(8,128)(2,1)S(1)}, u32[]{:S(2)}, u32[]{:S(2)}) collective-permute-start(bf16[2,48,3072]{2,1,0:T(8,128)(2,1)S(1)} %add_convert_fusion.4), channel_id=1, source_target_pairs={{0,4},{1,5},{2,6},{3,7},{4,0},{5,1},{6,2},{7,3},{8,12},{9,13},{10,... | collective-permute-start | bytes 1769480 | tf_op jit(solution)/shard_map/ppermute | solution.py:40
  709.8 6.5 collective-permute-start
  714.7 23.2 %collective-permute-start.18 = (bf16[2,192,768]{2,1,0:T(8,128)(2,1)S(1)}, bf16[2,192,768]{2,1,0:T(8,128)(2,1)S(1)}, u32[]{:S(2)}, u32[]{:S(2)}) collective-permute-start(bf16[2,192,768]{2,1,0:T(8,128)(2,1)S(1)} %add_convert_fusion.1), channel_id=1, source_target_pairs={{0,4},{1,5},{2,6},{3,7},{4,0},{5,1},{6,2},{7,3},{8,12},{9,13},{10,... | collective-permute-start | bytes 1769480 | tf_op jit(solution)/shard_map/ppermute | solution.py:40
  716.3 20.6 %collective-permute-start.1 = (f32[2,768]{1,0:T(2,128)S(1)}, f32[2,768]{1,0:T(2,128)S(1)}, u32[]{:S(2)}, u32[]{:S(2)}) collective-permute-start(f32[2,768]{1,0:T(2,128)S(1)} %fusion.64), channel_id=1, source_target_pairs={{0,32},{16,48},{32,0},{48,16},{64,96},{80,112},{96,64},{112,80},{1... | collective-permute-start | bytes 18440 | tf_op jit(solution)/shard_map/ppermute | solution.py:40
  717.3 29.2 %collective-permute-start.15 = (bf16[2,48,3072]{2,1,0:T(8,128)(2,1)S(1)}, bf16[2,48,3072]{2,1,0:T(8,128)(2,1)S(1)}, u32[]{:S(2)}, u32[]{:S(2)}) collective-permute-start(bf16[2,48,3072]{2,1,0:T(8,128)(2,1)S(1)} %add_convert_fusion.3), channel_id=1, source_target_pairs={{0,8},{1,9},{2,10},{3,11},{4,12},{5,13},{6,14},{7,15},{8,0},{9,1},... | collective-permute-start | bytes 1769480 | tf_op jit(solution)/shard_map/ppermute | solution.py:40
  736.6 7.4 collective-permute-start.8
  736.9 4.1 collective-permute-start.2
  738.0 18.0 %collective-permute-start.19 = (bf16[2,192,768]{2,1,0:T(8,128)(2,1)S(1)}, bf16[2,192,768]{2,1,0:T(8,128)(2,1)S(1)}, u32[]{:S(2)}, u32[]{:S(2)}) collective-permute-start(bf16[2,192,768]{2,1,0:T(8,128)(2,1)S(1)} %add_convert_fusion), channel_id=1, source_target_pairs={{0,8},{1,9},{2,10},{3,11},{4,12},{5,13},{6,14},{7,15},{8,0},{9,1},... | collective-permute-start | bytes 1769480 | tf_op jit(solution)/shard_map/ppermute | solution.py:40
  741.1 6.6 collective-permute-start.3
  745.1 26.7 %copy-start.2 = (f32[197,768]{1,0:T(8,128)S(1)}, f32[197,768]{1,0:T(8,128)}, u32[]{:S(2)}) copy-start(f32[197,768]{1,0:T(8,128)} %copy-done) | copy-start | bytes 1815556
  745.1 26.7 %copy-start.21 = (f32[197,768]{1,0:T(8,128)S(1)}, f32[197,768]{1,0:T(8,128)}, u32[]{:S(2)}) copy-start(f32[197,768]{1,0:T(8,128)} %get-tuple-element.86) | copy-start | bytes 1815556
  745.1 13.9 %collective-permute-start.9 = (bf16[48,3104]{1,0:T(8,128)(2,1)S(1)}, bf16[48,3104]{1,0:T(8,128)(2,1)S(1)}, u32[]{:S(2)}, u32[]{:S(2)}) collective-permute-start(bf16[48,3104]{1,0:T(8,128)(2,1)S(1)} %add_convert_fusion.8), channel_id=1, source_target_pairs={{0,2},{1,3},{2,0},{3,1},{4,6},{5,7},{6,4},{7,5},{8,10},{9,11},{10,... | collective-permute-start | bytes 893960 | tf_op jit(solution)/shard_map/ppermute | solution.py:40
  747.6 9.5 %collective-permute-start.4 = (f32[2,768]{1,0:T(2,128)S(1)}, f32[2,768]{1,0:T(2,128)S(1)}, u32[]{:S(2)}, u32[]{:S(2)}) collective-permute-start(f32[2,768]{1,0:T(2,128)S(1)} %add.128), channel_id=1, source_target_pairs={{0,1},{1,0},{2,3},{3,2},{4,5},{5,4},{6,7},{7,6},{8,9},{9,8},{10,11... | collective-permute-start | bytes 18440 | tf_op jit(solution)/shard_map/ppermute | solution.py:40
  757.2 4.6 collective-permute-start.5
  759.1 12.0 %collective-permute-start.10 = (bf16[48,3104]{1,0:T(8,128)(2,1)S(1)}, bf16[48,3104]{1,0:T(8,128)(2,1)S(1)}, u32[]{:S(2)}, u32[]{:S(2)}) collective-permute-start(bf16[48,3104]{1,0:T(8,128)(2,1)S(1)} %add_convert_fusion.7), channel_id=1, source_target_pairs={{0,4},{1,5},{2,6},{3,7},{4,0},{5,1},{6,2},{7,3},{8,12},{9,13},{10,... | collective-permute-start | bytes 893960 | tf_op jit(solution)/shard_map/ppermute | solution.py:40
  761.8 6.2 collective-permute-start.6
  768.1 5.1 collective-permute-start.7
  771.2 9.1 %collective-permute-start.11 = (bf16[48,3104]{1,0:T(8,128)(2,1)S(1)}, bf16[48,3104]{1,0:T(8,128)(2,1)S(1)}, u32[]{:S(2)}, u32[]{:S(2)}) collective-permute-start(bf16[48,3104]{1,0:T(8,128)(2,1)S(1)} %add_convert_fusion.6), channel_id=1, source_target_pairs={{0,8},{1,9},{2,10},{3,11},{4,12},{5,13},{6,14},{7,15},{8,0},{9,1},... | collective-permute-start | bytes 893960 | tf_op jit(solution)/shard_map/ppermute | solution.py:40
  (21 other events, 32.2 us)
Sparse Core Ops, SparseCore 0:
  11.2 94.2 all-gather.6
  107.9 10.3 all-gather.14
  121.5 92.4 all-gather.8
  215.7 10.4 all-gather.10
  233.8 109.4 reduce-scatter.7
  355.2 87.3 all-gather.12
  453.1 106.1 reduce-scatter.9
  562.5 26.7 all-reduce.3
  592.5 15.2 reduce-scatter.13
  612.2 124.3 reduce-scatter.11

commit v4 on v2

--- a/solution.py
+++ b/solution.py
@@ -158,34 +158,38 @@
         "rec,rd->ecd", dispatch, hidden2, preferred_element_type=jnp.float32
     ).astype(jnp.bfloat16)
     w_in_cols = lax.all_to_all(w_expert_in, "shard", 2, 1, tiled=True)
-    rows_all = lax.all_gather(expert_rows, "shard", axis=1, tiled=True)
+    grad = cotangent.astype(jnp.float32)
+    grad_eout = jnp.einsum("rec,rd->ecd", combine, grad, precision=high).astype(jnp.bfloat16)
+    gathered = lax.all_gather(
+        jnp.stack([expert_rows, grad_eout]), "shard", axis=2, tiled=True
+    )
+    rows_all, geout_all = gathered[0], gathered[1]
     pre = jnp.einsum("erd,edh->erh", rows_all, w_in_cols, preferred_element_type=jnp.float32)
     activated = jax.nn.gelu(pre, approximate=False).astype(jnp.bfloat16)
     out_part = jnp.einsum(
         "erh,ehd->erd", activated, w_expert_out, preferred_element_type=jnp.float32
     ).astype(jnp.bfloat16)
-    expert_out = lax.psum_scatter(out_part, "shard", scatter_dimension=1, tiled=True)
+    grad_act = jnp.einsum(
+        "erd,ehd->erh", geout_all, w_expert_out, preferred_element_type=jnp.float32
+    )
+    slope = (
+        0.5 * (1.0 + jax.scipy.special.erf(pre * 0.7071067811865476))
+        + pre * jnp.exp(-0.5 * pre * pre) * 0.3989422804014327
+    )
+    grad_pre = (grad_act * slope).astype(jnp.bfloat16)
+    rows_part = jnp.einsum(
+        "erh,edh->erd", grad_pre, w_in_cols, preferred_element_type=jnp.float32
+    ).astype(jnp.bfloat16)
+    scattered = lax.psum_scatter(
+        jnp.stack([out_part, rows_part]), "shard", scatter_dimension=2, tiled=True
+    )
+    expert_out, grad_rows = scattered[0], scattered[1]
     eout_float = expert_out.astype(jnp.float32)
     moe = jnp.einsum("rec,ecd->rd", combine, eout_float, precision=high)
     outputs = (attended + moe).astype(jnp.bfloat16)
-    grad = cotangent.astype(jnp.float32)
     matched = jnp.einsum("rd,ecd->rec", grad, eout_float, precision=high)
     grad_gate = jnp.sum(masks * matched[:, None, :, :], axis=(2, 3))
-    grad_eout = jnp.einsum("rec,rd->ecd", combine, grad, precision=high).astype(jnp.bfloat16)
     back_qkv, back_proj, back_router = (full_qkv, full_proj, full_router)
-    geout_all = lax.all_gather(grad_eout, "shard", axis=1, tiled=True)
-    grad_act = jnp.einsum(
-        "erd,ehd->erh", geout_all, w_expert_out, preferred_element_type=jnp.float32
-    )
-    slope = (
-        0.5 * (1.0 + jax.scipy.special.erf(pre * 0.7071067811865476))
-        + pre * jnp.exp(-0.5 * pre * pre) * 0.3989422804014327
-    )
-    grad_pre = (grad_act * slope).astype(jnp.bfloat16)
-    rows_part = jnp.einsum(
-        "erh,edh->erd", grad_pre, w_in_cols, preferred_element_type=jnp.float32
-    ).astype(jnp.bfloat16)
-    grad_rows = lax.psum_scatter(rows_part, "shard", scatter_dimension=1, tiled=True)
     gin_cols = jnp.einsum("erd,erh->edh", rows_all, grad_pre, preferred_element_type=jnp.float32)
     gin_local = lax.all_to_all(gin_cols.astype(jnp.bfloat16), "shard", 1, 2, tiled=True)
     gout_local = jnp.einsum(

time: 788 us -> 688 us (0.87)
  waiting for transfers between devices: 570 us -> 472 us
  matrix products: 59.2 us -> 49.7 us
    reduce_scatter x2 -> x1, waiting for transfers between devices: 229 us -> 172 us  [body(): lax.psum_scatter(jnp.stack([out_part, rows_part]), 'shard', scatter_dimen...]
    all_gather x2 -> x1, waiting for transfers between devices: 139 us -> 94.7 us  [body(): lax.all_gather(jnp.stack([expert_rows, grad_eout]), 'shard', axis=2, tile...]
    unnamed x96 -> x74, local copies, waits for them, and re-layouts: 23.1 us -> 16.6 us
  transfers between devices with their start and end apart: 27 -> 25, of which waited for: 20 -> 16; matrix products, arithmetic and copies ran while one was open for 6% -> 7% of each run, Pallas kernels for 0% -> 0%
where the time goes in v4:
time: 688 us; the launch traced here: 679 us
  waiting for transfers between devices  472 us (69%)
  matrix products  49.7 us (7%)
  other arithmetic  37.6 us (5%)
  blocking collectives  37.3 us (5%)
  local copies, waits for them, and re-layouts  35.7 us (5%)
  starting transfers between devices  31.1 us (5%)
  between operations  15 us (2%)
    reduce_scatter x1, waiting for transfers between devices, body(): lax.psum_scatter(jnp.stack([out_part, rows_part]), 'shard', scatter_dimen...  172 us
    ppermute x20, waiting for transfers between devices, butterfly_sum(): other = lax.ppermute(sent, axis, pairs)  108 us
    all_gather x1, waiting for transfers between devices, body(): lax.all_gather(jnp.stack([expert_rows, grad_eout]), 'shard', axis=2, tile...  94.7 us
    all_gather x1, waiting for transfers between devices, body(): lax.all_gather(jnp.concatenate([w_qkv, w_proj, w_router], axis=1), 'shard...  78.7 us
    all_to_all x1, blocking collectives, body(): w_in_cols = lax.all_to_all(w_expert_in, 'shard', 2, 1, tiled=True)  37.3 us
    ppermute x20, starting transfers between devices, butterfly_sum(): other = lax.ppermute(sent, axis, pairs)  26 us
    all_to_all x1, waiting for transfers between devices, body(): lax.all_to_all(gin_cols.astype(jnp.bfloat16), 'shard', 1, 2, tiled=True)  19.4 us
    unnamed x74, local copies, waits for them, and re-layouts  16.6 us
  transfers between devices with their start and end apart: 25, of which 16 were waited for; matrix products, arithmetic and copies ran while one was open for 7% of the time, Pallas kernels for 0%

profile of v4, /device:TPU:8, one launch (start us, length us, event | category | flops | bytes accessed | tf_op | source)
XLA Modules:
  0.0 678.7 jit_solution(1901787044144280053)
XLA Ops:
  8.1 1.7 pad_maximum_fusion.6
  17.6 78.7 %all-gather.3.cloned.1.call-done = bf16[768,3104]{1,0:T(8,128)(2,1)} async-done(((bf16[48,3104]{1,0:T(8,128)(2,1)}), bf16[768,3104]{1,0:T(8,128)(2,1)}) %all-gather.3.cloned.1.call-update) | async-done | bytes 4767760 | tf_op jit(solution)/shard_map/all_gather | solution.py:135
  96.3 3.1 convolution_convert_fusion.1
  101.5 1.8 multiply_reduce_fusion
  104.5 1.9 fusion.76
  109.5 2.4 multiply_reduce_fusion.2
  115.1 4.3 copy.162
  119.4 4.1 reshape.249
  123.5 37.3 %all_to_all.36 = bf16[16,2,9216]{2,1,0:T(2,128)(2,1)} all-to-all(bf16[16,2,9216]{2,1,0:T(2,128)(2,1)} %reshape.249), channel_id=1, replica_groups=mesh['shard'=16,'rep'=16] {'shard'}, dimensions={0} | all-to-all | bytes 1179648 | tf_op jit(solution)/shard_map/all_to_all | solution.py:160
  160.8 3.3 reshape.250
  164.1 4.7 copy.163
  168.8 94.7 %all-gather.5.cloned.1.call-done = bf16[2,2,2048,768]{3,2,1,0:T(8,128)(2,1)} async-done(((bf16[2,2,128,768]{3,2,1,0:T(8,128)(2,1)}), bf16[2,2,2048,768]{3,2,1,0:T(8,128)(2,1)}) %all-gather.5.cloned.1.call-update) | async-done | bytes 12582928 | tf_op jit(solution)/shard_map/all_gather | solution.py:163
  263.5 5.5 fusion.34
  269.1 4.6 fusion.12
  273.7 2.2 convert_bitcast_fusion
  275.9 7.2 %fusion.6 = bf16[2,2048,192]{1,2,0:T(8,128)(2,1)S(1)} fusion(f32[2,2048,192]{1,2,0:T(8,128)S(1)} %get-tuple-element.84, u8[2048,192]{0,1:T(8,128)(4,1)S(1)} %get-tuple-element.64, u8[2048,192]{0,1:T(8,128)(4,1)S(1)} %get-tuple-element.63), kind=kLoop, calls=%fused_computation.16 | loop fusion | flops 55050240 | bytes 5505024 | tf_op jit(solution)/shard_map/convert_element_type | solution.py:168
  283.1 1.9 convert_bitcast_fusion.1
  285.0 5.6 pad_maximum_fusion
  290.9 171.9 %reduce-scatter.3.cloned.1.call-done = bf16[2,2,128,768]{3,2,1,0:T(8,128)(2,1)} async-done(((bf16[2,2,2048,768]{3,2,1,0:T(8,128)(2,1)}), bf16[2,2,128,768]{3,2,1,0:T(8,128)(2,1)}) %reduce-scatter.3.cloned.1.call-update) | async-done | bytes 786448 | tf_op jit(solution)/shard_map/reduce_scatter | solution.py:183
  464.2 2.7 fusion.49
  469.4 1.7 multiply_reduce_fusion.3
  473.3 2.5 convolution_convert_fusion.7
  477.0 2.0 copy.171
  484.3 2.3 pad_maximum_fusion.1
  488.0 4.3 fusion.23
  493.4 4.4 fusion.24
  497.9 1.8 copy.178
  499.7 4.8 all-to-all-start.1
  505.9 1.6 collective-permute-start.17
  507.5 19.4 %all-to-all-done.1 = bf16[2,768,192]{2,0,1:T(2,128)(2,1)S(1)} async-done(((bf16[2,768,192]{2,0,1:T(2,128)(2,1)}), bf16[2,768,192]{2,0,1:T(2,128)(2,1)S(1)}, u32[]{:S(2)}, u32[]{:S(2)}) %all-to-all-start.1) | async-done | bytes 589856 | tf_op jit(solution)/shard_map/all_to_all | solution.py:194
  528.1 2.2 collective-permute-start.12
  530.3 46.7 %collective-permute-done.17 = bf16[2,192,768]{2,1,0:T(8,128)(2,1)S(1)} collective-permute-done((bf16[2,192,768]{2,1,0:T(8,128)(2,1)S(1)}, bf16[2,192,768]{2,1,0:T(8,128)(2,1)S(1)}, u32[]{:S(2)}, u32[]{:S(2)}) %collective-permute-start.17) | collective-permute-done | bytes 589856 | tf_op jit(solution)/shard_map/ppermute | solution.py:39
  577.1 1.6 collective-permute-start.18
  578.9 13.5 %collective-permute-done.18 = bf16[2,192,768]{2,1,0:T(8,128)(2,1)S(1)} collective-permute-done((bf16[2,192,768]{2,1,0:T(8,128)(2,1)S(1)}, bf16[2,192,768]{2,1,0:T(8,128)(2,1)S(1)}, u32[]{:S(2)}, u32[]{:S(2)}) %collective-permute-start.18) | collective-permute-done | bytes 589856 | tf_op jit(solution)/shard_map/ppermute | solution.py:39
  592.5 3.1 collective-permute-start.19
  595.7 3.5 fusion.46
  599.3 13.1 %collective-permute-done.13 = bf16[2,48,3072]{2,1,0:T(8,128)(2,1)S(1)} collective-permute-done((bf16[2,48,3072]{2,1,0:T(8,128)(2,1)S(1)}, bf16[2,48,3072]{2,1,0:T(8,128)(2,1)S(1)}, u32[]{:S(2)}, u32[]{:S(2)}) %collective-permute-start.13) | collective-permute-done | bytes 589856 | tf_op jit(solution)/shard_map/ppermute | solution.py:39
  613.3 4.3 collective-permute-start.1
  618.7 2.2 collective-permute-done.1
  621.7 6.3 collective-permute-done.14
  629.3 2.8 collective-permute-start.15
  632.1 2.2 collective-permute-start.3
  635.4 9.8 %collective-permute-done.15 = bf16[2,48,3072]{2,1,0:T(8,128)(2,1)S(1)} collective-permute-done((bf16[2,48,3072]{2,1,0:T(8,128)(2,1)S(1)}, bf16[2,48,3072]{2,1,0:T(8,128)(2,1)S(1)}, u32[]{:S(2)}, u32[]{:S(2)}) %collective-permute-start.15) | collective-permute-done | bytes 589856 | tf_op jit(solution)/shard_map/ppermute | solution.py:39
  646.5 4.0 collective-permute-done.4
  652.0 3.1 collective-permute-done.5
  656.6 3.4 collective-permute-done.6
  661.1 2.6 collective-permute-start.11
  665.9 3.6 collective-permute-done.11
  (195 shorter events, 51.2 us)
Async XLA Ops:
  7.2 261.9 %copy-start = (bf16[2,192,768]{2,1,0:T(8,128)(2,1)S(1)}, bf16[2,192,768]{2,1,0:T(8,128)(2,1)}, u32[]{:S(2)}) copy-start(bf16[2,192,768]{2,1,0:T(8,128)(2,1)} %param.18) | copy-start | bytes 1769476
  7.2 89.1 %all-gather.3.cloned.1.call-start = ((), (), s32[]{:S(2)}) async-start(), calls=%async_computation.4 | async-start | bytes 5222400 | tf_op jit(solution)/shard_map/all_gather | solution.py:135
  9.8 253.7 %all-gather.5.cloned.1.call-start = ((), (), s32[]{:S(2)}) async-start(), calls=%async_computation.5 | async-start | bytes 13369344 | tf_op jit(solution)/shard_map/all_gather | solution.py:163
  101.5 2.9 copy-start.9
  103.8 3.4 copy-start.32
  104.4 3.0 copy-start.13
  104.4 4.2 copy-start.31
  115.1 347.8 %reduce-scatter.3.cloned.1.call-start = ((), (), s32[]{:S(2)}) async-start(), calls=%async_computation.6 | async-start | bytes 13369344 | tf_op jit(solution)/shard_map/reduce_scatter | solution.py:183
  269.1 4.6 copy-start.15
  273.7 2.3 copy-start.24
  283.1 1.9 copy-start.7
  290.6 172.2 %copy-start.17 = (bf16[197,768]{1,0:T(8,128)(2,1)S(1)}, bf16[197,768]{1,0:T(8,128)(2,1)}, u32[]{:S(2)}) copy-start(bf16[197,768]{1,0:T(8,128)(2,1)} %param.21) | copy-start | bytes 907780
  290.6 173.6 %copy-start.22 = (f32[197,2,2]{2,1,0:T(2,128)S(1)}, f32[197,2,2]{2,1,0:T(2,128)}, u32[]{:S(2)}) copy-start(f32[197,2,2]{2,1,0:T(2,128)} %copy.157) | copy-start | bytes 9460
  290.7 331.1 %reduce-scatter.5.cloned.1.call-start = ((), (), s32[]{:S(2)}) async-start(), calls=%async_computation.7 | async-start | bytes 5222400 | tf_op jit(solution)/shard_map/reduce_scatter | solution.py:222
  475.8 4.7 copy-start.10
  480.6 1.7 copy-start.5
  481.4 1.6 copy-start.33
  481.9 2.4 copy-start.27
  482.3 2.0 copy-start.29
  488.0 5.4 copy-start.25
  492.3 13.4 %collective-permute-start.16 = (bf16[2,192,768]{2,1,0:T(8,128)(2,1)S(1)}, bf16[2,192,768]{2,1,0:T(8,128)(2,1)S(1)}, u32[]{:S(2)}, u32[]{:S(2)}) collective-permute-start(bf16[2,192,768]{2,1,0:T(8,128)(2,1)S(1)} %fusion.23), channel_id=1, source_target_pairs={{0,1},{1,0},{2,3},{3,2},{4,5},{5,4},{6,7},{7,6},{8,9},{9,8},{10,11... | collective-permute-start | bytes 1769480 | tf_op jit(solution)/shard_map/ppermute | solution.py:39
  499.7 27.2 %all-to-all-start.1 = ((bf16[2,768,192]{2,0,1:T(2,128)(2,1)}), bf16[2,768,192]{2,0,1:T(2,128)(2,1)S(1)}, u32[]{:S(2)}, u32[]{:S(2)}) async-start(bf16[2,768,192]{2,0,1:T(2,128)(2,1)} %copy.178), calls=%async_computation.3 | async-start | bytes 1572864 | tf_op jit(solution)/shard_map/all_to_all | solution.py:194
  505.9 71.0 %collective-permute-start.17 = (bf16[2,192,768]{2,1,0:T(8,128)(2,1)S(1)}, bf16[2,192,768]{2,1,0:T(8,128)(2,1)S(1)}, u32[]{:S(2)}, u32[]{:S(2)}) collective-permute-start(bf16[2,192,768]{2,1,0:T(8,128)(2,1)S(1)} %add_convert_fusion.2), channel_id=1, source_target_pairs={{0,2},{1,3},{2,0},{3,1},{4,6},{5,7},{6,4},{7,5},{8,10},{9,11},{10,... | collective-permute-start | bytes 1769480 | tf_op jit(solution)/shard_map/ppermute | solution.py:39
  528.1 67.6 %copy-start.28 = (bf16[12,64,197]{2,1,0:T(8,128)(2,1)S(1)}, bf16[12,64,197]{2,1,0:T(8,128)(2,1)}, u32[]{:S(2)}) copy-start(bf16[12,64,197]{2,1,0:T(8,128)(2,1)} %copy-done.27) | copy-start | bytes 907780
  528.1 67.6 %copy-start.30 = (bf16[12,64,197]{2,1,0:T(8,128)(2,1)S(1)}, bf16[12,64,197]{2,1,0:T(8,128)(2,1)}, u32[]{:S(2)}) copy-start(bf16[12,64,197]{2,1,0:T(8,128)(2,1)} %copy-done.29) | copy-start | bytes 907780
  528.1 50.5 %collective-permute-start.12 = (bf16[2,48,3072]{2,1,0:T(8,128)(2,1)S(1)}, bf16[2,48,3072]{2,1,0:T(8,128)(2,1)S(1)}, u32[]{:S(2)}, u32[]{:S(2)}) collective-permute-start(bf16[2,48,3072]{2,1,0:T(8,128)(2,1)S(1)} %all_to_all.33), channel_id=1, source_target_pairs={{0,1},{1,0},{2,3},{3,2},{4,5},{5,4},{6,7},{7,6},{8,9},{9,8},{10,11... | collective-permute-start | bytes 1769480 | tf_op jit(solution)/shard_map/ppermute | solution.py:39
  577.1 15.3 %collective-permute-start.18 = (bf16[2,192,768]{2,1,0:T(8,128)(2,1)S(1)}, bf16[2,192,768]{2,1,0:T(8,128)(2,1)S(1)}, u32[]{:S(2)}, u32[]{:S(2)}) collective-permute-start(bf16[2,192,768]{2,1,0:T(8,128)(2,1)S(1)} %add_convert_fusion.1), channel_id=1, source_target_pairs={{0,4},{1,5},{2,6},{3,7},{4,0},{5,1},{6,2},{7,3},{8,12},{9,13},{10,... | collective-permute-start | bytes 1769480 | tf_op jit(solution)/shard_map/ppermute | solution.py:39
  578.8 33.7 %collective-permute-start.13 = (bf16[2,48,3072]{2,1,0:T(8,128)(2,1)S(1)}, bf16[2,48,3072]{2,1,0:T(8,128)(2,1)S(1)}, u32[]{:S(2)}, u32[]{:S(2)}) collective-permute-start(bf16[2,48,3072]{2,1,0:T(8,128)(2,1)S(1)} %add_convert_fusion.5), channel_id=1, source_target_pairs={{0,2},{1,3},{2,0},{3,1},{4,6},{5,7},{6,4},{7,5},{8,10},{9,11},{10,... | collective-permute-start | bytes 1769480 | tf_op jit(solution)/shard_map/ppermute | solution.py:39
  592.5 25.1 %collective-permute-start.19 = (bf16[2,192,768]{2,1,0:T(8,128)(2,1)S(1)}, bf16[2,192,768]{2,1,0:T(8,128)(2,1)S(1)}, u32[]{:S(2)}, u32[]{:S(2)}) collective-permute-start(bf16[2,192,768]{2,1,0:T(8,128)(2,1)S(1)} %add_convert_fusion), channel_id=1, source_target_pairs={{0,8},{1,9},{2,10},{3,11},{4,12},{5,13},{6,14},{7,15},{8,0},{9,1},... | collective-permute-start | bytes 1769480 | tf_op jit(solution)/shard_map/ppermute | solution.py:39
  599.2 14.0 %collective-permute-start = (f32[2,768]{1,0:T(2,128)S(1)}, f32[2,768]{1,0:T(2,128)S(1)}, u32[]{:S(2)}, u32[]{:S(2)}) collective-permute-start(f32[2,768]{1,0:T(2,128)S(1)} %pad_maximum_fusion.7), channel_id=1, source_target_pairs={{0,16},{16,0},{32,48},{48,32},{64,80},{80,64},{96,112},{112,96},{1... | collective-permute-start | bytes 18440 | tf_op jit(solution)/shard_map/ppermute | solution.py:39
  612.6 15.4 %collective-permute-start.14 = (bf16[2,48,3072]{2,1,0:T(8,128)(2,1)S(1)}, bf16[2,48,3072]{2,1,0:T(8,128)(2,1)}, u32[]{:S(2)}, u32[]{:S(2)}) collective-permute-start(bf16[2,48,3072]{2,1,0:T(8,128)(2,1)S(1)} %add_convert_fusion.4), channel_id=1, source_target_pairs={{0,4},{1,5},{2,6},{3,7},{4,0},{5,1},{6,2},{7,3},{8,12},{9,13},{10,... | collective-permute-start | bytes 1769480 | tf_op jit(solution)/shard_map/ppermute | solution.py:39
  613.3 7.6 %collective-permute-start.1 = (f32[2,768]{1,0:T(2,128)S(1)}, f32[2,768]{1,0:T(2,128)S(1)}, u32[]{:S(2)}, u32[]{:S(2)}) collective-permute-start(f32[2,768]{1,0:T(2,128)S(1)} %fusion.72), channel_id=1, source_target_pairs={{0,32},{16,48},{32,0},{48,16},{64,96},{80,112},{96,64},{112,80},{1... | collective-permute-start | bytes 18440 | tf_op jit(solution)/shard_map/ppermute | solution.py:39
  618.7 36.8 %copy-start.6 = (f32[197,768]{1,0:T(8,128)S(1)}, f32[197,768]{1,0:T(8,128)}, u32[]{:S(2)}) copy-start(f32[197,768]{1,0:T(8,128)} %copy-done.4) | copy-start | bytes 1815556
  620.9 11.1 %collective-permute-start.2 = (f32[2,768]{1,0:T(2,128)S(1)}, f32[2,768]{1,0:T(2,128)S(1)}, u32[]{:S(2)}, u32[]{:S(2)}) collective-permute-start(f32[2,768]{1,0:T(2,128)S(1)} %fusion.102), channel_id=1, source_target_pairs={{0,64},{16,80},{32,96},{48,112},{64,0},{80,16},{96,32},{112,48},{1... | collective-permute-start | bytes 18440 | tf_op jit(solution)/shard_map/ppermute | solution.py:39
  621.7 12.5 %collective-permute-start.8 = (bf16[48,3104]{1,0:T(8,128)(2,1)}, bf16[48,3104]{1,0:T(8,128)(2,1)S(1)}, u32[]{:S(2)}, u32[]{:S(2)}) collective-permute-start(bf16[48,3104]{1,0:T(8,128)(2,1)} %reduce-scatter.5.cloned.1.call-done), channel_id=1, source_target_pairs={{0,1},{1,0},{2,3},{3,2},{4,5},{5,4},{6,7},{7,6},{8,9},{9,8},{10,11... | collective-permute-start | bytes 893960 | tf_op jit(solution)/shard_map/ppermute | solution.py:39
  629.3 16.0 %collective-permute-start.15 = (bf16[2,48,3072]{2,1,0:T(8,128)(2,1)S(1)}, bf16[2,48,3072]{2,1,0:T(8,128)(2,1)S(1)}, u32[]{:S(2)}, u32[]{:S(2)}) collective-permute-start(bf16[2,48,3072]{2,1,0:T(8,128)(2,1)S(1)} %add_convert_fusion.3), channel_id=1, source_target_pairs={{0,8},{1,9},{2,10},{3,11},{4,12},{5,13},{6,14},{7,15},{8,0},{9,1},... | collective-permute-start | bytes 1769480 | tf_op jit(solution)/shard_map/ppermute | solution.py:39
  632.1 14.4 %collective-permute-start.3 = (f32[2,768]{1,0:T(2,128)S(1)}, f32[2,768]{1,0:T(2,128)S(1)}, u32[]{:S(2)}, u32[]{:S(2)}) collective-permute-start(f32[2,768]{1,0:T(2,128)S(1)} %add.121), channel_id=1, source_target_pairs={{0,128},{16,144},{32,160},{48,176},{64,192},{80,208},{96,224},{112... | collective-permute-start | bytes 18440 | tf_op jit(solution)/shard_map/ppermute | solution.py:39
  635.3 28.4 %copy-start.3 = (f32[197,768]{1,0:T(8,128)S(1)}, f32[197,768]{1,0:T(8,128)}, u32[]{:S(2)}) copy-start(f32[197,768]{1,0:T(8,128)} %copy-done.2) | copy-start | bytes 1815556
  635.3 28.4 %copy-start.21 = (f32[197,2,128]{2,1,0:T(2,128)S(1)}, f32[197,2,128]{2,1,0:T(2,128)}, u32[]{:S(2)}) copy-start(f32[197,2,128]{2,1,0:T(2,128)} %copy-done.20) | copy-start | bytes 605188
  635.3 28.4 %copy-start.23 = (bf16[2,2,128,768]{3,2,1,0:T(8,128)(2,1)S(1)}, bf16[2,2,128,768]{3,2,1,0:T(8,128)(2,1)}, u32[]{:S(2)}) copy-start(bf16[2,2,128,768]{3,2,1,0:T(8,128)(2,1)} %reduce-scatter.3.cloned.1.call-done) | copy-start | bytes 2359300
  635.3 15.9 %collective-permute-start.9 = (bf16[48,3104]{1,0:T(8,128)(2,1)S(1)}, bf16[48,3104]{1,0:T(8,128)(2,1)S(1)}, u32[]{:S(2)}, u32[]{:S(2)}) collective-permute-start(bf16[48,3104]{1,0:T(8,128)(2,1)S(1)} %add_convert_fusion.8), channel_id=1, source_target_pairs={{0,2},{1,3},{2,0},{3,1},{4,6},{5,7},{6,4},{7,5},{8,10},{9,11},{10,... | collective-permute-start | bytes 893960 | tf_op jit(solution)/shard_map/ppermute | solution.py:39
  646.4 4.2 collective-permute-start.4
  650.6 4.5 collective-permute-start.5
  651.4 9.7 %collective-permute-start.10 = (bf16[48,3104]{1,0:T(8,128)(2,1)S(1)}, bf16[48,3104]{1,0:T(8,128)(2,1)S(1)}, u32[]{:S(2)}, u32[]{:S(2)}) collective-permute-start(bf16[48,3104]{1,0:T(8,128)(2,1)S(1)} %add_convert_fusion.7), channel_id=1, source_target_pairs={{0,4},{1,5},{2,6},{3,7},{4,0},{5,1},{6,2},{7,3},{8,12},{9,13},{10,... | collective-permute-start | bytes 893960 | tf_op jit(solution)/shard_map/ppermute | solution.py:39
  655.1 4.9 collective-permute-start.6
  655.6 16.2 %copy-start.1 = (bf16[2,192,768]{2,1,0:T(8,128)(2,1)S(1)}, bf16[2,192,768]{2,1,0:T(8,128)(2,1)}, u32[]{:S(2)}) copy-start(bf16[2,192,768]{2,1,0:T(8,128)(2,1)} %param.18) | copy-start | bytes 1769476
  660.0 5.3 collective-permute-start.7
  661.1 8.4 %collective-permute-start.11 = (bf16[48,3104]{1,0:T(8,128)(2,1)S(1)}, bf16[48,3104]{1,0:T(8,128)(2,1)S(1)}, u32[]{:S(2)}, u32[]{:S(2)}) collective-permute-start(bf16[48,3104]{1,0:T(8,128)(2,1)S(1)} %add_convert_fusion.6), channel_id=1, source_target_pairs={{0,8},{1,9},{2,10},{3,11},{4,12},{5,13},{6,14},{7,15},{8,0},{9,1},... | collective-permute-start | bytes 893960 | tf_op jit(solution)/shard_map/ppermute | solution.py:39
  (11 other events, 13.0 us)
Sparse Core Ops, SparseCore 0:
  11.2 85.0 all-gather.2
  115.2 148.2 all-gather.4
  290.8 171.9 reduce-scatter.2
  486.8 124.3 reduce-scatter.4

commit v5 on v4

--- a/solution.py
+++ b/solution.py
@@ -1,6 +1,7 @@
 import jax
 import jax.numpy as jnp
 from jax import lax
+from jax.experimental import pallas as pl
 from jax.sharding import PartitionSpec as P
 
 HEADS = 12
@@ -12,6 +13,51 @@
 
 
 EPS = 1e-06
+ROW_TILE = 256
+
+def expert_kernel(rows_ref, geout_ref, w_in_ref, w_out_ref, parts_ref, act_ref, gpre_ref):
+    rows = rows_ref[...]
+    w_in = w_in_ref[...]
+    w_out = w_out_ref[...]
+    pre = jnp.dot(rows, w_in, preferred_element_type=jnp.float32)
+    erf_term = lax.erf(pre * 0.7071067811865476)
+    activated = (0.5 * pre * (1.0 + erf_term)).astype(jnp.bfloat16)
+    act_ref[...] = activated
+    parts_ref[0] = jnp.dot(activated, w_out, preferred_element_type=jnp.float32).astype(jnp.bfloat16)
+    grad_act = lax.dot_general(
+        geout_ref[...], w_out, (((1,), (1,)), ((), ())), preferred_element_type=jnp.float32
+    )
+    slope = 0.5 * (1.0 + erf_term) + pre * jnp.exp(-0.5 * pre * pre) * 0.3989422804014327
+    grad_pre = (grad_act * slope).astype(jnp.bfloat16)
+    gpre_ref[...] = grad_pre
+    parts_ref[1] = lax.dot_general(
+        grad_pre, w_in, (((1,), (1,)), ((), ())), preferred_element_type=jnp.float32
+    ).astype(jnp.bfloat16)
+
+def expert_block(gathered, w_in_cols, w_out):
+    _, experts, rows, width = gathered.shape
+    hidden = w_in_cols.shape[2]
+    grid = (experts, rows // ROW_TILE)
+    return pl.pallas_call(
+        expert_kernel,
+        grid=grid,
+        in_specs=[
+            pl.BlockSpec((None, None, ROW_TILE, width), lambda e, i: (0, e, i, 0)),
+            pl.BlockSpec((None, None, ROW_TILE, width), lambda e, i: (1, e, i, 0)),
+            pl.BlockSpec((None, width, hidden), lambda e, i: (e, 0, 0)),
+            pl.BlockSpec((None, hidden, width), lambda e, i: (e, 0, 0)),
+        ],
+        out_specs=[
+            pl.BlockSpec((2, None, ROW_TILE, width), lambda e, i: (0, e, i, 0)),
+            pl.BlockSpec((None, ROW_TILE, hidden), lambda e, i: (e, i, 0)),
+            pl.BlockSpec((None, ROW_TILE, hidden), lambda e, i: (e, i, 0)),
+        ],
+        out_shape=[
+            jax.ShapeDtypeStruct((2, experts, rows, width), jnp.bfloat16),
+            jax.ShapeDtypeStruct((experts, rows, hidden), jnp.bfloat16),
+            jax.ShapeDtypeStruct((experts, rows, hidden), jnp.bfloat16),
+        ],
+    )(gathered, gathered, w_in_cols, w_out)
 
 
 def layer_norm(values, gain):
@@ -164,25 +210,8 @@
         jnp.stack([expert_rows, grad_eout]), "shard", axis=2, tiled=True
     )
     rows_all, geout_all = gathered[0], gathered[1]
-    pre = jnp.einsum("erd,edh->erh", rows_all, w_in_cols, preferred_element_type=jnp.float32)
-    activated = jax.nn.gelu(pre, approximate=False).astype(jnp.bfloat16)
-    out_part = jnp.einsum(
-        "erh,ehd->erd", activated, w_expert_out, preferred_element_type=jnp.float32
-    ).astype(jnp.bfloat16)
-    grad_act = jnp.einsum(
-        "erd,ehd->erh", geout_all, w_expert_out, preferred_element_type=jnp.float32
-    )
-    slope = (
-        0.5 * (1.0 + jax.scipy.special.erf(pre * 0.7071067811865476))
-        + pre * jnp.exp(-0.5 * pre * pre) * 0.3989422804014327
-    )
-    grad_pre = (grad_act * slope).astype(jnp.bfloat16)
-    rows_part = jnp.einsum(
-        "erh,edh->erd", grad_pre, w_in_cols, preferred_element_type=jnp.float32
-    ).astype(jnp.bfloat16)
-    scattered = lax.psum_scatter(
-        jnp.stack([out_part, rows_part]), "shard", scatter_dimension=2, tiled=True
-    )
+    parts, activated, grad_pre = expert_block(gathered, w_in_cols, w_expert_out)
+    scattered = lax.psum_scatter(parts, "shard", scatter_dimension=2, tiled=True)
     expert_out, grad_rows = scattered[0], scattered[1]
     eout_float = expert_out.astype(jnp.float32)
     moe = jnp.einsum("rec,ecd->rd", combine, eout_float, precision=high)

time: 688 us -> 680 us (0.988); the launches traced: 679 us -> 678 us
  Pallas kernels: 0 us -> 23.1 us
  matrix products: 49.7 us -> 38.7 us
  waiting for transfers between devices: 472 us -> 462 us
  other arithmetic: 37.6 us -> 27.7 us
  starting transfers between devices: 31.1 us -> 39.3 us
    pallas_call x0 -> x1, Pallas kernels: none -> 23.1 us  [expert_block(): pl.pallas_call(expert_kernel, grid=grid, in_specs=[pl.BlockSpec((None, No...]
    dot_general x4 -> x0, matrix products: 14.3 us -> none  [the longest x1 5.54 us: body(): jnp.einsum('erd,edh->erh', rows_all, w_in_cols, preferred_element_type=jn...]
    ppermute x20, waiting for transfers between devices: 108 us -> 98.2 us  [butterfly_sum(): other = lax.ppermute(sent, axis, pairs)]
    ppermute x20, starting transfers between devices: 26 us -> 34.2 us  [butterfly_sum(): other = lax.ppermute(sent, axis, pairs)]
    convert_element_type x1 -> x0, other arithmetic: 7.18 us -> none  [body(): activated = jax.nn.gelu(pre, approximate=False).astype(jnp.bfloat16)]
    unnamed x74 -> x70, local copies, waits for them, and re-layouts: 16.6 us -> 15.4 us
  transfers between devices with their start and end apart: 25 -> 25, of which waited for: 16 -> 17; matrix products, arithmetic and copies ran while one was open for 7% -> 7% of each run, Pallas kernels for 0% -> 0%
where the time goes in v5:
time: 680 us; the launch traced here: 678 us
  waiting for transfers between devices  462 us (68%)
  starting transfers between devices  39.3 us (6%)
  matrix products  38.7 us (6%)
  blocking collectives  37.3 us (5%)
  local copies, waits for them, and re-layouts  35.4 us (5%)
  other arithmetic  27.7 us (4%)
  Pallas kernels  23.1 us (3%)
  between operations  14.4 us (2%)
    reduce_scatter x1, waiting for transfers between devices, body(): lax.psum_scatter(parts, 'shard', scatter_dimension=2, tiled=True)  172 us
    ppermute x20, waiting for transfers between devices, butterfly_sum(): other = lax.ppermute(sent, axis, pairs)  98.2 us
    all_gather x1, waiting for transfers between devices, body(): lax.all_gather(jnp.stack([expert_rows, grad_eout]), 'shard', axis=2, tile...  94.7 us
    all_gather x1, waiting for transfers between devices, body(): lax.all_gather(jnp.concatenate([w_qkv, w_proj, w_router], axis=1), 'shard...  78.7 us
    all_to_all x1, blocking collectives, body(): w_in_cols = lax.all_to_all(w_expert_in, 'shard', 2, 1, tiled=True)  37.3 us
    ppermute x20, starting transfers between devices, butterfly_sum(): other = lax.ppermute(sent, axis, pairs)  34.2 us
    pallas_call x1, Pallas kernels, expert_block(): pl.pallas_call(expert_kernel, grid=grid, in_specs=[pl.BlockSpec((None, No...  23.1 us
    all_to_all x1, waiting for transfers between devices, body(): lax.all_to_all(gin_cols.astype(jnp.bfloat16), 'shard', 1, 2, tiled=True)  18.2 us
  transfers between devices with their start and end apart: 25, of which 17 were waited for; matrix products, arithmetic and copies ran while one was open for 7% of the time, Pallas kernels for 0%

profile of v5, /device:TPU:8, one launch (start us, length us, event | category | flops | bytes accessed | tf_op | source)
XLA Modules:
  0.0 677.7 jit_solution(13078768421761689419)
XLA Ops:
  8.0 1.7 pad_maximum_fusion.5
  17.5 78.7 %all-gather.3.cloned.1.call-done = bf16[768,3104]{1,0:T(8,128)(2,1)} async-done(((bf16[48,3104]{1,0:T(8,128)(2,1)}), bf16[768,3104]{1,0:T(8,128)(2,1)}) %all-gather.3.cloned.1.call-update) | async-done | bytes 4767760 | tf_op jit(solution)/shard_map/all_gather | solution.py:181
  96.3 3.1 convolution_convert_fusion.1
  103.6 2.0 fusion.57
  108.6 2.4 multiply_reduce_fusion.2
  111.7 1.5 fusion.13
  114.2 4.3 copy.164
  118.5 4.1 reshape.249
  122.7 37.3 %all_to_all.36 = bf16[16,2,9216]{2,1,0:T(2,128)(2,1)} all-to-all(bf16[16,2,9216]{2,1,0:T(2,128)(2,1)} %reshape.249), channel_id=1, replica_groups=mesh['shard'=16,'rep'=16] {'shard'}, dimensions={0} | all-to-all | bytes 1179648 | tf_op jit(solution)/shard_map/all_to_all | solution.py:206
  159.9 3.3 reshape.250
  163.2 4.7 copy.165
  168.0 94.7 %all-gather.5.cloned.1.call-done.rows_ref.geout_ref = bf16[2,2,2048,768]{3,2,1,0:T(8,128)(2,1)} async-done(((bf16[2,2,128,768]{3,2,1,0:T(8,128)(2,1)}), bf16[2,2,2048,768]{3,2,1,0:T(8,128)(2,1)}) %all-gather.5.cloned.1.call-update) | async-done | bytes 12582928 | tf_op jit(solution)/shard_map/all_gather | solution.py:209
  262.6 23.1 %shard_map.178 = (bf16[2,2,2048,768]{3,2,1,0:T(8,128)(2,1)}, bf16[2,2048,192]{2,1,0:T(8,128)(2,1)}, bf16[2,2048,192]{2,1,0:T(8,128)(2,1)}) custom-call(bf16[2,2,2048,768]{3,2,1,0:T(8,128)(2,1)} %all-gather.5.cloned.1.call-done.rows_ref.geout_ref, bf16[2,2,2048,768]{3,2,1,0:T(8,128)(2,1)} %all-gather.5.cloned.1.call-done.rows_ref.geout_ref, ...), custom_call_target="tpu_custom_call" | custom-call | tf_op jit(solution)/shard_map/pallas_call | solution.py:41
  286.0 171.9 %reduce-scatter.3.cloned.1.call-done = bf16[2,2,128,768]{3,2,1,0:T(8,128)(2,1)} async-done(((bf16[2,2,2048,768]{3,2,1,0:T(8,128)(2,1)}), bf16[2,2,128,768]{3,2,1,0:T(8,128)(2,1)}) %reduce-scatter.3.cloned.1.call-update) | async-done | bytes 786448 | tf_op jit(solution)/shard_map/reduce_scatter | solution.py:214
  459.4 2.8 fusion.30
  465.2 1.4 multiply_reduce_fusion.3
  468.5 2.5 convolution_convert_fusion.7
  471.0 2.0 copy.171
  473.1 1.9 copy.170
  476.3 1.9 multiply_convert_fusion
  483.1 2.4 convolution_convert_fusion
  485.5 2.3 pad_maximum_fusion
  487.8 5.0 fusion.7
  494.0 4.5 fusion.6
  498.5 1.8 copy.179
  500.3 4.8 all-to-all-start.1
  507.6 1.8 collective-permute-start.17
  509.4 18.2 %all-to-all-done.1 = bf16[2,768,192]{2,0,1:T(2,128)(2,1)S(1)} async-done(((bf16[2,768,192]{2,0,1:T(2,128)(2,1)}), bf16[2,768,192]{2,0,1:T(2,128)(2,1)S(1)}, u32[]{:S(2)}, u32[]{:S(2)}) %all-to-all-start.1) | async-done | bytes 589856 | tf_op jit(solution)/shard_map/all_to_all | solution.py:223
  528.9 1.6 collective-permute-start.12
  530.5 47.1 %collective-permute-done.17 = bf16[2,192,768]{2,1,0:T(8,128)(2,1)} collective-permute-done((bf16[2,192,768]{2,1,0:T(8,128)(2,1)S(1)}, bf16[2,192,768]{2,1,0:T(8,128)(2,1)}, u32[]{:S(2)}, u32[]{:S(2)}) %collective-permute-start.17) | collective-permute-done | bytes 589856 | tf_op jit(solution)/shard_map/ppermute | solution.py:85
  578.9 1.6 collective-permute-start.18
  580.7 13.5 %collective-permute-done.18 = bf16[2,192,768]{2,1,0:T(8,128)(2,1)S(1)} collective-permute-done((bf16[2,192,768]{2,1,0:T(8,128)(2,1)S(1)}, bf16[2,192,768]{2,1,0:T(8,128)(2,1)S(1)}, u32[]{:S(2)}, u32[]{:S(2)}) %collective-permute-start.18) | collective-permute-done | bytes 589856 | tf_op jit(solution)/shard_map/ppermute | solution.py:85
  594.4 3.1 collective-permute-start.19
  597.5 3.5 fusion.27
  601.2 10.0 %collective-permute-done.13 = bf16[2,48,3072]{2,1,0:T(8,128)(2,1)S(1)} collective-permute-done((bf16[2,48,3072]{2,1,0:T(8,128)(2,1)S(1)}, bf16[2,48,3072]{2,1,0:T(8,128)(2,1)S(1)}, u32[]{:S(2)}, u32[]{:S(2)}) %collective-permute-start.13) | collective-permute-done | bytes 589856 | tf_op jit(solution)/shard_map/ppermute | solution.py:85
  612.0 4.3 collective-permute-start.1
  617.5 2.2 collective-permute-done.1
  619.6 1.5 collective-permute-start.2
  621.1 6.2 collective-permute-start.8
  627.5 2.7 collective-permute-start.15
  630.2 2.2 collective-permute-start.3
  634.5 2.2 collective-permute-start.9
  636.7 6.1 collective-permute-done.15
  644.1 5.1 collective-permute-done.4
  650.0 3.8 collective-permute-done.5
  655.4 2.2 collective-permute-done.6
  657.6 2.7 collective-permute-start.7
  663.4 5.5 collective-permute-done.11
  (186 shorter events, 49.8 us)
Async XLA Ops:
  7.2 89.1 %all-gather.3.cloned.1.call-start = ((), (), s32[]{:S(2)}) async-start(), calls=%async_computation.4 | async-start | bytes 5222400 | tf_op jit(solution)/shard_map/all_gather | solution.py:181
  9.7 252.9 %all-gather.5.cloned.1.call-start = ((), (), s32[]{:S(2)}) async-start(), calls=%async_computation.5 | async-start | bytes 13369344 | tf_op jit(solution)/shard_map/all_gather | solution.py:209
  15.4 84.0 %copy-start.26 = (f32[197]{0:T(256)}, f32[197]{0:T(256)S(1)}, u32[]{:S(2)}) copy-start(f32[197]{0:T(256)S(1)} %broadcast_multiply_fusion.5) | copy-start | bytes 2368
  16.6 82.8 %copy-start.29 = (f32[197]{0:T(256)}, f32[197]{0:T(256)S(1)}, u32[]{:S(2)}) copy-start(f32[197]{0:T(256)S(1)} %add_rsqrt_fusion.1) | copy-start | bytes 2368
  103.6 4.1 copy-start.9
  103.6 2.8 copy-start.22
  103.6 4.2 copy-start.21
  107.7 355.5 %copy-start.23 = (f32[197]{0:T(256)}, f32[197]{0:T(256)S(1)}, u32[]{:S(2)}) copy-start(f32[197]{0:T(256)S(1)} %get-tuple-element.86) | copy-start | bytes 2368
  107.8 355.4 %copy-start.24 = (f32[197]{0:T(256)}, f32[197]{0:T(256)S(1)}, u32[]{:S(2)}) copy-start(f32[197]{0:T(256)S(1)} %fusion.46) | copy-start | bytes 2368
  114.2 343.7 %reduce-scatter.3.cloned.1.call-start = ((), (), s32[]{:S(2)}) async-start(), calls=%async_computation.6 | async-start | bytes 13369344 | tf_op jit(solution)/shard_map/reduce_scatter | solution.py:214
  285.8 335.4 %reduce-scatter.5.cloned.1.call-start = ((), (), s32[]{:S(2)}) async-start(), calls=%async_computation.7 | async-start | bytes 5222400 | tf_op jit(solution)/shard_map/reduce_scatter | solution.py:251
  463.2 3.5 copy-start.11
  476.3 2.0 copy-start.8
  476.3 3.1 copy-start.6
  478.3 2.4 copy-start.4
  479.4 2.6 copy-start.1
  479.4 2.6 copy-start.10
  480.6 2.2 copy-start.27
  480.6 2.2 copy-start.28
  480.6 2.2 copy-start.30
  487.8 6.2 copy-start.31
  492.8 13.5 %collective-permute-start.16 = (bf16[2,192,768]{2,1,0:T(8,128)(2,1)S(1)}, bf16[2,192,768]{2,1,0:T(8,128)(2,1)}, u32[]{:S(2)}, u32[]{:S(2)}) collective-permute-start(bf16[2,192,768]{2,1,0:T(8,128)(2,1)S(1)} %fusion.7), channel_id=1, source_target_pairs={{0,1},{1,0},{2,3},{3,2},{4,5},{5,4},{6,7},{7,6},{8,9},{9,8},{10,11... | collective-permute-start | bytes 1769480 | tf_op jit(solution)/shard_map/ppermute | solution.py:85
  500.3 27.3 %all-to-all-start.1 = ((bf16[2,768,192]{2,0,1:T(2,128)(2,1)}), bf16[2,768,192]{2,0,1:T(2,128)(2,1)S(1)}, u32[]{:S(2)}, u32[]{:S(2)}) async-start(bf16[2,768,192]{2,0,1:T(2,128)(2,1)} %copy.179), calls=%async_computation.3 | async-start | bytes 1572864 | tf_op jit(solution)/shard_map/all_to_all | solution.py:223
  507.6 70.0 %collective-permute-start.17 = (bf16[2,192,768]{2,1,0:T(8,128)(2,1)S(1)}, bf16[2,192,768]{2,1,0:T(8,128)(2,1)}, u32[]{:S(2)}, u32[]{:S(2)}) collective-permute-start(bf16[2,192,768]{2,1,0:T(8,128)(2,1)S(1)} %add_convert_fusion.2), channel_id=1, source_target_pairs={{0,2},{1,3},{2,0},{3,1},{4,6},{5,7},{6,4},{7,5},{8,10},{9,11},{10,... | collective-permute-start | bytes 1769480 | tf_op jit(solution)/shard_map/ppermute | solution.py:85
  528.8 68.6 %copy-start.18 = (bf16[12,64,197]{2,1,0:T(8,128)(2,1)S(1)}, bf16[12,64,197]{2,1,0:T(8,128)(2,1)}, u32[]{:S(2)}) copy-start(bf16[12,64,197]{2,1,0:T(8,128)(2,1)} %convolution_convert_fusion.3) | copy-start | bytes 907780
  528.9 68.6 %copy-start.19 = (bf16[12,64,197]{2,1,0:T(8,128)(2,1)S(1)}, bf16[12,64,197]{2,1,0:T(8,128)(2,1)}, u32[]{:S(2)}) copy-start(bf16[12,64,197]{2,1,0:T(8,128)(2,1)} %fusion.8) | copy-start | bytes 907780
  528.9 68.6 %copy-start.20 = (bf16[12,64,197]{2,1,0:T(8,128)(2,1)S(1)}, bf16[12,64,197]{2,1,0:T(8,128)(2,1)}, u32[]{:S(2)}) copy-start(bf16[12,64,197]{2,1,0:T(8,128)(2,1)} %fusion.9) | copy-start | bytes 907780
  528.9 51.6 %collective-permute-start.12 = (bf16[2,48,3072]{2,1,0:T(8,128)(2,1)S(1)}, bf16[2,48,3072]{2,1,0:T(8,128)(2,1)S(1)}, u32[]{:S(2)}, u32[]{:S(2)}) collective-permute-start(bf16[2,48,3072]{2,1,0:T(8,128)(2,1)S(1)} %all_to_all.33), channel_id=1, source_target_pairs={{0,1},{1,0},{2,3},{3,2},{4,5},{5,4},{6,7},{7,6},{8,9},{9,8},{10,11... | collective-permute-start | bytes 1769480 | tf_op jit(solution)/shard_map/ppermute | solution.py:85
  578.9 15.3 %collective-permute-start.18 = (bf16[2,192,768]{2,1,0:T(8,128)(2,1)S(1)}, bf16[2,192,768]{2,1,0:T(8,128)(2,1)S(1)}, u32[]{:S(2)}, u32[]{:S(2)}) collective-permute-start(bf16[2,192,768]{2,1,0:T(8,128)(2,1)S(1)} %add_convert_fusion.1), channel_id=1, source_target_pairs={{0,4},{1,5},{2,6},{3,7},{4,0},{5,1},{6,2},{7,3},{8,12},{9,13},{10,... | collective-permute-start | bytes 1769480 | tf_op jit(solution)/shard_map/ppermute | solution.py:85
  580.6 30.5 %collective-permute-start.13 = (bf16[2,48,3072]{2,1,0:T(8,128)(2,1)S(1)}, bf16[2,48,3072]{2,1,0:T(8,128)(2,1)S(1)}, u32[]{:S(2)}, u32[]{:S(2)}) collective-permute-start(bf16[2,48,3072]{2,1,0:T(8,128)(2,1)S(1)} %add_convert_fusion.5), channel_id=1, source_target_pairs={{0,2},{1,3},{2,0},{3,1},{4,6},{5,7},{6,4},{7,5},{8,10},{9,11},{10,... | collective-permute-start | bytes 1769480 | tf_op jit(solution)/shard_map/ppermute | solution.py:85
  594.4 21.9 %collective-permute-start.19 = (bf16[2,192,768]{2,1,0:T(8,128)(2,1)S(1)}, bf16[2,192,768]{2,1,0:T(8,128)(2,1)S(1)}, u32[]{:S(2)}, u32[]{:S(2)}) collective-permute-start(bf16[2,192,768]{2,1,0:T(8,128)(2,1)S(1)} %add_convert_fusion), channel_id=1, source_target_pairs={{0,8},{1,9},{2,10},{3,11},{4,12},{5,13},{6,14},{7,15},{8,0},{9,1},... | collective-permute-start | bytes 1769480 | tf_op jit(solution)/shard_map/ppermute | solution.py:85
  601.1 10.9 %collective-permute-start = (f32[2,768]{1,0:T(2,128)S(1)}, f32[2,768]{1,0:T(2,128)S(1)}, u32[]{:S(2)}, u32[]{:S(2)}) collective-permute-start(f32[2,768]{1,0:T(2,128)S(1)} %pad_maximum_fusion.6), channel_id=1, source_target_pairs={{0,16},{16,0},{32,48},{48,32},{64,80},{80,64},{96,112},{112,96},{1... | collective-permute-start | bytes 18440 | tf_op jit(solution)/shard_map/ppermute | solution.py:85
  611.3 16.1 %collective-permute-start.14 = (bf16[2,48,3072]{2,1,0:T(8,128)(2,1)S(1)}, bf16[2,48,3072]{2,1,0:T(8,128)(2,1)S(1)}, u32[]{:S(2)}, u32[]{:S(2)}) collective-permute-start(bf16[2,48,3072]{2,1,0:T(8,128)(2,1)S(1)} %add_convert_fusion.4), channel_id=1, source_target_pairs={{0,4},{1,5},{2,6},{3,7},{4,0},{5,1},{6,2},{7,3},{8,12},{9,13},{10,... | collective-permute-start | bytes 1769480 | tf_op jit(solution)/shard_map/ppermute | solution.py:85
  612.0 7.6 %collective-permute-start.1 = (f32[2,768]{1,0:T(2,128)S(1)}, f32[2,768]{1,0:T(2,128)S(1)}, u32[]{:S(2)}, u32[]{:S(2)}) collective-permute-start(f32[2,768]{1,0:T(2,128)S(1)} %fusion.53), channel_id=1, source_target_pairs={{0,32},{16,48},{32,0},{48,16},{64,96},{80,112},{96,64},{112,80},{1... | collective-permute-start | bytes 18440 | tf_op jit(solution)/shard_map/ppermute | solution.py:85
  619.6 10.6 %collective-permute-start.2 = (f32[2,768]{1,0:T(2,128)S(1)}, f32[2,768]{1,0:T(2,128)S(1)}, u32[]{:S(2)}, u32[]{:S(2)}) collective-permute-start(f32[2,768]{1,0:T(2,128)S(1)} %fusion.77), channel_id=1, source_target_pairs={{0,64},{16,80},{32,96},{48,112},{64,0},{80,16},{96,32},{112,48},{1... | collective-permute-start | bytes 18440 | tf_op jit(solution)/shard_map/ppermute | solution.py:85
  621.1 12.3 %collective-permute-start.8 = (bf16[48,3104]{1,0:T(8,128)(2,1)}, bf16[48,3104]{1,0:T(8,128)(2,1)S(1)}, u32[]{:S(2)}, u32[]{:S(2)}) collective-permute-start(bf16[48,3104]{1,0:T(8,128)(2,1)} %reduce-scatter.5.cloned.1.call-done), channel_id=1, source_target_pairs={{0,1},{1,0},{2,3},{3,2},{4,5},{5,4},{6,7},{7,6},{8,9},{9,8},{10,11... | collective-permute-start | bytes 893960 | tf_op jit(solution)/shard_map/ppermute | solution.py:85
  627.5 26.8 %copy-start.2 = (f32[197,768]{1,0:T(8,128)S(1)}, f32[197,768]{1,0:T(8,128)}, u32[]{:S(2)}) copy-start(f32[197,768]{1,0:T(8,128)} %copy-done) | copy-start | bytes 1815556
  627.5 15.3 %collective-permute-start.15 = (bf16[2,48,3072]{2,1,0:T(8,128)(2,1)S(1)}, bf16[2,48,3072]{2,1,0:T(8,128)(2,1)S(1)}, u32[]{:S(2)}, u32[]{:S(2)}) collective-permute-start(bf16[2,48,3072]{2,1,0:T(8,128)(2,1)S(1)} %add_convert_fusion.3), channel_id=1, source_target_pairs={{0,8},{1,9},{2,10},{3,11},{4,12},{5,13},{6,14},{7,15},{8,0},{9,1},... | collective-permute-start | bytes 1769480 | tf_op jit(solution)/shard_map/ppermute | solution.py:85
  630.2 13.7 %collective-permute-start.3 = (f32[2,768]{1,0:T(2,128)S(1)}, f32[2,768]{1,0:T(2,128)S(1)}, u32[]{:S(2)}, u32[]{:S(2)}) collective-permute-start(f32[2,768]{1,0:T(2,128)S(1)} %add.113), channel_id=1, source_target_pairs={{0,128},{16,144},{32,160},{48,176},{64,192},{80,208},{96,224},{112... | collective-permute-start | bytes 18440 | tf_op jit(solution)/shard_map/ppermute | solution.py:85
  634.5 14.8 %collective-permute-start.9 = (bf16[48,3104]{1,0:T(8,128)(2,1)S(1)}, bf16[48,3104]{1,0:T(8,128)(2,1)S(1)}, u32[]{:S(2)}, u32[]{:S(2)}) collective-permute-start(bf16[48,3104]{1,0:T(8,128)(2,1)S(1)} %add_convert_fusion.8), channel_id=1, source_target_pairs={{0,2},{1,3},{2,0},{3,1},{4,6},{5,7},{6,4},{7,5},{8,10},{9,11},{10,... | collective-permute-start | bytes 893960 | tf_op jit(solution)/shard_map/ppermute | solution.py:85
  643.9 17.4 %copy-start.15 = (f32[197,2,128]{2,1,0:T(2,128)S(1)}, f32[197,2,128]{2,1,0:T(2,128)}, u32[]{:S(2)}) copy-start(f32[197,2,128]{2,1,0:T(2,128)} %copy-done.14) | copy-start | bytes 605188
  643.9 17.4 %copy-start.16 = (bf16[2,2,128,768]{3,2,1,0:T(8,128)(2,1)S(1)}, bf16[2,2,128,768]{3,2,1,0:T(8,128)(2,1)}, u32[]{:S(2)}) copy-start(bf16[2,2,128,768]{3,2,1,0:T(8,128)(2,1)} %reduce-scatter.3.cloned.1.call-done) | copy-start | bytes 2359300
  643.9 5.2 collective-permute-start.4
  649.2 4.5 collective-permute-start.5
  649.4 11.0 %collective-permute-start.10 = (bf16[48,3104]{1,0:T(8,128)(2,1)S(1)}, bf16[48,3104]{1,0:T(8,128)(2,1)S(1)}, u32[]{:S(2)}, u32[]{:S(2)}) collective-permute-start(bf16[48,3104]{1,0:T(8,128)(2,1)S(1)} %add_convert_fusion.7), channel_id=1, source_target_pairs={{0,4},{1,5},{2,6},{3,7},{4,0},{5,1},{6,2},{7,3},{8,12},{9,13},{10,... | collective-permute-start | bytes 893960 | tf_op jit(solution)/shard_map/ppermute | solution.py:85
  653.7 3.9 collective-permute-start.6
  657.6 5.1 collective-permute-start.7
  660.4 8.5 %collective-permute-start.11 = (bf16[48,3104]{1,0:T(8,128)(2,1)S(1)}, bf16[48,3104]{1,0:T(8,128)(2,1)S(1)}, u32[]{:S(2)}, u32[]{:S(2)}) collective-permute-start(bf16[48,3104]{1,0:T(8,128)(2,1)S(1)} %add_convert_fusion.6), channel_id=1, source_target_pairs={{0,8},{1,9},{2,10},{3,11},{4,12},{5,13},{6,14},{7,15},{8,0},{9,1},... | collective-permute-start | bytes 893960 | tf_op jit(solution)/shard_map/ppermute | solution.py:85
  (9 other events, 9.1 us)
Sparse Core Ops, SparseCore 0:
  11.2 85.0 all-gather.2
  114.3 148.2 all-gather.4
  285.9 171.9 reduce-scatter.2
  488.0 126.3 reduce-scatter.4

commit v6 on v5

--- a/solution.py
+++ b/solution.py
@@ -13,7 +13,7 @@
 
 
 EPS = 1e-06
-ROW_TILE = 256
+ROW_TILE = 512
 
 def expert_kernel(rows_ref, geout_ref, w_in_ref, w_out_ref, parts_ref, act_ref, gpre_ref):
     rows = rows_ref[...]
@@ -80,11 +80,16 @@
 def butterfly_sum(value, axis, size, wire=None):
     step = 1
     while step < size:
-        pairs = [(i, i ^ step) for i in range(size)]
+        radix = 4 if (size // step) % 4 == 0 else 2
         sent = value if wire is None else value.astype(wire)
-        other = lax.ppermute(sent, axis, pairs)
-        value = sent.astype(jnp.float32) + other.astype(jnp.float32)
-        step *= 2
+        got = [
+            lax.ppermute(sent, axis, [(i, i ^ (shift * step)) for i in range(size)]).astype(jnp.float32)
+            for shift in range(1, radix)
+        ]
+        value = sent.astype(jnp.float32) + got[0]
+        if radix == 4:
+            value = value + (got[1] + got[2])
+        step *= radix
     return value
 
 

time: 680 us -> 768 us (1.13)
  starting transfers between devices: 39.3 us -> 114 us
  waiting for transfers between devices: 462 us -> 474 us
    ppermute x20 -> x30, starting transfers between devices: 34.2 us -> 109 us  [butterfly_sum(): lax.ppermute(sent, axis, [(i, i ^ shift * step) for i in range(size)])]
    ppermute x20 -> x30, waiting for transfers between devices: 98.2 us -> 123 us  [butterfly_sum(): lax.ppermute(sent, axis, [(i, i ^ shift * step) for i in range(size)])]
    all_to_all x1, waiting for transfers between devices: 18.2 us -> 5.05 us  [body(): lax.all_to_all(gin_cols.astype(jnp.bfloat16), 'shard', 1, 2, tiled=True)]
    unnamed x70 -> x62, local copies, waits for them, and re-layouts: 15.4 us -> 14.7 us
  transfers between devices with their start and end apart: 25 -> 35, of which waited for: 17 -> 17; matrix products, arithmetic and copies ran while one was open for 7% -> 7% of each run, Pallas kernels for 0% -> 0%
where the time goes in v6:
time: 768 us; the launch traced here: 758 us
  waiting for transfers between devices  474 us (62%)
  starting transfers between devices  114 us (15%)
  matrix products  40.7 us (5%)
  blocking collectives  37.3 us (5%)
  local copies, waits for them, and re-layouts  33.6 us (4%)
  other arithmetic  25.2 us (3%)
  Pallas kernels  18.7 us (2%)
  between operations  14.8 us (2%)
    reduce_scatter x1, waiting for transfers between devices, body(): lax.psum_scatter(parts, 'shard', scatter_dimension=2, tiled=True)  172 us
    ppermute x30, waiting for transfers between devices, butterfly_sum(): lax.ppermute(sent, axis, [(i, i ^ shift * step) for i in range(size)])  123 us
    ppermute x30, starting transfers between devices, butterfly_sum(): lax.ppermute(sent, axis, [(i, i ^ shift * step) for i in range(size)])  109 us
    all_gather x1, waiting for transfers between devices, body(): lax.all_gather(jnp.stack([expert_rows, grad_eout]), 'shard', axis=2, tile...  94.7 us
    all_gather x1, waiting for transfers between devices, body(): lax.all_gather(jnp.concatenate([w_qkv, w_proj, w_router], axis=1), 'shard...  78.8 us
    all_to_all x1, blocking collectives, body(): w_in_cols = lax.all_to_all(w_expert_in, 'shard', 2, 1, tiled=True)  37.3 us
    pallas_call x1, Pallas kernels, expert_block(): pl.pallas_call(expert_kernel, grid=grid, in_specs=[pl.BlockSpec((None, No...  18.7 us
  transfers between devices with their start and end apart: 35, of which 17 were waited for; matrix products, arithmetic and copies ran while one was open for 7% of the time, Pallas kernels for 0%

profile of v6, /device:TPU:8, one launch (start us, length us, event | category | flops | bytes accessed | tf_op | source)
XLA Modules:
  0.0 758.2 jit_solution(12984334254564584721)
XLA Ops:
  8.0 1.7 pad_maximum_fusion.5
  17.5 78.8 %all-gather.3.cloned.1.call-done = bf16[768,3104]{1,0:T(8,128)(2,1)} async-done(((bf16[48,3104]{1,0:T(8,128)(2,1)}), bf16[768,3104]{1,0:T(8,128)(2,1)}) %all-gather.3.cloned.1.call-update) | async-done | bytes 4767760 | tf_op jit(solution)/shard_map/all_gather | solution.py:186
  96.3 3.1 convolution_convert_fusion.1
  103.6 1.9 fusion.56
  108.1 2.4 multiply_reduce_fusion.2
  113.7 4.3 copy.164
  118.0 4.1 reshape.249
  122.1 37.3 %all_to_all.36 = bf16[16,2,9216]{2,1,0:T(2,128)(2,1)} all-to-all(bf16[16,2,9216]{2,1,0:T(2,128)(2,1)} %reshape.249), channel_id=1, replica_groups=mesh['shard'=16,'rep'=16] {'shard'}, dimensions={0} | all-to-all | bytes 1179648 | tf_op jit(solution)/shard_map/all_to_all | solution.py:211
  159.4 3.3 reshape.250
  162.7 4.7 copy.165
  167.4 94.7 %all-gather.5.cloned.1.call-done.rows_ref.geout_ref = bf16[2,2,2048,768]{3,2,1,0:T(8,128)(2,1)} async-done(((bf16[2,2,128,768]{3,2,1,0:T(8,128)(2,1)}), bf16[2,2,2048,768]{3,2,1,0:T(8,128)(2,1)}) %all-gather.5.cloned.1.call-update) | async-done | bytes 12582928 | tf_op jit(solution)/shard_map/all_gather | solution.py:214
  262.1 18.7 %shard_map.178 = (bf16[2,2,2048,768]{3,2,1,0:T(8,128)(2,1)}, bf16[2,2048,192]{2,1,0:T(8,128)(2,1)}, bf16[2,2048,192]{2,1,0:T(8,128)(2,1)}) custom-call(bf16[2,2,2048,768]{3,2,1,0:T(8,128)(2,1)} %all-gather.5.cloned.1.call-done.rows_ref.geout_ref, bf16[2,2,2048,768]{3,2,1,0:T(8,128)(2,1)} %all-gather.5.cloned.1.call-done.rows_ref.geout_ref, ...), custom_call_target="tpu_custom_call" | custom-call | tf_op jit(solution)/shard_map/pallas_call | solution.py:41
  281.0 172.0 %reduce-scatter.3.cloned.1.call-done = bf16[2,2,128,768]{3,2,1,0:T(8,128)(2,1)} async-done(((bf16[2,2,2048,768]{3,2,1,0:T(8,128)(2,1)}), bf16[2,2,128,768]{3,2,1,0:T(8,128)(2,1)}) %reduce-scatter.3.cloned.1.call-update) | async-done | bytes 786448 | tf_op jit(solution)/shard_map/reduce_scatter | solution.py:219
  454.5 2.8 fusion.30
  464.2 2.5 convolution_convert_fusion.7
  467.9 2.0 copy.171
  475.5 2.4 convolution_convert_fusion
  477.9 2.3 pad_maximum_fusion
  480.3 4.8 fusion.6
  485.1 1.8 copy.179
  486.9 4.5 all-to-all-start.1
  491.4 6.1 fusion.7
  497.6 2.1 collective-permute-start.26
  500.3 1.8 collective-permute-start.24
  502.1 5.1 all-to-all-done.1
  508.4 4.2 collective-permute-start.20
  512.6 26.5 %collective-permute-start.19 = (bf16[2,48,3072]{2,1,0:T(8,128)(2,1)S(1)}, bf16[2,48,3072]{2,1,0:T(8,128)(2,1)S(1)}, u32[]{:S(2)}, u32[]{:S(2)}) collective-permute-start(bf16[2,48,3072]{2,1,0:T(8,128)(2,1)S(1)} %all_to_all.33), channel_id=1, source_target_pairs={{0,2},{1,3},{2,0},{3,1},{4,6},{5,7},{6,4},{7,5},{8,10},{9,11},{10,... | collective-permute-start | bytes 1769480 | tf_op jit(solution)/shard_map/ppermute | solution.py:86
  539.1 37.9 %collective-permute-start.18 = (bf16[2,48,3072]{2,1,0:T(8,128)(2,1)S(1)}, bf16[2,48,3072]{2,1,0:T(8,128)(2,1)S(1)}, u32[]{:S(2)}, u32[]{:S(2)}) collective-permute-start(bf16[2,48,3072]{2,1,0:T(8,128)(2,1)S(1)} %all_to_all.33), channel_id=1, source_target_pairs={{0,1},{1,0},{2,3},{3,2},{4,5},{5,4},{6,7},{7,6},{8,9},{9,8},{10,11... | collective-permute-start | bytes 1769480 | tf_op jit(solution)/shard_map/ppermute | solution.py:86
  577.1 43.5 %collective-permute-done.25 = bf16[2,192,768]{2,1,0:T(8,128)(2,1)} collective-permute-done((bf16[2,192,768]{2,1,0:T(8,128)(2,1)}, bf16[2,192,768]{2,1,0:T(8,128)(2,1)}, u32[]{:S(2)}, u32[]{:S(2)}) %collective-permute-start.25) | collective-permute-done | bytes 589856 | tf_op jit(solution)/shard_map/ppermute | solution.py:86
  620.6 1.9 add_convert_fusion
  622.5 2.8 collective-permute-start.29
  626.7 19.1 %collective-permute-done.19 = bf16[2,48,3072]{2,1,0:T(8,128)(2,1)S(1)} collective-permute-done((bf16[2,48,3072]{2,1,0:T(8,128)(2,1)S(1)}, bf16[2,48,3072]{2,1,0:T(8,128)(2,1)S(1)}, u32[]{:S(2)}, u32[]{:S(2)}) %collective-permute-start.19) | collective-permute-done | bytes 589856 | tf_op jit(solution)/shard_map/ppermute | solution.py:86
  646.1 2.8 collective-permute-start.23
  649.7 2.9 collective-permute-done.29
  654.8 22.2 %collective-permute-done.23 = bf16[2,48,3072]{2,1,0:T(8,128)(2,1)S(1)} collective-permute-done((bf16[2,48,3072]{2,1,0:T(8,128)(2,1)S(1)}, bf16[2,48,3072]{2,1,0:T(8,128)(2,1)S(1)}, u32[]{:S(2)}, u32[]{:S(2)}) %collective-permute-start.23) | collective-permute-done | bytes 589856 | tf_op jit(solution)/shard_map/ppermute | solution.py:86
  679.0 3.5 fusion.27
  682.6 4.6 collective-permute-start.1
  690.2 3.9 collective-permute-done.2
  698.3 2.5 collective-permute-done.4
  700.8 2.9 collective-permute-start.8
  704.8 1.9 collective-permute-start.6
  706.6 2.5 collective-permute-start.14
  709.2 1.8 collective-permute-start.12
  712.2 4.6 collective-permute-done.7
  716.8 2.8 collective-permute-start.11
  721.0 11.1 %collective-permute-done.13 = bf16[48,3104]{1,0:T(8,128)(2,1)S(1)} collective-permute-done((bf16[48,3104]{1,0:T(8,128)(2,1)}, bf16[48,3104]{1,0:T(8,128)(2,1)S(1)}, u32[]{:S(2)}, u32[]{:S(2)}) %collective-permute-start.13) | collective-permute-done | bytes 298016 | tf_op jit(solution)/shard_map/ppermute | solution.py:86
  733.2 2.7 collective-permute-start.17
  738.1 10.2 %collective-permute-done.17 = bf16[48,3104]{1,0:T(8,128)(2,1)S(1)} collective-permute-done((bf16[48,3104]{1,0:T(8,128)(2,1)S(1)}, bf16[48,3104]{1,0:T(8,128)(2,1)S(1)}, u32[]{:S(2)}, u32[]{:S(2)}) %collective-permute-start.17) | collective-permute-done | bytes 298016 | tf_op jit(solution)/shard_map/ppermute | solution.py:86
  (188 shorter events, 59.2 us)
Async XLA Ops:
  7.2 89.1 %all-gather.3.cloned.1.call-start = ((), (), s32[]{:S(2)}) async-start(), calls=%async_computation.4 | async-start | bytes 5222400 | tf_op jit(solution)/shard_map/all_gather | solution.py:186
  9.7 252.3 %all-gather.5.cloned.1.call-start = ((), (), s32[]{:S(2)}) async-start(), calls=%async_computation.5 | async-start | bytes 13369344 | tf_op jit(solution)/shard_map/all_gather | solution.py:214
  15.4 84.0 %copy-start.23 = (f32[197]{0:T(256)}, f32[197]{0:T(256)S(1)}, u32[]{:S(2)}) copy-start(f32[197]{0:T(256)S(1)} %broadcast_multiply_fusion.5) | copy-start | bytes 2368
  16.6 82.8 %copy-start.26 = (f32[197]{0:T(256)}, f32[197]{0:T(256)S(1)}, u32[]{:S(2)}) copy-start(f32[197]{0:T(256)S(1)} %add_rsqrt_fusion.1) | copy-start | bytes 2368
  99.6 3.3 copy-start.4
  103.6 3.6 copy-start.7
  103.6 3.6 copy-start.21
  113.6 339.3 %reduce-scatter.3.cloned.1.call-start = ((), (), s32[]{:S(2)}) async-start(), calls=%async_computation.6 | async-start | bytes 13369344 | tf_op jit(solution)/shard_map/reduce_scatter | solution.py:219
  280.8 425.8 %reduce-scatter.5.cloned.1.call-start = ((), (), s32[]{:S(2)}) async-start(), calls=%async_computation.7 | async-start | bytes 5222400 | tf_op jit(solution)/shard_map/reduce_scatter | solution.py:256
  458.8 4.3 copy-start.10
  471.4 2.2 copy-start.5
  472.4 2.4 copy-start.1
  486.9 20.3 %all-to-all-start.1 = ((bf16[2,768,192]{2,0,1:T(2,128)(2,1)}), bf16[2,768,192]{2,0,1:T(2,128)(2,1)S(1)}, u32[]{:S(2)}, u32[]{:S(2)}) async-start(bf16[2,768,192]{2,0,1:T(2,128)(2,1)} %copy.179), calls=%async_computation.3 | async-start | bytes 1572864 | tf_op jit(solution)/shard_map/all_to_all | solution.py:228
  497.6 41.6 %collective-permute-start.26 = (bf16[2,192,768]{2,1,0:T(8,128)(2,1)}, bf16[2,192,768]{2,1,0:T(8,128)(2,1)}, u32[]{:S(2)}, u32[]{:S(2)}) collective-permute-start(bf16[2,192,768]{2,1,0:T(8,128)(2,1)} %fusion.7), channel_id=1, source_target_pairs={{0,3},{1,2},{2,1},{3,0},{4,7},{5,6},{6,5},{7,4},{8,11},{9,10},{10,... | collective-permute-start | bytes 1769480 | tf_op jit(solution)/shard_map/ppermute | solution.py:86
  499.7 120.9 %collective-permute-start.25 = (bf16[2,192,768]{2,1,0:T(8,128)(2,1)}, bf16[2,192,768]{2,1,0:T(8,128)(2,1)}, u32[]{:S(2)}, u32[]{:S(2)}) collective-permute-start(bf16[2,192,768]{2,1,0:T(8,128)(2,1)} %fusion.7), channel_id=1, source_target_pairs={{0,2},{1,3},{2,0},{3,1},{4,6},{5,7},{6,4},{7,5},{8,10},{9,11},{10,... | collective-permute-start | bytes 1769480 | tf_op jit(solution)/shard_map/ppermute | solution.py:86
  500.3 120.3 %collective-permute-start.24 = (bf16[2,192,768]{2,1,0:T(8,128)(2,1)}, bf16[2,192,768]{2,1,0:T(8,128)(2,1)}, u32[]{:S(2)}, u32[]{:S(2)}) collective-permute-start(bf16[2,192,768]{2,1,0:T(8,128)(2,1)} %fusion.7), channel_id=1, source_target_pairs={{0,1},{1,0},{2,3},{3,2},{4,5},{5,4},{6,7},{7,6},{8,9},{9,8},{10,11... | collective-permute-start | bytes 1769480 | tf_op jit(solution)/shard_map/ppermute | solution.py:86
  508.4 117.7 %collective-permute-start.20 = (bf16[2,48,3072]{2,1,0:T(8,128)(2,1)S(1)}, bf16[2,48,3072]{2,1,0:T(8,128)(2,1)S(1)}, u32[]{:S(2)}, u32[]{:S(2)}) collective-permute-start(bf16[2,48,3072]{2,1,0:T(8,128)(2,1)S(1)} %all_to_all.33), channel_id=1, source_target_pairs={{0,3},{1,2},{2,1},{3,0},{4,7},{5,6},{6,5},{7,4},{8,11},{9,10},{10,... | collective-permute-start | bytes 1769480 | tf_op jit(solution)/shard_map/ppermute | solution.py:86
  512.6 133.1 %collective-permute-start.19 = (bf16[2,48,3072]{2,1,0:T(8,128)(2,1)S(1)}, bf16[2,48,3072]{2,1,0:T(8,128)(2,1)S(1)}, u32[]{:S(2)}, u32[]{:S(2)}) collective-permute-start(bf16[2,48,3072]{2,1,0:T(8,128)(2,1)S(1)} %all_to_all.33), channel_id=1, source_target_pairs={{0,2},{1,3},{2,0},{3,1},{4,6},{5,7},{6,4},{7,5},{8,10},{9,11},{10,... | collective-permute-start | bytes 1769480 | tf_op jit(solution)/shard_map/ppermute | solution.py:86
  539.1 106.6 %collective-permute-start.18 = (bf16[2,48,3072]{2,1,0:T(8,128)(2,1)S(1)}, bf16[2,48,3072]{2,1,0:T(8,128)(2,1)S(1)}, u32[]{:S(2)}, u32[]{:S(2)}) collective-permute-start(bf16[2,48,3072]{2,1,0:T(8,128)(2,1)S(1)} %all_to_all.33), channel_id=1, source_target_pairs={{0,1},{1,0},{2,3},{3,2},{4,5},{5,4},{6,7},{7,6},{8,9},{9,8},{10,11... | collective-permute-start | bytes 1769480 | tf_op jit(solution)/shard_map/ppermute | solution.py:86
  622.5 30.1 %collective-permute-start.29 = (bf16[2,192,768]{2,1,0:T(8,128)(2,1)S(1)}, bf16[2,192,768]{2,1,0:T(8,128)(2,1)S(1)}, u32[]{:S(2)}, u32[]{:S(2)}) collective-permute-start(bf16[2,192,768]{2,1,0:T(8,128)(2,1)S(1)} %add_convert_fusion), channel_id=1, source_target_pairs={{0,12},{1,13},{2,14},{3,15},{4,8},{5,9},{6,10},{7,11},{8,4},{9,5},... | collective-permute-start | bytes 1769480 | tf_op jit(solution)/shard_map/ppermute | solution.py:86
  625.3 27.6 %collective-permute-start.28 = (bf16[2,192,768]{2,1,0:T(8,128)(2,1)S(1)}, bf16[2,192,768]{2,1,0:T(8,128)(2,1)S(1)}, u32[]{:S(2)}, u32[]{:S(2)}) collective-permute-start(bf16[2,192,768]{2,1,0:T(8,128)(2,1)S(1)} %add_convert_fusion), channel_id=1, source_target_pairs={{0,8},{1,9},{2,10},{3,11},{4,12},{5,13},{6,14},{7,15},{8,0},{9,1},... | collective-permute-start | bytes 1769480 | tf_op jit(solution)/shard_map/ppermute | solution.py:86
  626.1 27.4 %collective-permute-start.27 = (bf16[2,192,768]{2,1,0:T(8,128)(2,1)S(1)}, bf16[2,192,768]{2,1,0:T(8,128)(2,1)S(1)}, u32[]{:S(2)}, u32[]{:S(2)}) collective-permute-start(bf16[2,192,768]{2,1,0:T(8,128)(2,1)S(1)} %add_convert_fusion), channel_id=1, source_target_pairs={{0,4},{1,5},{2,6},{3,7},{4,0},{5,1},{6,2},{7,3},{8,12},{9,13},{10,... | collective-permute-start | bytes 1769480 | tf_op jit(solution)/shard_map/ppermute | solution.py:86
  646.1 30.9 %collective-permute-start.23 = (bf16[2,48,3072]{2,1,0:T(8,128)(2,1)S(1)}, bf16[2,48,3072]{2,1,0:T(8,128)(2,1)S(1)}, u32[]{:S(2)}, u32[]{:S(2)}) collective-permute-start(bf16[2,48,3072]{2,1,0:T(8,128)(2,1)S(1)} %add_convert_fusion.1), channel_id=1, source_target_pairs={{0,12},{1,13},{2,14},{3,15},{4,8},{5,9},{6,10},{7,11},{8,4},{9,5},... | collective-permute-start | bytes 1769480 | tf_op jit(solution)/shard_map/ppermute | solution.py:86
  648.9 28.1 %collective-permute-start.22 = (bf16[2,48,3072]{2,1,0:T(8,128)(2,1)S(1)}, bf16[2,48,3072]{2,1,0:T(8,128)(2,1)S(1)}, u32[]{:S(2)}, u32[]{:S(2)}) collective-permute-start(bf16[2,48,3072]{2,1,0:T(8,128)(2,1)S(1)} %add_convert_fusion.1), channel_id=1, source_target_pairs={{0,8},{1,9},{2,10},{3,11},{4,12},{5,13},{6,14},{7,15},{8,0},{9,1},... | collective-permute-start | bytes 1769480 | tf_op jit(solution)/shard_map/ppermute | solution.py:86
  652.6 25.0 %collective-permute-start.21 = (bf16[2,48,3072]{2,1,0:T(8,128)(2,1)S(1)}, bf16[2,48,3072]{2,1,0:T(8,128)(2,1)S(1)}, u32[]{:S(2)}, u32[]{:S(2)}) collective-permute-start(bf16[2,48,3072]{2,1,0:T(8,128)(2,1)S(1)} %add_convert_fusion.1), channel_id=1, source_target_pairs={{0,4},{1,5},{2,6},{3,7},{4,0},{5,1},{6,2},{7,3},{8,12},{9,13},{10,... | collective-permute-start | bytes 1769480 | tf_op jit(solution)/shard_map/ppermute | solution.py:86
  654.8 24.2 %copy-start.17 = (bf16[12,64,197]{2,1,0:T(8,128)(2,1)S(1)}, bf16[12,64,197]{2,1,0:T(8,128)(2,1)}, u32[]{:S(2)}) copy-start(bf16[12,64,197]{2,1,0:T(8,128)(2,1)} %convolution_convert_fusion.3) | copy-start | bytes 907780
  654.8 24.2 %copy-start.18 = (bf16[12,64,197]{2,1,0:T(8,128)(2,1)S(1)}, bf16[12,64,197]{2,1,0:T(8,128)(2,1)}, u32[]{:S(2)}) copy-start(bf16[12,64,197]{2,1,0:T(8,128)(2,1)} %fusion.9) | copy-start | bytes 907780
  654.8 24.2 %copy-start.19 = (bf16[12,64,197]{2,1,0:T(8,128)(2,1)S(1)}, bf16[12,64,197]{2,1,0:T(8,128)(2,1)}, u32[]{:S(2)}) copy-start(bf16[12,64,197]{2,1,0:T(8,128)(2,1)} %fusion.8) | copy-start | bytes 907780
  682.5 28.5 %copy-start.14 = (f32[197,2,128]{2,1,0:T(2,128)S(1)}, f32[197,2,128]{2,1,0:T(2,128)}, u32[]{:S(2)}) copy-start(f32[197,2,128]{2,1,0:T(2,128)} %copy-done.13) | copy-start | bytes 605188
  682.5 28.5 %copy-start.15 = (bf16[2,2,128,768]{3,2,1,0:T(8,128)(2,1)S(1)}, bf16[2,2,128,768]{3,2,1,0:T(8,128)(2,1)}, u32[]{:S(2)}) copy-start(bf16[2,2,128,768]{3,2,1,0:T(8,128)(2,1)} %reduce-scatter.3.cloned.1.call-done) | copy-start | bytes 2359300
  682.6 7.6 %collective-permute-start.1 = (f32[2,768]{1,0:T(2,128)S(1)}, f32[2,768]{1,0:T(2,128)S(1)}, u32[]{:S(2)}, u32[]{:S(2)}) collective-permute-start(f32[2,768]{1,0:T(2,128)S(1)} %pad_maximum_fusion.6), channel_id=1, source_target_pairs={{0,32},{16,48},{32,0},{48,16},{64,96},{80,112},{96,64},{112,80},{1... | collective-permute-start | bytes 18440 | tf_op jit(solution)/shard_map/ppermute | solution.py:86
  687.1 7.0 collective-permute-start.2
  687.1 7.0 collective-permute-start
  694.1 4.2 collective-permute-start.5
  695.7 5.1 collective-permute-start.4
  696.8 4.0 collective-permute-start.3
  700.8 8.4 %collective-permute-start.8 = (f32[2,768]{1,0:T(2,128)S(1)}, f32[2,768]{1,0:T(2,128)S(1)}, u32[]{:S(2)}, u32[]{:S(2)}) collective-permute-start(f32[2,768]{1,0:T(2,128)S(1)} %add_add_fusion.5), channel_id=1, source_target_pairs={{0,3},{1,2},{2,1},{3,0},{4,7},{5,6},{6,5},{7,4},{8,11},{9,10},{10,... | collective-permute-start | bytes 18440 | tf_op jit(solution)/shard_map/ppermute | solution.py:86
  704.7 12.0 %collective-permute-start.7 = (f32[2,768]{1,0:T(2,128)S(1)}, f32[2,768]{1,0:T(2,128)S(1)}, u32[]{:S(2)}, u32[]{:S(2)}) collective-permute-start(f32[2,768]{1,0:T(2,128)S(1)} %add_add_fusion.5), channel_id=1, source_target_pairs={{0,2},{1,3},{2,0},{3,1},{4,6},{5,7},{6,4},{7,5},{8,10},{9,11},{10,... | collective-permute-start | bytes 18440 | tf_op jit(solution)/shard_map/ppermute | solution.py:86
  704.8 12.0 %collective-permute-start.6 = (f32[2,768]{1,0:T(2,128)S(1)}, f32[2,768]{1,0:T(2,128)S(1)}, u32[]{:S(2)}, u32[]{:S(2)}) collective-permute-start(f32[2,768]{1,0:T(2,128)S(1)} %add_add_fusion.5), channel_id=1, source_target_pairs={{0,1},{1,0},{2,3},{3,2},{4,5},{5,4},{6,7},{7,6},{8,9},{9,8},{10,11... | collective-permute-start | bytes 18440 | tf_op jit(solution)/shard_map/ppermute | solution.py:86
  706.6 13.8 %collective-permute-start.14 = (bf16[48,3104]{1,0:T(8,128)(2,1)}, bf16[48,3104]{1,0:T(8,128)(2,1)S(1)}, u32[]{:S(2)}, u32[]{:S(2)}) collective-permute-start(bf16[48,3104]{1,0:T(8,128)(2,1)} %reduce-scatter.5.cloned.1.call-done), channel_id=1, source_target_pairs={{0,3},{1,2},{2,1},{3,0},{4,7},{5,6},{6,5},{7,4},{8,11},{9,10},{10,... | collective-permute-start | bytes 893960 | tf_op jit(solution)/shard_map/ppermute | solution.py:86
  709.2 22.9 %collective-permute-start.13 = (bf16[48,3104]{1,0:T(8,128)(2,1)}, bf16[48,3104]{1,0:T(8,128)(2,1)S(1)}, u32[]{:S(2)}, u32[]{:S(2)}) collective-permute-start(bf16[48,3104]{1,0:T(8,128)(2,1)} %reduce-scatter.5.cloned.1.call-done), channel_id=1, source_target_pairs={{0,2},{1,3},{2,0},{3,1},{4,6},{5,7},{6,4},{7,5},{8,10},{9,11},{10,... | collective-permute-start | bytes 893960 | tf_op jit(solution)/shard_map/ppermute | solution.py:86
  709.2 22.9 %collective-permute-start.12 = (bf16[48,3104]{1,0:T(8,128)(2,1)}, bf16[48,3104]{1,0:T(8,128)(2,1)S(1)}, u32[]{:S(2)}, u32[]{:S(2)}) collective-permute-start(bf16[48,3104]{1,0:T(8,128)(2,1)} %reduce-scatter.5.cloned.1.call-done), channel_id=1, source_target_pairs={{0,1},{1,0},{2,3},{3,2},{4,5},{5,4},{6,7},{7,6},{8,9},{9,8},{10,11... | collective-permute-start | bytes 893960 | tf_op jit(solution)/shard_map/ppermute | solution.py:86
  716.8 20.1 %collective-permute-start.11 = (f32[2,768]{1,0:T(2,128)S(1)}, f32[2,768]{1,0:T(2,128)S(1)}, u32[]{:S(2)}, u32[]{:S(2)}) collective-permute-start(f32[2,768]{1,0:T(2,128)S(1)} %add_add_fusion.4), channel_id=1, source_target_pairs={{0,12},{1,13},{2,14},{3,15},{4,8},{5,9},{6,10},{7,11},{8,4},{9,5},... | collective-permute-start | bytes 18440 | tf_op jit(solution)/shard_map/ppermute | solution.py:86
  719.6 17.8 %collective-permute-start.10 = (f32[2,768]{1,0:T(2,128)S(1)}, f32[2,768]{1,0:T(2,128)S(1)}, u32[]{:S(2)}, u32[]{:S(2)}) collective-permute-start(f32[2,768]{1,0:T(2,128)S(1)} %add_add_fusion.4), channel_id=1, source_target_pairs={{0,8},{1,9},{2,10},{3,11},{4,12},{5,13},{6,14},{7,15},{8,0},{9,1},... | collective-permute-start | bytes 18440 | tf_op jit(solution)/shard_map/ppermute | solution.py:86
  720.4 17.0 %collective-permute-start.9 = (f32[2,768]{1,0:T(2,128)S(1)}, f32[2,768]{1,0:T(2,128)S(1)}, u32[]{:S(2)}, u32[]{:S(2)}) collective-permute-start(f32[2,768]{1,0:T(2,128)S(1)} %add_add_fusion.4), channel_id=1, source_target_pairs={{0,4},{1,5},{2,6},{3,7},{4,0},{5,1},{6,2},{7,3},{8,12},{9,13},{10,... | collective-permute-start | bytes 18440 | tf_op jit(solution)/shard_map/ppermute | solution.py:86
  733.2 15.0 %collective-permute-start.17 = (bf16[48,3104]{1,0:T(8,128)(2,1)S(1)}, bf16[48,3104]{1,0:T(8,128)(2,1)S(1)}, u32[]{:S(2)}, u32[]{:S(2)}) collective-permute-start(bf16[48,3104]{1,0:T(8,128)(2,1)S(1)} %add_convert_fusion.2), channel_id=1, source_target_pairs={{0,12},{1,13},{2,14},{3,15},{4,8},{5,9},{6,10},{7,11},{8,4},{9,5},... | collective-permute-start | bytes 893960 | tf_op jit(solution)/shard_map/ppermute | solution.py:86
  736.0 12.3 %collective-permute-start.16 = (bf16[48,3104]{1,0:T(8,128)(2,1)S(1)}, bf16[48,3104]{1,0:T(8,128)(2,1)S(1)}, u32[]{:S(2)}, u32[]{:S(2)}) collective-permute-start(bf16[48,3104]{1,0:T(8,128)(2,1)S(1)} %add_convert_fusion.2), channel_id=1, source_target_pairs={{0,8},{1,9},{2,10},{3,11},{4,12},{5,13},{6,14},{7,15},{8,0},{9,1},... | collective-permute-start | bytes 893960 | tf_op jit(solution)/shard_map/ppermute | solution.py:86
  736.9 12.0 %collective-permute-start.15 = (bf16[48,3104]{1,0:T(8,128)(2,1)S(1)}, bf16[48,3104]{1,0:T(8,128)(2,1)S(1)}, u32[]{:S(2)}, u32[]{:S(2)}) collective-permute-start(bf16[48,3104]{1,0:T(8,128)(2,1)S(1)} %add_convert_fusion.2), channel_id=1, source_target_pairs={{0,4},{1,5},{2,6},{3,7},{4,0},{5,1},{6,2},{7,3},{8,12},{9,13},{10,... | collective-permute-start | bytes 893960 | tf_op jit(solution)/shard_map/ppermute | solution.py:86
  (15 other events, 23.0 us)
Sparse Core Ops, SparseCore 0:
  11.2 85.0 all-gather.2
  113.8 148.2 all-gather.4
  280.9 172.0 reduce-scatter.2
  480.4 129.5 reduce-scatter.4

commit v7 on v5

--- a/solution.py
+++ b/solution.py
@@ -13,7 +13,7 @@
 
 
 EPS = 1e-06
-ROW_TILE = 256
+ROW_TILE = 512
 
 def expert_kernel(rows_ref, geout_ref, w_in_ref, w_out_ref, parts_ref, act_ref, gpre_ref):
     rows = rows_ref[...]

time: 680 us -> 684 us (level); the launches traced: 678 us -> 673 us
  waiting for transfers between devices: 462 us -> 455 us
    all_to_all x1, waiting for transfers between devices: 18.2 us -> 8.17 us  [body(): lax.all_to_all(gin_cols.astype(jnp.bfloat16), 'shard', 1, 2, tiled=True)]
where the time goes in v7:
time: 684 us; the launch traced here: 673 us
  waiting for transfers between devices  455 us (67%)
  starting transfers between devices  45.7 us (7%)
  matrix products  38.7 us (6%)
  blocking collectives  37.3 us (5%)
  local copies, waits for them, and re-layouts  35.4 us (5%)
  other arithmetic  27.7 us (4%)
  Pallas kernels  18.7 us (3%)
  between operations  14.7 us (2%)
    reduce_scatter x1, waiting for transfers between devices, body(): lax.psum_scatter(parts, 'shard', scatter_dimension=2, tiled=True)  172 us
    ppermute x20, waiting for transfers between devices, butterfly_sum(): other = lax.ppermute(sent, axis, pairs)  102 us
    all_gather x1, waiting for transfers between devices, body(): lax.all_gather(jnp.stack([expert_rows, grad_eout]), 'shard', axis=2, tile...  94.7 us
    all_gather x1, waiting for transfers between devices, body(): lax.all_gather(jnp.concatenate([w_qkv, w_proj, w_router], axis=1), 'shard...  78.7 us
    ppermute x20, starting transfers between devices, butterfly_sum(): other = lax.ppermute(sent, axis, pairs)  40.5 us
    all_to_all x1, blocking collectives, body(): w_in_cols = lax.all_to_all(w_expert_in, 'shard', 2, 1, tiled=True)  37.3 us
    pallas_call x1, Pallas kernels, expert_block(): pl.pallas_call(expert_kernel, grid=grid, in_specs=[pl.BlockSpec((None, No...  18.7 us
    unnamed x70, local copies, waits for them, and re-layouts  15.4 us
  transfers between devices with their start and end apart: 25, of which 17 were waited for; matrix products, arithmetic and copies ran while one was open for 7% of the time, Pallas kernels for 0%

profile of v7, /device:TPU:8, one launch (start us, length us, event | category | flops | bytes accessed | tf_op | source)
XLA Modules:
  0.0 673.3 jit_solution(9053657161327820946)
XLA Ops:
  8.0 1.7 pad_maximum_fusion.5
  17.5 78.7 %all-gather.3.cloned.1.call-done = bf16[768,3104]{1,0:T(8,128)(2,1)} async-done(((bf16[48,3104]{1,0:T(8,128)(2,1)}), bf16[768,3104]{1,0:T(8,128)(2,1)}) %all-gather.3.cloned.1.call-update) | async-done | bytes 4767760 | tf_op jit(solution)/shard_map/all_gather | solution.py:181
  96.3 3.1 convolution_convert_fusion.1
  103.6 2.0 fusion.57
  108.6 2.4 multiply_reduce_fusion.2
  111.7 1.5 fusion.13
  114.2 4.3 copy.164
  118.5 4.1 reshape.249
  122.6 37.3 %all_to_all.36 = bf16[16,2,9216]{2,1,0:T(2,128)(2,1)} all-to-all(bf16[16,2,9216]{2,1,0:T(2,128)(2,1)} %reshape.249), channel_id=1, replica_groups=mesh['shard'=16,'rep'=16] {'shard'}, dimensions={0} | all-to-all | bytes 1179648 | tf_op jit(solution)/shard_map/all_to_all | solution.py:206
  159.9 3.3 reshape.250
  163.2 4.7 copy.165
  167.9 94.7 %all-gather.5.cloned.1.call-done.rows_ref.geout_ref = bf16[2,2,2048,768]{3,2,1,0:T(8,128)(2,1)} async-done(((bf16[2,2,128,768]{3,2,1,0:T(8,128)(2,1)}), bf16[2,2,2048,768]{3,2,1,0:T(8,128)(2,1)}) %all-gather.5.cloned.1.call-update) | async-done | bytes 12582928 | tf_op jit(solution)/shard_map/all_gather | solution.py:209
  262.6 18.7 %shard_map.178 = (bf16[2,2,2048,768]{3,2,1,0:T(8,128)(2,1)}, bf16[2,2048,192]{2,1,0:T(8,128)(2,1)}, bf16[2,2048,192]{2,1,0:T(8,128)(2,1)}) custom-call(bf16[2,2,2048,768]{3,2,1,0:T(8,128)(2,1)} %all-gather.5.cloned.1.call-done.rows_ref.geout_ref, bf16[2,2,2048,768]{3,2,1,0:T(8,128)(2,1)} %all-gather.5.cloned.1.call-done.rows_ref.geout_ref, ...), custom_call_target="tpu_custom_call" | custom-call | tf_op jit(solution)/shard_map/pallas_call | solution.py:41
  281.6 171.9 %reduce-scatter.3.cloned.1.call-done = bf16[2,2,128,768]{3,2,1,0:T(8,128)(2,1)} async-done(((bf16[2,2,2048,768]{3,2,1,0:T(8,128)(2,1)}), bf16[2,2,128,768]{3,2,1,0:T(8,128)(2,1)}) %reduce-scatter.3.cloned.1.call-update) | async-done | bytes 786448 | tf_op jit(solution)/shard_map/reduce_scatter | solution.py:214
  453.5 1.4 convolution_bitcast_fusion.2
  455.0 2.8 fusion.30
  460.8 1.4 multiply_reduce_fusion.3
  464.1 2.5 convolution_convert_fusion.7
  466.6 2.0 copy.171
  468.6 1.9 copy.170
  471.9 1.9 multiply_convert_fusion
  478.6 2.4 convolution_convert_fusion
  481.1 2.3 pad_maximum_fusion
  483.4 5.0 fusion.7
  489.5 4.5 fusion.6
  494.0 1.8 copy.179
  495.8 4.8 all-to-all-start.1
  503.2 11.8 %collective-permute-start.17 = (bf16[2,192,768]{2,1,0:T(8,128)(2,1)S(1)}, bf16[2,192,768]{2,1,0:T(8,128)(2,1)}, u32[]{:S(2)}, u32[]{:S(2)}) collective-permute-start(bf16[2,192,768]{2,1,0:T(8,128)(2,1)S(1)} %add_convert_fusion.2), channel_id=1, source_target_pairs={{0,2},{1,3},{2,0},{3,1},{4,6},{5,7},{6,4},{7,5},{8,10},{9,11},{10,... | collective-permute-start | bytes 1769480 | tf_op jit(solution)/shard_map/ppermute | solution.py:85
  515.0 8.2 %all-to-all-done.1 = bf16[2,768,192]{2,0,1:T(2,128)(2,1)S(1)} async-done(((bf16[2,768,192]{2,0,1:T(2,128)(2,1)}), bf16[2,768,192]{2,0,1:T(2,128)(2,1)S(1)}, u32[]{:S(2)}, u32[]{:S(2)}) %all-to-all-start.1) | async-done | bytes 589856 | tf_op jit(solution)/shard_map/all_to_all | solution.py:223
  524.4 2.0 collective-permute-start.12
  526.4 46.7 %collective-permute-done.17 = bf16[2,192,768]{2,1,0:T(8,128)(2,1)} collective-permute-done((bf16[2,192,768]{2,1,0:T(8,128)(2,1)S(1)}, bf16[2,192,768]{2,1,0:T(8,128)(2,1)}, u32[]{:S(2)}, u32[]{:S(2)}) %collective-permute-start.17) | collective-permute-done | bytes 589856 | tf_op jit(solution)/shard_map/ppermute | solution.py:85
  574.4 1.6 collective-permute-start.18
  576.2 13.5 %collective-permute-done.18 = bf16[2,192,768]{2,1,0:T(8,128)(2,1)S(1)} collective-permute-done((bf16[2,192,768]{2,1,0:T(8,128)(2,1)S(1)}, bf16[2,192,768]{2,1,0:T(8,128)(2,1)S(1)}, u32[]{:S(2)}, u32[]{:S(2)}) %collective-permute-start.18) | collective-permute-done | bytes 589856 | tf_op jit(solution)/shard_map/ppermute | solution.py:85
  589.9 3.1 collective-permute-start.19
  593.0 3.5 fusion.27
  596.6 11.4 %collective-permute-done.13 = bf16[2,48,3072]{2,1,0:T(8,128)(2,1)S(1)} collective-permute-done((bf16[2,48,3072]{2,1,0:T(8,128)(2,1)S(1)}, bf16[2,48,3072]{2,1,0:T(8,128)(2,1)S(1)}, u32[]{:S(2)}, u32[]{:S(2)}) %collective-permute-start.13) | collective-permute-done | bytes 589856 | tf_op jit(solution)/shard_map/ppermute | solution.py:85
  608.9 3.0 collective-permute-start.1
  613.0 3.5 collective-permute-done.1
  616.6 6.3 collective-permute-start.8
  623.7 2.9 collective-permute-start.15
  626.6 2.1 collective-permute-start.3
  630.1 2.0 collective-permute-start.9
  632.1 7.6 %collective-permute-done.15 = bf16[2,48,3072]{2,1,0:T(8,128)(2,1)S(1)} collective-permute-done((bf16[2,48,3072]{2,1,0:T(8,128)(2,1)S(1)}, bf16[2,48,3072]{2,1,0:T(8,128)(2,1)S(1)}, u32[]{:S(2)}, u32[]{:S(2)}) %collective-permute-start.15) | collective-permute-done | bytes 589856 | tf_op jit(solution)/shard_map/ppermute | solution.py:85
  641.0 4.4 collective-permute-done.4
  645.6 4.3 collective-permute-done.5
  651.1 3.4 collective-permute-done.6
  655.9 2.3 collective-permute-start.11
  660.3 4.1 collective-permute-done.11
  (186 shorter events, 47.8 us)
Async XLA Ops:
  7.2 89.1 %all-gather.3.cloned.1.call-start = ((), (), s32[]{:S(2)}) async-start(), calls=%async_computation.4 | async-start | bytes 5222400 | tf_op jit(solution)/shard_map/all_gather | solution.py:181
  9.7 252.9 %all-gather.5.cloned.1.call-start = ((), (), s32[]{:S(2)}) async-start(), calls=%async_computation.5 | async-start | bytes 13369344 | tf_op jit(solution)/shard_map/all_gather | solution.py:209
  15.4 84.0 %copy-start.26 = (f32[197]{0:T(256)}, f32[197]{0:T(256)S(1)}, u32[]{:S(2)}) copy-start(f32[197]{0:T(256)S(1)} %broadcast_multiply_fusion.5) | copy-start | bytes 2368
  16.6 82.8 %copy-start.29 = (f32[197]{0:T(256)}, f32[197]{0:T(256)S(1)}, u32[]{:S(2)}) copy-start(f32[197]{0:T(256)S(1)} %add_rsqrt_fusion.1) | copy-start | bytes 2368
  103.6 4.1 copy-start.9
  103.6 2.8 copy-start.22
  103.6 4.2 copy-start.21
  107.7 351.1 %copy-start.23 = (f32[197]{0:T(256)}, f32[197]{0:T(256)S(1)}, u32[]{:S(2)}) copy-start(f32[197]{0:T(256)S(1)} %get-tuple-element.86) | copy-start | bytes 2368
  107.8 351.0 %copy-start.24 = (f32[197]{0:T(256)}, f32[197]{0:T(256)S(1)}, u32[]{:S(2)}) copy-start(f32[197]{0:T(256)S(1)} %fusion.46) | copy-start | bytes 2368
  114.2 339.3 %reduce-scatter.3.cloned.1.call-start = ((), (), s32[]{:S(2)}) async-start(), calls=%async_computation.6 | async-start | bytes 13369344 | tf_op jit(solution)/shard_map/reduce_scatter | solution.py:214
  281.3 335.3 %reduce-scatter.5.cloned.1.call-start = ((), (), s32[]{:S(2)}) async-start(), calls=%async_computation.7 | async-start | bytes 5222400 | tf_op jit(solution)/shard_map/reduce_scatter | solution.py:251
  458.7 3.5 copy-start.11
  471.9 2.0 copy-start.8
  471.9 3.1 copy-start.6
  473.9 2.4 copy-start.4
  475.0 2.6 copy-start.1
  475.0 2.6 copy-start.10
  476.2 2.2 copy-start.27
  476.2 2.2 copy-start.28
  476.2 2.2 copy-start.30
  483.4 6.1 copy-start.31
  488.4 13.5 %collective-permute-start.16 = (bf16[2,192,768]{2,1,0:T(8,128)(2,1)S(1)}, bf16[2,192,768]{2,1,0:T(8,128)(2,1)}, u32[]{:S(2)}, u32[]{:S(2)}) collective-permute-start(bf16[2,192,768]{2,1,0:T(8,128)(2,1)S(1)} %fusion.7), channel_id=1, source_target_pairs={{0,1},{1,0},{2,3},{3,2},{4,5},{5,4},{6,7},{7,6},{8,9},{9,8},{10,11... | collective-permute-start | bytes 1769480 | tf_op jit(solution)/shard_map/ppermute | solution.py:85
  495.8 27.4 %all-to-all-start.1 = ((bf16[2,768,192]{2,0,1:T(2,128)(2,1)}), bf16[2,768,192]{2,0,1:T(2,128)(2,1)S(1)}, u32[]{:S(2)}, u32[]{:S(2)}) async-start(bf16[2,768,192]{2,0,1:T(2,128)(2,1)} %copy.179), calls=%async_computation.3 | async-start | bytes 1572864 | tf_op jit(solution)/shard_map/all_to_all | solution.py:223
  503.2 70.0 %collective-permute-start.17 = (bf16[2,192,768]{2,1,0:T(8,128)(2,1)S(1)}, bf16[2,192,768]{2,1,0:T(8,128)(2,1)}, u32[]{:S(2)}, u32[]{:S(2)}) collective-permute-start(bf16[2,192,768]{2,1,0:T(8,128)(2,1)S(1)} %add_convert_fusion.2), channel_id=1, source_target_pairs={{0,2},{1,3},{2,0},{3,1},{4,6},{5,7},{6,4},{7,5},{8,10},{9,11},{10,... | collective-permute-start | bytes 1769480 | tf_op jit(solution)/shard_map/ppermute | solution.py:85
  524.4 68.6 %copy-start.18 = (bf16[12,64,197]{2,1,0:T(8,128)(2,1)S(1)}, bf16[12,64,197]{2,1,0:T(8,128)(2,1)}, u32[]{:S(2)}) copy-start(bf16[12,64,197]{2,1,0:T(8,128)(2,1)} %convolution_convert_fusion.3) | copy-start | bytes 907780
  524.4 68.6 %copy-start.19 = (bf16[12,64,197]{2,1,0:T(8,128)(2,1)S(1)}, bf16[12,64,197]{2,1,0:T(8,128)(2,1)}, u32[]{:S(2)}) copy-start(bf16[12,64,197]{2,1,0:T(8,128)(2,1)} %fusion.8) | copy-start | bytes 907780
  524.4 68.6 %copy-start.20 = (bf16[12,64,197]{2,1,0:T(8,128)(2,1)S(1)}, bf16[12,64,197]{2,1,0:T(8,128)(2,1)}, u32[]{:S(2)}) copy-start(bf16[12,64,197]{2,1,0:T(8,128)(2,1)} %fusion.9) | copy-start | bytes 907780
  524.4 51.6 %collective-permute-start.12 = (bf16[2,48,3072]{2,1,0:T(8,128)(2,1)S(1)}, bf16[2,48,3072]{2,1,0:T(8,128)(2,1)S(1)}, u32[]{:S(2)}, u32[]{:S(2)}) collective-permute-start(bf16[2,48,3072]{2,1,0:T(8,128)(2,1)S(1)} %all_to_all.33), channel_id=1, source_target_pairs={{0,1},{1,0},{2,3},{3,2},{4,5},{5,4},{6,7},{7,6},{8,9},{9,8},{10,11... | collective-permute-start | bytes 1769480 | tf_op jit(solution)/shard_map/ppermute | solution.py:85
  574.4 15.3 %collective-permute-start.18 = (bf16[2,192,768]{2,1,0:T(8,128)(2,1)S(1)}, bf16[2,192,768]{2,1,0:T(8,128)(2,1)S(1)}, u32[]{:S(2)}, u32[]{:S(2)}) collective-permute-start(bf16[2,192,768]{2,1,0:T(8,128)(2,1)S(1)} %add_convert_fusion.1), channel_id=1, source_target_pairs={{0,4},{1,5},{2,6},{3,7},{4,0},{5,1},{6,2},{7,3},{8,12},{9,13},{10,... | collective-permute-start | bytes 1769480 | tf_op jit(solution)/shard_map/ppermute | solution.py:85
  576.1 32.0 %collective-permute-start.13 = (bf16[2,48,3072]{2,1,0:T(8,128)(2,1)S(1)}, bf16[2,48,3072]{2,1,0:T(8,128)(2,1)S(1)}, u32[]{:S(2)}, u32[]{:S(2)}) collective-permute-start(bf16[2,48,3072]{2,1,0:T(8,128)(2,1)S(1)} %add_convert_fusion.5), channel_id=1, source_target_pairs={{0,2},{1,3},{2,0},{3,1},{4,6},{5,7},{6,4},{7,5},{8,10},{9,11},{10,... | collective-permute-start | bytes 1769480 | tf_op jit(solution)/shard_map/ppermute | solution.py:85
  589.9 21.9 %collective-permute-start.19 = (bf16[2,192,768]{2,1,0:T(8,128)(2,1)S(1)}, bf16[2,192,768]{2,1,0:T(8,128)(2,1)S(1)}, u32[]{:S(2)}, u32[]{:S(2)}) collective-permute-start(bf16[2,192,768]{2,1,0:T(8,128)(2,1)S(1)} %add_convert_fusion), channel_id=1, source_target_pairs={{0,8},{1,9},{2,10},{3,11},{4,12},{5,13},{6,14},{7,15},{8,0},{9,1},... | collective-permute-start | bytes 1769480 | tf_op jit(solution)/shard_map/ppermute | solution.py:85
  596.5 12.3 %collective-permute-start = (f32[2,768]{1,0:T(2,128)S(1)}, f32[2,768]{1,0:T(2,128)S(1)}, u32[]{:S(2)}, u32[]{:S(2)}) collective-permute-start(f32[2,768]{1,0:T(2,128)S(1)} %pad_maximum_fusion.6), channel_id=1, source_target_pairs={{0,16},{16,0},{32,48},{48,32},{64,80},{80,64},{96,112},{112,96},{1... | collective-permute-start | bytes 18440 | tf_op jit(solution)/shard_map/ppermute | solution.py:85
  608.2 15.3 %collective-permute-start.14 = (bf16[2,48,3072]{2,1,0:T(8,128)(2,1)S(1)}, bf16[2,48,3072]{2,1,0:T(8,128)(2,1)S(1)}, u32[]{:S(2)}, u32[]{:S(2)}) collective-permute-start(bf16[2,48,3072]{2,1,0:T(8,128)(2,1)S(1)} %add_convert_fusion.4), channel_id=1, source_target_pairs={{0,4},{1,5},{2,6},{3,7},{4,0},{5,1},{6,2},{7,3},{8,12},{9,13},{10,... | collective-permute-start | bytes 1769480 | tf_op jit(solution)/shard_map/ppermute | solution.py:85
  608.9 7.6 %collective-permute-start.1 = (f32[2,768]{1,0:T(2,128)S(1)}, f32[2,768]{1,0:T(2,128)S(1)}, u32[]{:S(2)}, u32[]{:S(2)}) collective-permute-start(f32[2,768]{1,0:T(2,128)S(1)} %fusion.53), channel_id=1, source_target_pairs={{0,32},{16,48},{32,0},{48,16},{64,96},{80,112},{96,64},{112,80},{1... | collective-permute-start | bytes 18440 | tf_op jit(solution)/shard_map/ppermute | solution.py:85
  616.5 10.1 %collective-permute-start.2 = (f32[2,768]{1,0:T(2,128)S(1)}, f32[2,768]{1,0:T(2,128)S(1)}, u32[]{:S(2)}, u32[]{:S(2)}) collective-permute-start(f32[2,768]{1,0:T(2,128)S(1)} %fusion.77), channel_id=1, source_target_pairs={{0,64},{16,80},{32,96},{48,112},{64,0},{80,16},{96,32},{112,48},{1... | collective-permute-start | bytes 18440 | tf_op jit(solution)/shard_map/ppermute | solution.py:85
  616.6 12.4 %collective-permute-start.8 = (bf16[48,3104]{1,0:T(8,128)(2,1)}, bf16[48,3104]{1,0:T(8,128)(2,1)S(1)}, u32[]{:S(2)}, u32[]{:S(2)}) collective-permute-start(bf16[48,3104]{1,0:T(8,128)(2,1)} %reduce-scatter.5.cloned.1.call-done), channel_id=1, source_target_pairs={{0,1},{1,0},{2,3},{3,2},{4,5},{5,4},{6,7},{7,6},{8,9},{9,8},{10,11... | collective-permute-start | bytes 893960 | tf_op jit(solution)/shard_map/ppermute | solution.py:85
  623.7 26.2 %copy-start.2 = (f32[197,768]{1,0:T(8,128)S(1)}, f32[197,768]{1,0:T(8,128)}, u32[]{:S(2)}) copy-start(f32[197,768]{1,0:T(8,128)} %copy-done) | copy-start | bytes 1815556
  623.7 16.0 %collective-permute-start.15 = (bf16[2,48,3072]{2,1,0:T(8,128)(2,1)S(1)}, bf16[2,48,3072]{2,1,0:T(8,128)(2,1)S(1)}, u32[]{:S(2)}, u32[]{:S(2)}) collective-permute-start(bf16[2,48,3072]{2,1,0:T(8,128)(2,1)S(1)} %add_convert_fusion.3), channel_id=1, source_target_pairs={{0,8},{1,9},{2,10},{3,11},{4,12},{5,13},{6,14},{7,15},{8,0},{9,1},... | collective-permute-start | bytes 1769480 | tf_op jit(solution)/shard_map/ppermute | solution.py:85
  626.6 14.3 %collective-permute-start.3 = (f32[2,768]{1,0:T(2,128)S(1)}, f32[2,768]{1,0:T(2,128)S(1)}, u32[]{:S(2)}, u32[]{:S(2)}) collective-permute-start(f32[2,768]{1,0:T(2,128)S(1)} %add.113), channel_id=1, source_target_pairs={{0,128},{16,144},{32,160},{48,176},{64,192},{80,208},{96,224},{112... | collective-permute-start | bytes 18440 | tf_op jit(solution)/shard_map/ppermute | solution.py:85
  630.1 15.3 %collective-permute-start.9 = (bf16[48,3104]{1,0:T(8,128)(2,1)S(1)}, bf16[48,3104]{1,0:T(8,128)(2,1)S(1)}, u32[]{:S(2)}, u32[]{:S(2)}) collective-permute-start(bf16[48,3104]{1,0:T(8,128)(2,1)S(1)} %add_convert_fusion.8), channel_id=1, source_target_pairs={{0,2},{1,3},{2,0},{3,1},{4,6},{5,7},{6,4},{7,5},{8,10},{9,11},{10,... | collective-permute-start | bytes 893960 | tf_op jit(solution)/shard_map/ppermute | solution.py:85
  640.9 17.3 %copy-start.15 = (f32[197,2,128]{2,1,0:T(2,128)S(1)}, f32[197,2,128]{2,1,0:T(2,128)}, u32[]{:S(2)}) copy-start(f32[197,2,128]{2,1,0:T(2,128)} %copy-done.14) | copy-start | bytes 605188
  640.9 17.3 %copy-start.16 = (bf16[2,2,128,768]{3,2,1,0:T(8,128)(2,1)S(1)}, bf16[2,2,128,768]{3,2,1,0:T(8,128)(2,1)}, u32[]{:S(2)}) copy-start(bf16[2,2,128,768]{3,2,1,0:T(8,128)(2,1)} %reduce-scatter.3.cloned.1.call-done) | copy-start | bytes 2359300
  640.9 4.5 collective-permute-start.4
  645.4 4.5 collective-permute-start.5
  645.5 10.3 %collective-permute-start.10 = (bf16[48,3104]{1,0:T(8,128)(2,1)S(1)}, bf16[48,3104]{1,0:T(8,128)(2,1)S(1)}, u32[]{:S(2)}, u32[]{:S(2)}) collective-permute-start(bf16[48,3104]{1,0:T(8,128)(2,1)S(1)} %add_convert_fusion.7), channel_id=1, source_target_pairs={{0,4},{1,5},{2,6},{3,7},{4,0},{5,1},{6,2},{7,3},{8,12},{9,13},{10,... | collective-permute-start | bytes 893960 | tf_op jit(solution)/shard_map/ppermute | solution.py:85
  650.0 4.5 collective-permute-start.6
  654.4 5.3 collective-permute-start.7
  655.9 8.5 %collective-permute-start.11 = (bf16[48,3104]{1,0:T(8,128)(2,1)S(1)}, bf16[48,3104]{1,0:T(8,128)(2,1)S(1)}, u32[]{:S(2)}, u32[]{:S(2)}) collective-permute-start(bf16[48,3104]{1,0:T(8,128)(2,1)S(1)} %add_convert_fusion.6), channel_id=1, source_target_pairs={{0,8},{1,9},{2,10},{3,11},{4,12},{5,13},{6,14},{7,15},{8,0},{9,1},... | collective-permute-start | bytes 893960 | tf_op jit(solution)/shard_map/ppermute | solution.py:85
  (9 other events, 9.1 us)
Sparse Core Ops, SparseCore 0:
  11.2 85.0 all-gather.2
  114.3 148.2 all-gather.4
  281.4 172.0 reduce-scatter.2
  483.5 125.8 reduce-scatter.4

commit v8 on v6

--- a/solution.py
+++ b/solution.py
@@ -13,7 +13,7 @@
 
 
 EPS = 1e-06
-ROW_TILE = 512
+ROW_TILE = 256
 
 def expert_kernel(rows_ref, geout_ref, w_in_ref, w_out_ref, parts_ref, act_ref, gpre_ref):
     rows = rows_ref[...]
@@ -77,19 +77,19 @@
     return (grad_in, jnp.sum(grad_out * normed, axis=0))
 
 
-def butterfly_sum(value, axis, size, wire=None):
+def butterfly_sum(value, axis, size, wire=None, radix=2):
     step = 1
     while step < size:
-        radix = 4 if (size // step) % 4 == 0 else 2
+        width = radix if (size // step) % radix == 0 else 2
         sent = value if wire is None else value.astype(wire)
         got = [
             lax.ppermute(sent, axis, [(i, i ^ (shift * step)) for i in range(size)]).astype(jnp.float32)
-            for shift in range(1, radix)
+            for shift in range(1, width)
         ]
         value = sent.astype(jnp.float32) + got[0]
-        if radix == 4:
+        if width == 4:
             value = value + (got[1] + got[2])
-        step *= radix
+        step *= width
     return value
 
 
@@ -250,8 +250,8 @@
     grad_inputs = grad_attended + grad_norm1
     n_shard = lax.axis_size("shard")
     n_rep = lax.axis_size("rep")
-    gains = butterfly_sum(jnp.stack([gain1, gain2]), "shard", n_shard)
-    gains = butterfly_sum(gains, "rep", n_rep)
+    gains = butterfly_sum(jnp.stack([gain1, gain2]), "shard", n_shard, radix=4)
+    gains = butterfly_sum(gains, "rep", n_rep, radix=4)
     gain1_total, gain2_total = gains[0], gains[1]
     dense_local = lax.psum_scatter(
         jnp.concatenate(

time: 768 us -> 708 us (0.922)
  starting transfers between devices: 114 us -> 52.6 us
    ppermute x30 -> x24, starting transfers between devices: 109 us -> 46.2 us  [butterfly_sum(): lax.ppermute(sent, axis, [(i, i ^ shift * step) for i in range(size)])]
    reduce_scatter x1, waiting for transfers between devices: 172 us -> 157 us  [body(): lax.psum_scatter(parts, 'shard', scatter_dimension=2, tiled=True)]
    ppermute x30 -> x24, waiting for transfers between devices: 123 us -> 137 us  [butterfly_sum(): lax.ppermute(sent, axis, [(i, i ^ shift * step) for i in range(size)])]
    unnamed x62 -> x72, local copies, waits for them, and re-layouts: 14.7 us -> 15.4 us
  transfers between devices with their start and end apart: 35 -> 29, of which waited for: 17 -> 16; matrix products, arithmetic and copies ran while one was open for 7% -> 11% of each run, Pallas kernels for 0% -> 0%
where the time goes in v8:
time: 708 us; the launch traced here: 698 us
  waiting for transfers between devices  468 us (66%)
  starting transfers between devices  52.6 us (7%)
  local copies, waits for them, and re-layouts  37.8 us (5%)
  matrix products  37.7 us (5%)
  blocking collectives  37.3 us (5%)
  other arithmetic  26.5 us (4%)
  Pallas kernels  23.1 us (3%)
  between operations  14.7 us (2%)
    reduce_scatter x1, waiting for transfers between devices, body(): lax.psum_scatter(parts, 'shard', scatter_dimension=2, tiled=True)  157 us
    ppermute x24, waiting for transfers between devices, butterfly_sum(): lax.ppermute(sent, axis, [(i, i ^ shift * step) for i in range(size)])  137 us
    all_gather x1, waiting for transfers between devices, body(): lax.all_gather(jnp.stack([expert_rows, grad_eout]), 'shard', axis=2, tile...  94.7 us
    all_gather x1, waiting for transfers between devices, body(): lax.all_gather(jnp.concatenate([w_qkv, w_proj, w_router], axis=1), 'shard...  78.7 us
    ppermute x24, starting transfers between devices, butterfly_sum(): lax.ppermute(sent, axis, [(i, i ^ shift * step) for i in range(size)])  46.2 us
    all_to_all x1, blocking collectives, body(): w_in_cols = lax.all_to_all(w_expert_in, 'shard', 2, 1, tiled=True)  37.3 us
    pallas_call x1, Pallas kernels, expert_block(): pl.pallas_call(expert_kernel, grid=grid, in_specs=[pl.BlockSpec((None, No...  23.1 us
    unnamed x72, local copies, waits for them, and re-layouts  15.4 us
  transfers between devices with their start and end apart: 29, of which 16 were waited for; matrix products, arithmetic and copies ran while one was open for 11% of the time, Pallas kernels for 0%

profile of v8, /device:TPU:8, one launch (start us, length us, event | category | flops | bytes accessed | tf_op | source)
XLA Modules:
  0.0 697.7 jit_solution(7792979079463342722)
XLA Ops:
  8.0 1.7 pad_maximum_fusion.5
  17.5 78.7 %all-gather.3.cloned.1.call-done = bf16[768,3104]{1,0:T(8,128)(2,1)} async-done(((bf16[48,3104]{1,0:T(8,128)(2,1)}), bf16[768,3104]{1,0:T(8,128)(2,1)}) %all-gather.3.cloned.1.call-update) | async-done | bytes 4767760 | tf_op jit(solution)/shard_map/all_gather | solution.py:186
  96.3 3.1 convolution_convert_fusion.1
  103.6 2.0 fusion.56
  108.6 2.4 multiply_reduce_fusion.2
  111.7 1.5 fusion.13
  114.2 4.3 copy.164
  118.5 4.1 reshape.249
  122.6 37.3 %all_to_all.36 = bf16[16,2,9216]{2,1,0:T(2,128)(2,1)} all-to-all(bf16[16,2,9216]{2,1,0:T(2,128)(2,1)} %reshape.249), channel_id=1, replica_groups=mesh['shard'=16,'rep'=16] {'shard'}, dimensions={0} | all-to-all | bytes 1179648 | tf_op jit(solution)/shard_map/all_to_all | solution.py:211
  159.9 3.3 reshape.250
  163.2 4.7 copy.165
  167.9 94.7 %all-gather.5.cloned.1.call-done.rows_ref.geout_ref = bf16[2,2,2048,768]{3,2,1,0:T(8,128)(2,1)} async-done(((bf16[2,2,128,768]{3,2,1,0:T(8,128)(2,1)}), bf16[2,2,2048,768]{3,2,1,0:T(8,128)(2,1)}) %all-gather.5.cloned.1.call-update) | async-done | bytes 12582928 | tf_op jit(solution)/shard_map/all_gather | solution.py:214
  262.6 23.1 %shard_map.178 = (bf16[2,2,2048,768]{3,2,1,0:T(8,128)(2,1)}, bf16[2,2048,192]{2,1,0:T(8,128)(2,1)}, bf16[2,2048,192]{2,1,0:T(8,128)(2,1)}) custom-call(bf16[2,2,2048,768]{3,2,1,0:T(8,128)(2,1)} %all-gather.5.cloned.1.call-done.rows_ref.geout_ref, bf16[2,2,2048,768]{3,2,1,0:T(8,128)(2,1)} %all-gather.5.cloned.1.call-done.rows_ref.geout_ref, ...), custom_call_target="tpu_custom_call" | custom-call | tf_op jit(solution)/shard_map/pallas_call | solution.py:41
  285.8 5.7 fusion.6
  291.4 3.0 copy.179
  294.4 6.0 all-to-all-start.1
  300.8 157.2 %reduce-scatter.3.cloned.1.call-done = bf16[2,2,128,768]{3,2,1,0:T(8,128)(2,1)} async-done(((bf16[2,2,2048,768]{3,2,1,0:T(8,128)(2,1)}), bf16[2,2,128,768]{3,2,1,0:T(8,128)(2,1)}) %reduce-scatter.3.cloned.1.call-update) | async-done | bytes 786448 | tf_op jit(solution)/shard_map/reduce_scatter | solution.py:219
  459.4 2.8 fusion.30
  468.5 2.5 convolution_convert_fusion.7
  471.1 2.0 copy.171
  473.1 1.9 copy.170
  476.3 2.0 multiply_convert_fusion
  483.1 2.4 convolution_convert_fusion
  485.6 2.3 pad_maximum_fusion
  487.9 4.9 fusion.7
  497.3 18.2 %collective-permute-done.20 = bf16[2,192,768]{2,1,0:T(8,128)(2,1)} collective-permute-done((bf16[2,192,768]{2,1,0:T(8,128)(2,1)S(1)}, bf16[2,192,768]{2,1,0:T(8,128)(2,1)}, u32[]{:S(2)}, u32[]{:S(2)}) %collective-permute-start.20) | collective-permute-done | bytes 589856 | tf_op jit(solution)/shard_map/ppermute | solution.py:86
  516.9 8.8 %collective-permute-done.16 = bf16[2,48,3072]{2,1,0:T(8,128)(2,1)S(1)} collective-permute-done((bf16[2,48,3072]{2,1,0:T(8,128)(2,1)S(1)}, bf16[2,48,3072]{2,1,0:T(8,128)(2,1)S(1)}, u32[]{:S(2)}, u32[]{:S(2)}) %collective-permute-start.16) | collective-permute-done | bytes 589856 | tf_op jit(solution)/shard_map/ppermute | solution.py:86
  525.9 3.2 collective-permute-start.17
  529.0 53.9 %collective-permute-done.21 = bf16[2,192,768]{2,1,0:T(8,128)(2,1)S(1)} collective-permute-done((bf16[2,192,768]{2,1,0:T(8,128)(2,1)S(1)}, bf16[2,192,768]{2,1,0:T(8,128)(2,1)S(1)}, u32[]{:S(2)}, u32[]{:S(2)}) %collective-permute-start.21) | collective-permute-done | bytes 589856 | tf_op jit(solution)/shard_map/ppermute | solution.py:86
  583.1 11.4 %collective-permute-start.22 = (bf16[2,192,768]{2,1,0:T(8,128)(2,1)S(1)}, bf16[2,192,768]{2,1,0:T(8,128)(2,1)S(1)}, u32[]{:S(2)}, u32[]{:S(2)}) collective-permute-start(bf16[2,192,768]{2,1,0:T(8,128)(2,1)S(1)} %add_convert_fusion.1), channel_id=1, source_target_pairs={{0,4},{1,5},{2,6},{3,7},{4,0},{5,1},{6,2},{7,3},{8,12},{9,13},{10,... | collective-permute-start | bytes 1769480 | tf_op jit(solution)/shard_map/ppermute | solution.py:86
  595.4 14.0 %collective-permute-done.22 = bf16[2,192,768]{2,1,0:T(8,128)(2,1)S(1)} collective-permute-done((bf16[2,192,768]{2,1,0:T(8,128)(2,1)S(1)}, bf16[2,192,768]{2,1,0:T(8,128)(2,1)S(1)}, u32[]{:S(2)}, u32[]{:S(2)}) %collective-permute-start.22) | collective-permute-done | bytes 589856 | tf_op jit(solution)/shard_map/ppermute | solution.py:86
  609.5 3.0 collective-permute-start.23
  612.5 6.2 collective-permute-done.18
  618.9 3.0 collective-permute-start.19
  621.9 5.2 collective-permute-done.23
  628.2 5.2 collective-permute-done.19
  634.6 1.5 fusion.27
  637.1 5.0 collective-permute-start.2
  642.1 1.8 collective-permute-done.1
  644.0 3.4 collective-permute-start.3
  649.0 2.9 collective-permute-done.12
  655.6 1.8 collective-permute-start.6
  657.4 2.6 collective-permute-start.8
  660.1 9.5 %collective-permute-done.13 = bf16[48,3104]{1,0:T(8,128)(2,1)S(1)} collective-permute-done((bf16[48,3104]{1,0:T(8,128)(2,1)S(1)}, bf16[48,3104]{1,0:T(8,128)(2,1)S(1)}, u32[]{:S(2)}, u32[]{:S(2)}) %collective-permute-start.13) | collective-permute-done | bytes 298016 | tf_op jit(solution)/shard_map/ppermute | solution.py:86
  671.2 1.9 collective-permute-start.10
  673.1 2.6 collective-permute-start.11
  675.8 3.3 collective-permute-done.14
  680.7 8.1 %collective-permute-done.15 = bf16[48,3104]{1,0:T(8,128)(2,1)S(1)} collective-permute-done((bf16[48,3104]{1,0:T(8,128)(2,1)S(1)}, bf16[48,3104]{1,0:T(8,128)(2,1)S(1)}, u32[]{:S(2)}, u32[]{:S(2)}) %collective-permute-start.15) | collective-permute-done | bytes 298016 | tf_op jit(solution)/shard_map/ppermute | solution.py:86
  (193 shorter events, 52.8 us)
Async XLA Ops:
  7.2 89.1 %all-gather.3.cloned.1.call-start = ((), (), s32[]{:S(2)}) async-start(), calls=%async_computation.4 | async-start | bytes 5222400 | tf_op jit(solution)/shard_map/all_gather | solution.py:186
  9.7 252.9 %all-gather.5.cloned.1.call-start = ((), (), s32[]{:S(2)}) async-start(), calls=%async_computation.5 | async-start | bytes 13369344 | tf_op jit(solution)/shard_map/all_gather | solution.py:214
  15.4 84.0 %copy-start.26 = (f32[197]{0:T(256)}, f32[197]{0:T(256)S(1)}, u32[]{:S(2)}) copy-start(f32[197]{0:T(256)S(1)} %broadcast_multiply_fusion.5) | copy-start | bytes 2368
  16.6 82.8 %copy-start.29 = (f32[197]{0:T(256)}, f32[197]{0:T(256)S(1)}, u32[]{:S(2)}) copy-start(f32[197]{0:T(256)S(1)} %add_rsqrt_fusion.1) | copy-start | bytes 2368
  103.6 4.1 copy-start.9
  103.6 2.8 copy-start.22
  103.6 4.2 copy-start.21
  107.7 355.5 %copy-start.23 = (f32[197]{0:T(256)}, f32[197]{0:T(256)S(1)}, u32[]{:S(2)}) copy-start(f32[197]{0:T(256)S(1)} %get-tuple-element.86) | copy-start | bytes 2368
  107.8 355.5 %copy-start.24 = (f32[197]{0:T(256)}, f32[197]{0:T(256)S(1)}, u32[]{:S(2)}) copy-start(f32[197]{0:T(256)S(1)} %fusion.46) | copy-start | bytes 2368
  114.2 343.8 %reduce-scatter.3.cloned.1.call-start = ((), (), s32[]{:S(2)}) async-start(), calls=%async_computation.6 | async-start | bytes 13369344 | tf_op jit(solution)/shard_map/reduce_scatter | solution.py:219
  294.4 199.4 %all-to-all-start.1 = ((bf16[2,768,192]{2,0,1:T(2,128)(2,1)}), bf16[2,768,192]{2,0,1:T(2,128)(2,1)}, u32[]{:S(2)}, u32[]{:S(2)}) async-start(bf16[2,768,192]{2,0,1:T(2,128)(2,1)} %copy.179), calls=%async_computation.3 | async-start | bytes 1572864 | tf_op jit(solution)/shard_map/all_to_all | solution.py:228
  300.4 341.6 %reduce-scatter.5.cloned.1.call-start = ((), (), s32[]{:S(2)}) async-start(), calls=%async_computation.7 | async-start | bytes 5222400 | tf_op jit(solution)/shard_map/reduce_scatter | solution.py:256
  463.2 3.5 copy-start.11
  476.3 3.1 copy-start.6
  479.4 2.6 copy-start.1
  479.4 2.6 copy-start.10
  492.8 22.8 %collective-permute-start.20 = (bf16[2,192,768]{2,1,0:T(8,128)(2,1)S(1)}, bf16[2,192,768]{2,1,0:T(8,128)(2,1)}, u32[]{:S(2)}, u32[]{:S(2)}) collective-permute-start(bf16[2,192,768]{2,1,0:T(8,128)(2,1)S(1)} %fusion.7), channel_id=1, source_target_pairs={{0,1},{1,0},{2,3},{3,2},{4,5},{5,4},{6,7},{7,6},{8,9},{9,8},{10,11... | collective-permute-start | bytes 1769480 | tf_op jit(solution)/shard_map/ppermute | solution.py:86
  496.2 29.5 %collective-permute-start.16 = (bf16[2,48,3072]{2,1,0:T(8,128)(2,1)S(1)}, bf16[2,48,3072]{2,1,0:T(8,128)(2,1)S(1)}, u32[]{:S(2)}, u32[]{:S(2)}) collective-permute-start(bf16[2,48,3072]{2,1,0:T(8,128)(2,1)S(1)} %all_to_all.33), channel_id=1, source_target_pairs={{0,1},{1,0},{2,3},{3,2},{4,5},{5,4},{6,7},{7,6},{8,9},{9,8},{10,11... | collective-permute-start | bytes 1769480 | tf_op jit(solution)/shard_map/ppermute | solution.py:86
  516.8 66.2 %collective-permute-start.21 = (bf16[2,192,768]{2,1,0:T(8,128)(2,1)S(1)}, bf16[2,192,768]{2,1,0:T(8,128)(2,1)S(1)}, u32[]{:S(2)}, u32[]{:S(2)}) collective-permute-start(bf16[2,192,768]{2,1,0:T(8,128)(2,1)S(1)} %add_convert_fusion.2), channel_id=1, source_target_pairs={{0,2},{1,3},{2,0},{3,1},{4,6},{5,7},{6,4},{7,5},{8,10},{9,11},{10,... | collective-permute-start | bytes 1769480 | tf_op jit(solution)/shard_map/ppermute | solution.py:86
  525.7 108.8 %slice-start = ((s8[4915200]{0:T(1024)(128)(4,1)}), s8[4194304]{0:T(1024)(128)(4,1)S(1)}, s32[]{:S(2)}) async-start(s8[4915200]{0:T(1024)(128)(4,1)} %bitcast.126), calls=%async_computation.8 | async-start | bytes 8388608
  525.9 68.6 %collective-permute-start.17 = (bf16[2,48,3072]{2,1,0:T(8,128)(2,1)S(1)}, bf16[2,48,3072]{2,1,0:T(8,128)(2,1)S(1)}, u32[]{:S(2)}, u32[]{:S(2)}) collective-permute-start(bf16[2,48,3072]{2,1,0:T(8,128)(2,1)S(1)} %add_convert_fusion.5), channel_id=1, source_target_pairs={{0,2},{1,3},{2,0},{3,1},{4,6},{5,7},{6,4},{7,5},{8,10},{9,11},{10,... | collective-permute-start | bytes 1769480 | tf_op jit(solution)/shard_map/ppermute | solution.py:86
  583.1 26.2 %collective-permute-start.22 = (bf16[2,192,768]{2,1,0:T(8,128)(2,1)S(1)}, bf16[2,192,768]{2,1,0:T(8,128)(2,1)S(1)}, u32[]{:S(2)}, u32[]{:S(2)}) collective-permute-start(bf16[2,192,768]{2,1,0:T(8,128)(2,1)S(1)} %add_convert_fusion.1), channel_id=1, source_target_pairs={{0,4},{1,5},{2,6},{3,7},{4,0},{5,1},{6,2},{7,3},{8,12},{9,13},{10,... | collective-permute-start | bytes 1769480 | tf_op jit(solution)/shard_map/ppermute | solution.py:86
  594.6 39.9 %slice-start.1 = ((s8[4915200]{0:T(1024)(128)(4,1)}), s8[720896]{0:T(1024)(128)(4,1)S(1)}, s32[]{:S(2)}) async-start(s8[4915200]{0:T(1024)(128)(4,1)} %bitcast.126), calls=%async_computation.9 | async-start | bytes 1441792
  594.6 24.0 %collective-permute-start.18 = (bf16[2,48,3072]{2,1,0:T(8,128)(2,1)S(1)}, bf16[2,48,3072]{2,1,0:T(8,128)(2,1)S(1)}, u32[]{:S(2)}, u32[]{:S(2)}) collective-permute-start(bf16[2,48,3072]{2,1,0:T(8,128)(2,1)S(1)} %add_convert_fusion.4), channel_id=1, source_target_pairs={{0,4},{1,5},{2,6},{3,7},{4,0},{5,1},{6,2},{7,3},{8,12},{9,13},{10,... | collective-permute-start | bytes 1769480 | tf_op jit(solution)/shard_map/ppermute | solution.py:86
  609.5 17.6 %collective-permute-start.23 = (bf16[2,192,768]{2,1,0:T(8,128)(2,1)S(1)}, bf16[2,192,768]{2,1,0:T(8,128)(2,1)S(1)}, u32[]{:S(2)}, u32[]{:S(2)}) collective-permute-start(bf16[2,192,768]{2,1,0:T(8,128)(2,1)S(1)} %add_convert_fusion), channel_id=1, source_target_pairs={{0,8},{1,9},{2,10},{3,11},{4,12},{5,13},{6,14},{7,15},{8,0},{9,1},... | collective-permute-start | bytes 1769480 | tf_op jit(solution)/shard_map/ppermute | solution.py:86
  618.8 15.7 %copy-start.18 = (bf16[12,64,197]{2,1,0:T(8,128)(2,1)S(1)}, bf16[12,64,197]{2,1,0:T(8,128)(2,1)}, u32[]{:S(2)}) copy-start(bf16[12,64,197]{2,1,0:T(8,128)(2,1)} %convolution_convert_fusion.3) | copy-start | bytes 907780
  618.8 15.7 %copy-start.19 = (bf16[12,64,197]{2,1,0:T(8,128)(2,1)S(1)}, bf16[12,64,197]{2,1,0:T(8,128)(2,1)}, u32[]{:S(2)}) copy-start(bf16[12,64,197]{2,1,0:T(8,128)(2,1)} %fusion.8) | copy-start | bytes 907780
  618.9 15.7 %copy-start.20 = (bf16[12,64,197]{2,1,0:T(8,128)(2,1)S(1)}, bf16[12,64,197]{2,1,0:T(8,128)(2,1)}, u32[]{:S(2)}) copy-start(bf16[12,64,197]{2,1,0:T(8,128)(2,1)} %fusion.9) | copy-start | bytes 907780
  618.9 14.5 %collective-permute-start.19 = (bf16[2,48,3072]{2,1,0:T(8,128)(2,1)S(1)}, bf16[2,48,3072]{2,1,0:T(8,128)(2,1)S(1)}, u32[]{:S(2)}, u32[]{:S(2)}) collective-permute-start(bf16[2,48,3072]{2,1,0:T(8,128)(2,1)S(1)} %add_convert_fusion.3), channel_id=1, source_target_pairs={{0,8},{1,9},{2,10},{3,11},{4,12},{5,13},{6,14},{7,15},{8,0},{9,1},... | collective-permute-start | bytes 1769480 | tf_op jit(solution)/shard_map/ppermute | solution.py:86
  634.6 19.9 %copy-start.2 = (f32[197,768]{1,0:T(8,128)S(1)}, f32[197,768]{1,0:T(8,128)}, u32[]{:S(2)}) copy-start(f32[197,768]{1,0:T(8,128)} %copy-done) | copy-start | bytes 1815556
  636.1 33.9 %copy-start.15 = (f32[197,2,128]{2,1,0:T(2,128)S(1)}, f32[197,2,128]{2,1,0:T(2,128)}, u32[]{:S(2)}) copy-start(f32[197,2,128]{2,1,0:T(2,128)} %copy-done.14) | copy-start | bytes 605188
  636.1 33.9 %copy-start.16 = (bf16[2,2,128,768]{3,2,1,0:T(8,128)(2,1)S(1)}, bf16[2,2,128,768]{3,2,1,0:T(8,128)(2,1)}, u32[]{:S(2)}) copy-start(bf16[2,2,128,768]{3,2,1,0:T(8,128)(2,1)} %reduce-scatter.3.cloned.1.call-done) | copy-start | bytes 2359300
  636.2 5.9 collective-permute-start
  636.3 7.6 %collective-permute-start.1 = (f32[2,768]{1,0:T(2,128)S(1)}, f32[2,768]{1,0:T(2,128)S(1)}, u32[]{:S(2)}, u32[]{:S(2)}) collective-permute-start(f32[2,768]{1,0:T(2,128)S(1)} %pad_maximum_fusion.6), channel_id=1, source_target_pairs={{0,32},{16,48},{32,0},{48,16},{64,96},{80,112},{96,64},{112,80},{1... | collective-permute-start | bytes 18440 | tf_op jit(solution)/shard_map/ppermute | solution.py:86
  637.1 7.0 collective-permute-start.2
  642.1 9.9 %collective-permute-start.12 = (bf16[48,3104]{1,0:T(8,128)(2,1)}, bf16[48,3104]{1,0:T(8,128)(2,1)S(1)}, u32[]{:S(2)}, u32[]{:S(2)}) collective-permute-start(bf16[48,3104]{1,0:T(8,128)(2,1)} %reduce-scatter.5.cloned.1.call-done), channel_id=1, source_target_pairs={{0,1},{1,0},{2,3},{3,2},{4,5},{5,4},{6,7},{7,6},{8,9},{9,8},{10,11... | collective-permute-start | bytes 893960 | tf_op jit(solution)/shard_map/ppermute | solution.py:86
  644.0 11.5 %collective-permute-start.3 = (f32[2,768]{1,0:T(2,128)S(1)}, f32[2,768]{1,0:T(2,128)S(1)}, u32[]{:S(2)}, u32[]{:S(2)}) collective-permute-start(f32[2,768]{1,0:T(2,128)S(1)} %add_add_fusion.3), channel_id=1, source_target_pairs={{0,64},{16,80},{32,96},{48,112},{64,0},{80,16},{96,32},{112,48},{1... | collective-permute-start | bytes 18440 | tf_op jit(solution)/shard_map/ppermute | solution.py:86
  647.5 8.1 %collective-permute-start.4 = (f32[2,768]{1,0:T(2,128)S(1)}, f32[2,768]{1,0:T(2,128)S(1)}, u32[]{:S(2)}, u32[]{:S(2)}) collective-permute-start(f32[2,768]{1,0:T(2,128)S(1)} %add_add_fusion.3), channel_id=1, source_target_pairs={{0,128},{16,144},{32,160},{48,176},{64,192},{80,208},{96,224},{112... | collective-permute-start | bytes 18440 | tf_op jit(solution)/shard_map/ppermute | solution.py:86
  648.3 7.3 %collective-permute-start.5 = (f32[2,768]{1,0:T(2,128)S(1)}, f32[2,768]{1,0:T(2,128)S(1)}, u32[]{:S(2)}, u32[]{:S(2)}) collective-permute-start(f32[2,768]{1,0:T(2,128)S(1)} %add_add_fusion.3), channel_id=1, source_target_pairs={{0,192},{16,208},{32,224},{48,240},{64,128},{80,144},{96,160},{112... | collective-permute-start | bytes 18440 | tf_op jit(solution)/shard_map/ppermute | solution.py:86
  653.0 16.6 %collective-permute-start.13 = (bf16[48,3104]{1,0:T(8,128)(2,1)S(1)}, bf16[48,3104]{1,0:T(8,128)(2,1)S(1)}, u32[]{:S(2)}, u32[]{:S(2)}) collective-permute-start(bf16[48,3104]{1,0:T(8,128)(2,1)S(1)} %add_convert_fusion.8), channel_id=1, source_target_pairs={{0,2},{1,3},{2,0},{3,1},{4,6},{5,7},{6,4},{7,5},{8,10},{9,11},{10,... | collective-permute-start | bytes 893960 | tf_op jit(solution)/shard_map/ppermute | solution.py:86
  655.6 15.6 %collective-permute-start.6 = (f32[2,768]{1,0:T(2,128)S(1)}, f32[2,768]{1,0:T(2,128)S(1)}, u32[]{:S(2)}, u32[]{:S(2)}) collective-permute-start(f32[2,768]{1,0:T(2,128)S(1)} %add_add_fusion.2), channel_id=1, source_target_pairs={{0,1},{1,0},{2,3},{3,2},{4,5},{5,4},{6,7},{7,6},{8,9},{9,8},{10,11... | collective-permute-start | bytes 18440 | tf_op jit(solution)/shard_map/ppermute | solution.py:86
  657.4 13.8 %collective-permute-start.7 = (f32[2,768]{1,0:T(2,128)S(1)}, f32[2,768]{1,0:T(2,128)S(1)}, u32[]{:S(2)}, u32[]{:S(2)}) collective-permute-start(f32[2,768]{1,0:T(2,128)S(1)} %add_add_fusion.2), channel_id=1, source_target_pairs={{0,2},{1,3},{2,0},{3,1},{4,6},{5,7},{6,4},{7,5},{8,10},{9,11},{10,... | collective-permute-start | bytes 18440 | tf_op jit(solution)/shard_map/ppermute | solution.py:86
  657.4 13.8 %collective-permute-start.8 = (f32[2,768]{1,0:T(2,128)S(1)}, f32[2,768]{1,0:T(2,128)S(1)}, u32[]{:S(2)}, u32[]{:S(2)}) collective-permute-start(f32[2,768]{1,0:T(2,128)S(1)} %add_add_fusion.2), channel_id=1, source_target_pairs={{0,3},{1,2},{2,1},{3,0},{4,7},{5,6},{6,5},{7,4},{8,11},{9,10},{10,... | collective-permute-start | bytes 18440 | tf_op jit(solution)/shard_map/ppermute | solution.py:86
  669.7 9.3 %collective-permute-start.14 = (bf16[48,3104]{1,0:T(8,128)(2,1)S(1)}, bf16[48,3104]{1,0:T(8,128)(2,1)S(1)}, u32[]{:S(2)}, u32[]{:S(2)}) collective-permute-start(bf16[48,3104]{1,0:T(8,128)(2,1)S(1)} %add_convert_fusion.7), channel_id=1, source_target_pairs={{0,4},{1,5},{2,6},{3,7},{4,0},{5,1},{6,2},{7,3},{8,12},{9,13},{10,... | collective-permute-start | bytes 893960 | tf_op jit(solution)/shard_map/ppermute | solution.py:86
  671.2 8.8 %collective-permute-start.10 = (f32[2,768]{1,0:T(2,128)S(1)}, f32[2,768]{1,0:T(2,128)S(1)}, u32[]{:S(2)}, u32[]{:S(2)}) collective-permute-start(f32[2,768]{1,0:T(2,128)S(1)} %add_add_fusion.1), channel_id=1, source_target_pairs={{0,8},{1,9},{2,10},{3,11},{4,12},{5,13},{6,14},{7,15},{8,0},{9,1},... | collective-permute-start | bytes 18440 | tf_op jit(solution)/shard_map/ppermute | solution.py:86
  673.1 6.9 collective-permute-start.11
  675.8 4.3 collective-permute-start.9
  679.1 9.7 %collective-permute-start.15 = (bf16[48,3104]{1,0:T(8,128)(2,1)S(1)}, bf16[48,3104]{1,0:T(8,128)(2,1)S(1)}, u32[]{:S(2)}, u32[]{:S(2)}) collective-permute-start(bf16[48,3104]{1,0:T(8,128)(2,1)S(1)} %add_convert_fusion.6), channel_id=1, source_target_pairs={{0,8},{1,9},{2,10},{3,11},{4,12},{5,13},{6,14},{7,15},{8,0},{9,1},... | collective-permute-start | bytes 893960 | tf_op jit(solution)/shard_map/ppermute | solution.py:86
  (14 other events, 20.0 us)
Sparse Core Ops, SparseCore 0:
  11.2 85.0 all-gather.2
  114.3 148.2 all-gather.4
  285.9 172.0 reduce-scatter.2
  488.0 117.5 reduce-scatter.4

commit v9 on v5

--- a/solution.py
+++ b/solution.py
@@ -205,7 +205,13 @@
     ).astype(jnp.bfloat16)
     w_in_cols = lax.all_to_all(w_expert_in, "shard", 2, 1, tiled=True)
     grad = cotangent.astype(jnp.float32)
-    grad_eout = jnp.einsum("rec,rd->ecd", combine, grad, precision=high).astype(jnp.bfloat16)
+    combine_hi = combine.astype(jnp.bfloat16)
+    combine_lo = (combine - combine_hi.astype(jnp.float32)).astype(jnp.bfloat16)
+    grad_bf = cotangent
+    grad_eout = (
+        jnp.einsum("rec,rd->ecd", combine_hi, grad_bf, preferred_element_type=jnp.float32)
+        + jnp.einsum("rec,rd->ecd", combine_lo, grad_bf, preferred_element_type=jnp.float32)
+    ).astype(jnp.bfloat16)
     gathered = lax.all_gather(
         jnp.stack([expert_rows, grad_eout]), "shard", axis=2, tiled=True
     )
@@ -213,10 +219,11 @@
     parts, activated, grad_pre = expert_block(gathered, w_in_cols, w_expert_out)
     scattered = lax.psum_scatter(parts, "shard", scatter_dimension=2, tiled=True)
     expert_out, grad_rows = scattered[0], scattered[1]
-    eout_float = expert_out.astype(jnp.float32)
-    moe = jnp.einsum("rec,ecd->rd", combine, eout_float, precision=high)
+    moe = jnp.einsum(
+        "rec,ecd->rd", combine_hi, expert_out, preferred_element_type=jnp.float32
+    ) + jnp.einsum("rec,ecd->rd", combine_lo, expert_out, preferred_element_type=jnp.float32)
     outputs = (attended + moe).astype(jnp.bfloat16)
-    matched = jnp.einsum("rd,ecd->rec", grad, eout_float, precision=high)
+    matched = jnp.einsum("rd,ecd->rec", grad_bf, expert_out, preferred_element_type=jnp.float32)
     grad_gate = jnp.sum(masks * matched[:, None, :, :], axis=(2, 3))
     back_qkv, back_proj, back_router = (full_qkv, full_proj, full_router)
     gin_cols = jnp.einsum("erd,erh->edh", rows_all, grad_pre, preferred_element_type=jnp.float32)

time: 680 us -> 704 us (1.035)
  waiting for transfers between devices: 462 us -> 491 us
    ppermute x20, waiting for transfers between devices: 98.2 us -> 129 us  [butterfly_sum(): other = lax.ppermute(sent, axis, pairs)]
    unnamed x70 -> x74, local copies, waits for them, and re-layouts: 15.4 us -> 15.1 us
where the time goes in v9:
time: 704 us; the launch traced here: 701 us
  waiting for transfers between devices  491 us (70%)
  matrix products  39.6 us (6%)
  blocking collectives  37.3 us (5%)
  local copies, waits for them, and re-layouts  34.5 us (5%)
  starting transfers between devices  34.3 us (5%)
  other arithmetic  26.8 us (4%)
  Pallas kernels  23.1 us (3%)
  between operations  14.5 us (2%)
    reduce_scatter x1, waiting for transfers between devices, body(): lax.psum_scatter(parts, 'shard', scatter_dimension=2, tiled=True)  172 us
    ppermute x20, waiting for transfers between devices, butterfly_sum(): other = lax.ppermute(sent, axis, pairs)  129 us
    all_gather x1, waiting for transfers between devices, body(): lax.all_gather(jnp.stack([expert_rows, grad_eout]), 'shard', axis=2, tile...  94.7 us
    all_gather x1, waiting for transfers between devices, body(): lax.all_gather(jnp.concatenate([w_qkv, w_proj, w_router], axis=1), 'shard...  78.8 us
    all_to_all x1, blocking collectives, body(): w_in_cols = lax.all_to_all(w_expert_in, 'shard', 2, 1, tiled=True)  37.3 us
    ppermute x20, starting transfers between devices, butterfly_sum(): other = lax.ppermute(sent, axis, pairs)  29.4 us
    pallas_call x1, Pallas kernels, expert_block(): pl.pallas_call(expert_kernel, grid=grid, in_specs=[pl.BlockSpec((None, No...  23.1 us
    all_to_all x1, waiting for transfers between devices, body(): lax.all_to_all(gin_cols.astype(jnp.bfloat16), 'shard', 1, 2, tiled=True)  17.2 us
  transfers between devices with their start and end apart: 25, of which 17 were waited for; matrix products, arithmetic and copies ran while one was open for 7% of the time, Pallas kernels for 0%

profile of v9, /device:TPU:8, one launch (start us, length us, event | category | flops | bytes accessed | tf_op | source)
XLA Modules:
  0.0 701.2 jit_solution(14962946475595494844)
XLA Ops:
  8.0 1.7 pad_maximum_fusion.5
  17.5 78.8 %all-gather.3.cloned.1.call-done = bf16[768,3104]{1,0:T(8,128)(2,1)} async-done(((bf16[48,3104]{1,0:T(8,128)(2,1)}), bf16[768,3104]{1,0:T(8,128)(2,1)}) %all-gather.3.cloned.1.call-update) | async-done | bytes 4767760 | tf_op jit(solution)/shard_map/all_gather | solution.py:181
  96.3 3.1 convolution_convert_fusion.1
  103.6 2.0 fusion.63
  108.0 2.4 multiply_reduce_fusion.2
  113.5 4.3 copy.167
  117.8 4.1 reshape.250
  122.0 37.3 %all_to_all.36 = bf16[16,2,9216]{2,1,0:T(2,128)(2,1)} all-to-all(bf16[16,2,9216]{2,1,0:T(2,128)(2,1)} %reshape.250), channel_id=1, replica_groups=mesh['shard'=16,'rep'=16] {'shard'}, dimensions={0} | all-to-all | bytes 1179648 | tf_op jit(solution)/shard_map/all_to_all | solution.py:206
  159.2 3.3 reshape.251
  162.6 4.7 copy.168
  167.3 94.7 %all-gather.5.cloned.1.call-done.rows_ref.geout_ref = bf16[2,2,2048,768]{3,2,1,0:T(8,128)(2,1)} async-done(((bf16[2,2,128,768]{3,2,1,0:T(8,128)(2,1)}), bf16[2,2,2048,768]{3,2,1,0:T(8,128)(2,1)}) %all-gather.5.cloned.1.call-update) | async-done | bytes 12582928 | tf_op jit(solution)/shard_map/all_gather | solution.py:215
  261.9 23.1 %shard_map.178 = (bf16[2,2,2048,768]{3,2,1,0:T(8,128)(2,1)}, bf16[2,2048,192]{2,1,0:T(8,128)(2,1)}, bf16[2,2048,192]{2,1,0:T(8,128)(2,1)}) custom-call(bf16[2,2,2048,768]{3,2,1,0:T(8,128)(2,1)} %all-gather.5.cloned.1.call-done.rows_ref.geout_ref, bf16[2,2,2048,768]{3,2,1,0:T(8,128)(2,1)} %all-gather.5.cloned.1.call-done.rows_ref.geout_ref, ...), custom_call_target="tpu_custom_call" | custom-call | tf_op jit(solution)/shard_map/pallas_call | solution.py:41
  285.3 171.9 %reduce-scatter.3.cloned.1.call-done = bf16[2,2,128,768]{3,2,1,0:T(8,128)(2,1)} async-done(((bf16[2,2,2048,768]{3,2,1,0:T(8,128)(2,1)}), bf16[2,2,128,768]{3,2,1,0:T(8,128)(2,1)}) %reduce-scatter.3.cloned.1.call-update) | async-done | bytes 786448 | tf_op jit(solution)/shard_map/reduce_scatter | solution.py:220
  458.7 2.8 fusion.32
  467.9 2.5 convolution_convert_fusion.6
  470.4 2.0 copy.175
  472.4 1.9 copy.174
  475.7 2.0 multiply_convert_fusion
  482.5 2.4 convolution_convert_fusion
  484.9 2.3 pad_maximum_fusion
  487.2 4.8 fusion.6
  492.1 1.8 copy.183
  493.9 4.5 all-to-all-start.1
  498.4 5.3 fusion.7
  505.0 17.2 %all-to-all-done.1 = bf16[2,768,192]{2,0,1:T(2,128)(2,1)S(1)} async-done(((bf16[2,768,192]{2,0,1:T(2,128)(2,1)}), bf16[2,768,192]{2,0,1:T(2,128)(2,1)S(1)}, u32[]{:S(2)}, u32[]{:S(2)}) %all-to-all-start.1) | async-done | bytes 589856 | tf_op jit(solution)/shard_map/all_to_all | solution.py:230
  525.0 17.1 %collective-permute-done.16 = bf16[2,192,768]{2,1,0:T(8,128)(2,1)} collective-permute-done((bf16[2,192,768]{2,1,0:T(8,128)(2,1)S(1)}, bf16[2,192,768]{2,1,0:T(8,128)(2,1)}, u32[]{:S(2)}, u32[]{:S(2)}) %collective-permute-start.16) | collective-permute-done | bytes 589856 | tf_op jit(solution)/shard_map/ppermute | solution.py:85
  543.9 36.2 %collective-permute-done.12 = bf16[2,48,3072]{2,1,0:T(8,128)(2,1)S(1)} collective-permute-done((bf16[2,48,3072]{2,1,0:T(8,128)(2,1)S(1)}, bf16[2,48,3072]{2,1,0:T(8,128)(2,1)S(1)}, u32[]{:S(2)}, u32[]{:S(2)}) %collective-permute-start.12) | collective-permute-done | bytes 589856 | tf_op jit(solution)/shard_map/ppermute | solution.py:85
  580.7 17.7 %collective-permute-done.17 = bf16[2,192,768]{2,1,0:T(8,128)(2,1)S(1)} collective-permute-done((bf16[2,192,768]{2,1,0:T(8,128)(2,1)S(1)}, bf16[2,192,768]{2,1,0:T(8,128)(2,1)S(1)}, u32[]{:S(2)}, u32[]{:S(2)}) %collective-permute-start.17) | collective-permute-done | bytes 589856 | tf_op jit(solution)/shard_map/ppermute | solution.py:85
  598.6 1.6 collective-permute-start.18
  600.2 13.3 %collective-permute-done.13 = bf16[2,48,3072]{2,1,0:T(8,128)(2,1)S(1)} collective-permute-done((bf16[2,48,3072]{2,1,0:T(8,128)(2,1)S(1)}, bf16[2,48,3072]{2,1,0:T(8,128)(2,1)S(1)}, u32[]{:S(2)}, u32[]{:S(2)}) %collective-permute-start.13) | collective-permute-done | bytes 589856 | tf_op jit(solution)/shard_map/ppermute | solution.py:85
  613.6 1.6 collective-permute-start.14
  615.4 2.7 collective-permute-start.19
  618.1 3.5 fusion.29
  621.8 8.2 %collective-permute-done.14 = bf16[2,48,3072]{2,1,0:T(8,128)(2,1)S(1)} collective-permute-done((bf16[2,48,3072]{2,1,0:T(8,128)(2,1)S(1)}, bf16[2,48,3072]{2,1,0:T(8,128)(2,1)S(1)}, u32[]{:S(2)}, u32[]{:S(2)}) %collective-permute-start.14) | collective-permute-done | bytes 589856 | tf_op jit(solution)/shard_map/ppermute | solution.py:85
  630.1 3.1 collective-permute-start.15
  633.2 4.0 collective-permute-start.1
  637.2 7.5 %collective-permute-done.19 = bf16[2,192,768]{2,1,0:T(8,128)(2,1)S(1)} collective-permute-done((bf16[2,192,768]{2,1,0:T(8,128)(2,1)S(1)}, bf16[2,192,768]{2,1,0:T(8,128)(2,1)S(1)}, u32[]{:S(2)}, u32[]{:S(2)}) %collective-permute-start.19) | collective-permute-done | bytes 589856 | tf_op jit(solution)/shard_map/ppermute | solution.py:85
  646.6 8.8 %collective-permute-done.15 = bf16[2,48,3072]{2,1,0:T(8,128)(2,1)} collective-permute-done((bf16[2,48,3072]{2,1,0:T(8,128)(2,1)S(1)}, bf16[2,48,3072]{2,1,0:T(8,128)(2,1)}, u32[]{:S(2)}, u32[]{:S(2)}) %collective-permute-start.15) | collective-permute-done | bytes 589856 | tf_op jit(solution)/shard_map/ppermute | solution.py:85
  655.4 2.2 convert_add_fusion.1
  657.7 2.2 collective-permute-start.3
  660.0 2.9 collective-permute-done.3
  663.5 3.0 collective-permute-done.4
  666.5 3.2 collective-permute-start.5
  669.7 4.8 collective-permute-done.9
  676.1 1.8 collective-permute-start.6
  678.2 4.7 collective-permute-done.6
  684.0 2.6 collective-permute-start.11
  688.8 3.7 collective-permute-done.11
  (193 shorter events, 49.1 us)
Async XLA Ops:
  7.2 89.1 %all-gather.3.cloned.1.call-start = ((), (), s32[]{:S(2)}) async-start(), calls=%async_computation.4 | async-start | bytes 5222400 | tf_op jit(solution)/shard_map/all_gather | solution.py:181
  9.7 252.2 %all-gather.5.cloned.1.call-start = ((), (), s32[]{:S(2)}) async-start(), calls=%async_computation.5 | async-start | bytes 13369344 | tf_op jit(solution)/shard_map/all_gather | solution.py:215
  15.3 84.0 %copy-start.29 = (f32[197]{0:T(256)}, f32[197]{0:T(256)S(1)}, u32[]{:S(2)}) copy-start(f32[197]{0:T(256)S(1)} %broadcast_multiply_fusion.5) | copy-start | bytes 2368
  16.6 82.8 %copy-start.32 = (f32[197]{0:T(256)}, f32[197]{0:T(256)S(1)}, u32[]{:S(2)}) copy-start(f32[197]{0:T(256)S(1)} %add_rsqrt_fusion.1) | copy-start | bytes 2368
  103.6 4.1 copy-start.11
  103.6 2.8 copy-start.25
  103.6 4.2 copy-start.24
  107.7 354.8 %copy-start.26 = (f32[197]{0:T(256)}, f32[197]{0:T(256)S(1)}, u32[]{:S(2)}) copy-start(f32[197]{0:T(256)S(1)} %get-tuple-element.88) | copy-start | bytes 2368
  107.8 354.8 %copy-start.27 = (f32[197]{0:T(256)}, f32[197]{0:T(256)S(1)}, u32[]{:S(2)}) copy-start(f32[197]{0:T(256)S(1)} %fusion.52) | copy-start | bytes 2368
  108.0 4.2 copy-start.3
  113.5 343.8 %reduce-scatter.3.cloned.1.call-start = ((), (), s32[]{:S(2)}) async-start(), calls=%async_computation.6 | async-start | bytes 13369344 | tf_op jit(solution)/shard_map/reduce_scatter | solution.py:220
  285.1 361.5 %reduce-scatter.5.cloned.1.call-start = ((), (), s32[]{:S(2)}) async-start(), calls=%async_computation.7 | async-start | bytes 5222400 | tf_op jit(solution)/shard_map/reduce_scatter | solution.py:258
  462.5 3.6 copy-start.4
  475.7 3.1 copy-start.8
  477.7 2.4 copy-start.6
  478.8 2.6 copy-start.1
  478.8 2.6 copy-start.12
  480.0 2.2 copy-start.30
  480.0 2.2 copy-start.31
  480.0 2.2 copy-start.33
  493.9 28.4 %all-to-all-start.1 = ((bf16[2,768,192]{2,0,1:T(2,128)(2,1)}), bf16[2,768,192]{2,0,1:T(2,128)(2,1)S(1)}, u32[]{:S(2)}, u32[]{:S(2)}) async-start(bf16[2,768,192]{2,0,1:T(2,128)(2,1)} %copy.183), calls=%async_computation.3 | async-start | bytes 1572864 | tf_op jit(solution)/shard_map/all_to_all | solution.py:230
  503.7 38.4 %collective-permute-start.16 = (bf16[2,192,768]{2,1,0:T(8,128)(2,1)S(1)}, bf16[2,192,768]{2,1,0:T(8,128)(2,1)}, u32[]{:S(2)}, u32[]{:S(2)}) collective-permute-start(bf16[2,192,768]{2,1,0:T(8,128)(2,1)S(1)} %fusion.7), channel_id=1, source_target_pairs={{0,1},{1,0},{2,3},{3,2},{4,5},{5,4},{6,7},{7,6},{8,9},{9,8},{10,11... | collective-permute-start | bytes 1769480 | tf_op jit(solution)/shard_map/ppermute | solution.py:85
  523.5 56.6 %collective-permute-start.12 = (bf16[2,48,3072]{2,1,0:T(8,128)(2,1)S(1)}, bf16[2,48,3072]{2,1,0:T(8,128)(2,1)S(1)}, u32[]{:S(2)}, u32[]{:S(2)}) collective-permute-start(bf16[2,48,3072]{2,1,0:T(8,128)(2,1)S(1)} %all_to_all.33), channel_id=1, source_target_pairs={{0,1},{1,0},{2,3},{3,2},{4,5},{5,4},{6,7},{7,6},{8,9},{9,8},{10,11... | collective-permute-start | bytes 1769480 | tf_op jit(solution)/shard_map/ppermute | solution.py:85
  543.4 55.0 %collective-permute-start.17 = (bf16[2,192,768]{2,1,0:T(8,128)(2,1)S(1)}, bf16[2,192,768]{2,1,0:T(8,128)(2,1)S(1)}, u32[]{:S(2)}, u32[]{:S(2)}) collective-permute-start(bf16[2,192,768]{2,1,0:T(8,128)(2,1)S(1)} %add_convert_fusion.2), channel_id=1, source_target_pairs={{0,2},{1,3},{2,0},{3,1},{4,6},{5,7},{6,4},{7,5},{8,10},{9,11},{10,... | collective-permute-start | bytes 1769480 | tf_op jit(solution)/shard_map/ppermute | solution.py:85
  580.3 37.9 %copy-start.20 = (bf16[12,64,197]{2,1,0:T(8,128)(2,1)S(1)}, bf16[12,64,197]{2,1,0:T(8,128)(2,1)}, u32[]{:S(2)}) copy-start(bf16[12,64,197]{2,1,0:T(8,128)(2,1)} %convolution_convert_fusion.3) | copy-start | bytes 907780
  580.3 37.8 %copy-start.21 = (bf16[12,64,197]{2,1,0:T(8,128)(2,1)S(1)}, bf16[12,64,197]{2,1,0:T(8,128)(2,1)}, u32[]{:S(2)}) copy-start(bf16[12,64,197]{2,1,0:T(8,128)(2,1)} %fusion.9) | copy-start | bytes 907780
  580.3 37.8 %copy-start.22 = (bf16[12,64,197]{2,1,0:T(8,128)(2,1)S(1)}, bf16[12,64,197]{2,1,0:T(8,128)(2,1)}, u32[]{:S(2)}) copy-start(bf16[12,64,197]{2,1,0:T(8,128)(2,1)} %fusion.10) | copy-start | bytes 907780
  580.3 33.2 %collective-permute-start.13 = (bf16[2,48,3072]{2,1,0:T(8,128)(2,1)S(1)}, bf16[2,48,3072]{2,1,0:T(8,128)(2,1)S(1)}, u32[]{:S(2)}, u32[]{:S(2)}) collective-permute-start(bf16[2,48,3072]{2,1,0:T(8,128)(2,1)S(1)} %add_convert_fusion.5), channel_id=1, source_target_pairs={{0,2},{1,3},{2,0},{3,1},{4,6},{5,7},{6,4},{7,5},{8,10},{9,11},{10,... | collective-permute-start | bytes 1769480 | tf_op jit(solution)/shard_map/ppermute | solution.py:85
  598.6 16.7 %collective-permute-start.18 = (bf16[2,192,768]{2,1,0:T(8,128)(2,1)S(1)}, bf16[2,192,768]{2,1,0:T(8,128)(2,1)S(1)}, u32[]{:S(2)}, u32[]{:S(2)}) collective-permute-start(bf16[2,192,768]{2,1,0:T(8,128)(2,1)S(1)} %add_convert_fusion.1), channel_id=1, source_target_pairs={{0,4},{1,5},{2,6},{3,7},{4,0},{5,1},{6,2},{7,3},{8,12},{9,13},{10,... | collective-permute-start | bytes 1769480 | tf_op jit(solution)/shard_map/ppermute | solution.py:85
  613.6 16.4 %collective-permute-start.14 = (bf16[2,48,3072]{2,1,0:T(8,128)(2,1)S(1)}, bf16[2,48,3072]{2,1,0:T(8,128)(2,1)S(1)}, u32[]{:S(2)}, u32[]{:S(2)}) collective-permute-start(bf16[2,48,3072]{2,1,0:T(8,128)(2,1)S(1)} %add_convert_fusion.4), channel_id=1, source_target_pairs={{0,4},{1,5},{2,6},{3,7},{4,0},{5,1},{6,2},{7,3},{8,12},{9,13},{10,... | collective-permute-start | bytes 1769480 | tf_op jit(solution)/shard_map/ppermute | solution.py:85
  615.4 29.4 %collective-permute-start.19 = (bf16[2,192,768]{2,1,0:T(8,128)(2,1)S(1)}, bf16[2,192,768]{2,1,0:T(8,128)(2,1)S(1)}, u32[]{:S(2)}, u32[]{:S(2)}) collective-permute-start(bf16[2,192,768]{2,1,0:T(8,128)(2,1)S(1)} %add_convert_fusion), channel_id=1, source_target_pairs={{0,8},{1,9},{2,10},{3,11},{4,12},{5,13},{6,14},{7,15},{8,0},{9,1},... | collective-permute-start | bytes 1769480 | tf_op jit(solution)/shard_map/ppermute | solution.py:85
  621.7 11.5 %collective-permute-start = (f32[2,768]{1,0:T(2,128)S(1)}, f32[2,768]{1,0:T(2,128)S(1)}, u32[]{:S(2)}, u32[]{:S(2)}) collective-permute-start(f32[2,768]{1,0:T(2,128)S(1)} %pad_maximum_fusion.6), channel_id=1, source_target_pairs={{0,16},{16,0},{32,48},{48,32},{64,80},{80,64},{96,112},{112,96},{1... | collective-permute-start | bytes 18440 | tf_op jit(solution)/shard_map/ppermute | solution.py:85
  630.1 25.3 %collective-permute-start.15 = (bf16[2,48,3072]{2,1,0:T(8,128)(2,1)S(1)}, bf16[2,48,3072]{2,1,0:T(8,128)(2,1)}, u32[]{:S(2)}, u32[]{:S(2)}) collective-permute-start(bf16[2,48,3072]{2,1,0:T(8,128)(2,1)S(1)} %add_convert_fusion.3), channel_id=1, source_target_pairs={{0,8},{1,9},{2,10},{3,11},{4,12},{5,13},{6,14},{7,15},{8,0},{9,1},... | collective-permute-start | bytes 1769480 | tf_op jit(solution)/shard_map/ppermute | solution.py:85
  633.2 12.7 %collective-permute-start.1 = (f32[2,768]{1,0:T(2,128)S(1)}, f32[2,768]{1,0:T(2,128)S(1)}, u32[]{:S(2)}, u32[]{:S(2)}) collective-permute-start(f32[2,768]{1,0:T(2,128)S(1)} %fusion.59), channel_id=1, source_target_pairs={{0,32},{16,48},{32,0},{48,16},{64,96},{80,112},{96,64},{112,80},{1... | collective-permute-start | bytes 18440 | tf_op jit(solution)/shard_map/ppermute | solution.py:85
  645.9 29.1 %copy-start.2 = (f32[197,768]{1,0:T(8,128)S(1)}, f32[197,768]{1,0:T(8,128)}, u32[]{:S(2)}) copy-start(f32[197,768]{1,0:T(8,128)} %copy-done) | copy-start | bytes 1815556
  645.9 11.7 %collective-permute-start.2 = (f32[2,768]{1,0:T(2,128)S(1)}, f32[2,768]{1,0:T(2,128)S(1)}, u32[]{:S(2)}, u32[]{:S(2)}) collective-permute-start(f32[2,768]{1,0:T(2,128)S(1)} %fusion.83), channel_id=1, source_target_pairs={{0,64},{16,80},{32,96},{48,112},{64,0},{80,16},{96,32},{112,48},{1... | collective-permute-start | bytes 18440 | tf_op jit(solution)/shard_map/ppermute | solution.py:85
  646.6 13.2 %copy-start.23 = (bf16[48,3104]{1,0:T(8,128)(2,1)S(1)}, bf16[48,3104]{1,0:T(8,128)(2,1)}, u32[]{:S(2)}) copy-start(bf16[48,3104]{1,0:T(8,128)(2,1)} %reduce-scatter.5.cloned.1.call-done) | copy-start | bytes 893956
  646.6 13.2 %collective-permute-start.8 = (bf16[48,3104]{1,0:T(8,128)(2,1)}, bf16[48,3104]{1,0:T(8,128)(2,1)S(1)}, u32[]{:S(2)}, u32[]{:S(2)}) collective-permute-start(bf16[48,3104]{1,0:T(8,128)(2,1)} %reduce-scatter.5.cloned.1.call-done), channel_id=1, source_target_pairs={{0,1},{1,0},{2,3},{3,2},{4,5},{5,4},{6,7},{7,6},{8,9},{9,8},{10,11... | collective-permute-start | bytes 893960 | tf_op jit(solution)/shard_map/ppermute | solution.py:85
  657.6 20.3 %copy-start.13 = (bf16[2,2,128,768]{3,2,1,0:T(8,128)(2,1)S(1)}, bf16[2,2,128,768]{3,2,1,0:T(8,128)(2,1)}, u32[]{:S(2)}) copy-start(bf16[2,2,128,768]{3,2,1,0:T(8,128)(2,1)} %reduce-scatter.3.cloned.1.call-done) | copy-start | bytes 2359300
  657.7 5.2 collective-permute-start.3
  659.9 14.7 %collective-permute-start.9 = (bf16[48,3104]{1,0:T(8,128)(2,1)S(1)}, bf16[48,3104]{1,0:T(8,128)(2,1)S(1)}, u32[]{:S(2)}, u32[]{:S(2)}) collective-permute-start(bf16[48,3104]{1,0:T(8,128)(2,1)S(1)} %add_convert_fusion.8), channel_id=1, source_target_pairs={{0,2},{1,3},{2,0},{3,1},{4,6},{5,7},{6,4},{7,5},{8,10},{9,11},{10,... | collective-permute-start | bytes 893960 | tf_op jit(solution)/shard_map/ppermute | solution.py:85
  662.9 3.6 collective-permute-start.4
  666.5 20.1 %copy-start.18 = (bf16[197,2,128]{2,1,0:T(2,128)(2,1)S(1)}, bf16[197,2,128]{2,1,0:T(2,128)(2,1)}, u32[]{:S(2)}) copy-start(bf16[197,2,128]{2,1,0:T(2,128)(2,1)} %copy-done.17) | copy-start | bytes 302596
  666.5 9.6 %collective-permute-start.5 = (f32[2,768]{1,0:T(2,128)S(1)}, f32[2,768]{1,0:T(2,128)S(1)}, u32[]{:S(2)}, u32[]{:S(2)}) collective-permute-start(f32[2,768]{1,0:T(2,128)S(1)} %add.123), channel_id=1, source_target_pairs={{0,2},{1,3},{2,0},{3,1},{4,6},{5,7},{6,4},{7,5},{8,10},{9,11},{10,... | collective-permute-start | bytes 18440 | tf_op jit(solution)/shard_map/ppermute | solution.py:85
  674.7 9.2 %collective-permute-start.10 = (bf16[48,3104]{1,0:T(8,128)(2,1)S(1)}, bf16[48,3104]{1,0:T(8,128)(2,1)S(1)}, u32[]{:S(2)}, u32[]{:S(2)}) collective-permute-start(bf16[48,3104]{1,0:T(8,128)(2,1)S(1)} %add_convert_fusion.7), channel_id=1, source_target_pairs={{0,4},{1,5},{2,6},{3,7},{4,0},{5,1},{6,2},{7,3},{8,12},{9,13},{10,... | collective-permute-start | bytes 893960 | tf_op jit(solution)/shard_map/ppermute | solution.py:85
  676.1 6.8 collective-permute-start.6
  682.9 5.3 collective-permute-start.7
  684.0 8.5 %collective-permute-start.11 = (bf16[48,3104]{1,0:T(8,128)(2,1)S(1)}, bf16[48,3104]{1,0:T(8,128)(2,1)S(1)}, u32[]{:S(2)}, u32[]{:S(2)}) collective-permute-start(bf16[48,3104]{1,0:T(8,128)(2,1)S(1)} %add_convert_fusion.6), channel_id=1, source_target_pairs={{0,8},{1,9},{2,10},{3,11},{4,12},{5,13},{6,14},{7,15},{8,0},{9,1},... | collective-permute-start | bytes 893960 | tf_op jit(solution)/shard_map/ppermute | solution.py:85
  (11 other events, 13.9 us)
Sparse Core Ops, SparseCore 0:
  11.2 85.0 all-gather.2
  113.6 148.2 all-gather.4
  285.2 171.9 reduce-scatter.2
  487.4 127.2 reduce-scatter.4
